TPU v7x, 32 devices: a whole 2x2x4 slice. The times are simulated.
32 devices in a mesh: seq: 4 (over y, x), col: 8 (over z, core).
Axes of the slice: x: 2, y: 2, z: 4, core: 2. Of those that a mesh axis runs over, the one named last changes fastest.
Arguments:
- alignment: bfloat16 [32, 128, 256], P('seq', 'col')
- row_query: bfloat16 [256, 128], replicated
- row_key: bfloat16 [256, 128], replicated
- row_value: bfloat16 [256, 128], replicated, may hold values from -0.375 to 0.375
- row_output: bfloat16 [128, 256], replicated, may hold values from -0.5 to 0.5
- column_query: bfloat16 [256, 128], replicated
- column_key: bfloat16 [256, 128], replicated
- column_value: bfloat16 [256, 128], replicated, may hold values from -0.375 to 0.375
- column_output: bfloat16 [128, 256], replicated, may hold values from -0.5 to 0.5
Outputs:
- row_update: bfloat16 [32, 128, 256], P('seq', 'col')
- layer_output: bfloat16 [32, 128, 256], P('seq', 'col')
All inputs are finite; a program needn't handle non-finite values.
Results may differ from a plain program's by a relative error of at most 0.014.
Values may be sent and summed in bfloat16 or wider, within the bound.
No kernel may reach another device: no remote copies, remote signals or barrier semaphores. Data moves between devices by JAX's collectives and lax.ppermute only.
A program may use at most 64 MiB of HBM per device.

v0:
```python
import jax
import jax.numpy as jnp
from jax import lax
from jax.sharding import PartitionSpec as P

HEADS = 4
HEAD_DIM = 32


def layer_norm(field):
    values = field.astype(jnp.float32)
    mean = jnp.mean(values, axis=-1, keepdims=True)
    centred = values - mean
    variance = jnp.mean(centred * centred, axis=-1, keepdims=True)
    return (centred * lax.rsqrt(variance + 1e-05)).astype(jnp.bfloat16)


def project(field, weight):
    return jnp.dot(field, weight, preferred_element_type=jnp.float32)


def column_attend(queries, keys, values):
    seq_rows, columns, inner = queries.shape
    query_heads = queries.reshape(seq_rows, columns, HEADS, HEAD_DIM)
    key_heads = keys.reshape(keys.shape[0], columns, HEADS, HEAD_DIM)
    value_heads = values.reshape(values.shape[0], columns, HEADS, HEAD_DIM)
    scores = jnp.einsum(
        "schd,tchd->chst", query_heads, key_heads, preferred_element_type=jnp.float32
    ) * float(HEAD_DIM) ** (-0.5)
    weights = jax.nn.softmax(scores, axis=-1).astype(jnp.bfloat16)
    context = jnp.einsum(
        "chst,tchd->schd", weights, value_heads, preferred_element_type=jnp.float32
    )
    return context.reshape(seq_rows, columns, inner).astype(jnp.bfloat16)


def on_device(
    alignment,
    row_query,
    row_key,
    row_value,
    row_output,
    column_query,
    column_key,
    column_value,
    column_output,
):
    seq_dev, col_dev, width = alignment.shape
    inner = row_query.shape[1]
    scale = float(HEAD_DIM * seq_dev * lax.axis_size("seq")) ** (-0.5)
    normed = layer_norm(alignment)
    queries = project(normed, row_query).astype(jnp.bfloat16)
    keys = project(normed, row_key).astype(jnp.bfloat16)
    values = project(normed, row_value).astype(jnp.bfloat16)
    query_heads = queries.reshape(seq_dev, col_dev, HEADS, HEAD_DIM)
    piece = lax.all_gather(keys, "col", axis=1, tiled=True)
    piece_heads = piece.reshape(seq_dev, piece.shape[1], HEADS, HEAD_DIM)
    partial_value = jnp.einsum(
        "sihd,sjhd->hij", query_heads, piece_heads, preferred_element_type=jnp.float32
    )
    logits = lax.psum(partial_value, "seq") * scale
    probs = jax.nn.softmax(logits, axis=-1).astype(jnp.bfloat16)
    piece = lax.all_gather(values, "col", axis=1, tiled=True)
    piece_heads = piece.reshape(seq_dev, piece.shape[1], HEADS, HEAD_DIM)
    context = jnp.einsum("hij,sjhd->sihd", probs, piece_heads, preferred_element_type=jnp.float32)
    context = context.reshape(seq_dev, col_dev, inner).astype(jnp.bfloat16)
    row_update = project(context, row_output).astype(jnp.bfloat16)
    middle = (alignment.astype(jnp.float32) + row_update.astype(jnp.float32)).astype(jnp.bfloat16)
    column_normed = layer_norm(middle)
    column_queries = project(column_normed, column_query).astype(jnp.bfloat16)
    column_keys = project(column_normed, column_key).astype(jnp.bfloat16)
    column_values = project(column_normed, column_value).astype(jnp.bfloat16)
    every_keys, every_values = (
        lax.all_gather(column_keys, "seq", axis=0, tiled=True),
        lax.all_gather(column_values, "seq", axis=0, tiled=True),
    )
    column_context = column_attend(column_queries, every_keys, every_values)
    layer_output = (middle.astype(jnp.float32) + project(column_context, column_output)).astype(
        jnp.bfloat16
    )
    return (row_update, layer_output)


def solution(mesh):
    return jax.shard_map(
        on_device,
        mesh=mesh,
        in_specs=(P("seq", "col", None), P(), P(), P(), P(), P(), P(), P(), P()),
        out_specs=(P("seq", "col", None), P("seq", "col", None)),
        check_vma=False,
    )
```

profile of v0, /device:TPU:0, one launch (start us, length us, event | category | flops | bytes accessed | tf_op | source)
XLA Modules:
  0.0 75.1 jit_solution(4044517943388862189)
XLA Ops:
  0.6 0.0 copy-start
  0.6 0.0 copy-start.1
  0.7 0.0 copy-start.3
  0.7 1.0 %convert_reduce_fusion.1 = f32[8,16]{1,0:T(8,128)S(1)} fusion(bf16[8,16,256]{2,1,0:T(8,128)(2,1)} %param.9), kind=kLoop, calls=%fused_computation.30 | loop fusion | flops 65408 | bytes 66048 | tf_op jit(solution)/shard_map/reduce_sum | solution.py:12
  1.7 0.0 copy-done.1
  1.7 0.2 fusion.19
  1.9 0.0 copy-done.3
  1.9 0.2 convolution_convert_fusion.6
  2.1 15.9 %all_gather.13 = bf16[8,128,128]{2,1,0:T(8,128)(2,1)S(1)} all-gather(bf16[8,16,128]{2,1,0:T(8,128)(2,1)S(1)} %convolution_convert_fusion.6), channel_id=1, replica_groups=mesh['seq'=4,'col'=8] {'col'}, dimensions={1}, use_global_device_ids=true | all-gather | bytes 294912 | tf_op jit(solution)/shard_map/all_gather | solution.py:56
  18.0 0.0 copy-start.4
  18.0 0.2 copy.36
  18.2 0.7 copy-done.4
  18.8 0.2 convolution_convert_fusion.7
  19.1 0.1 reshape.55
  19.2 0.2 convolution_bitcast_fusion
  19.4 0.0 copy-start.5
  19.4 16.4 %psum.7 = f32[4,16,128]{2,1,0:T(8,128)S(1)} all-reduce(f32[4,16,128]{2,1,0:T(8,128)S(1)} %convolution_bitcast_fusion), channel_id=1, replica_groups=mesh['seq'=4,'col'=8] {'seq'}, use_global_device_ids=true, to_apply=%region_2.0 | all-reduce | flops 8192 | bytes 65536 | tf_op jit(solution)/shard_map/psum | solution.py:61
  35.9 0.2 fusion.51
  36.0 0.0 copy-done.5
  36.0 0.2 convolution_convert_fusion.8
  36.3 14.3 %all_gather.12 = bf16[8,128,128]{2,1,0:T(8,128)(2,1)S(1)} all-gather(bf16[8,16,128]{2,1,0:T(8,128)(2,1)S(1)} %convolution_convert_fusion.8), channel_id=1, replica_groups=mesh['seq'=4,'col'=8] {'col'}, dimensions={1}, use_global_device_ids=true | all-gather | bytes 294912 | tf_op jit(solution)/shard_map/all_gather | solution.py:63
  50.6 0.2 copy.35
  50.8 0.5 fusion.5
  51.2 0.1 copy.40
  51.4 0.1 convert_element_type.76
  51.5 0.0 copy-done
  51.5 0.8 %convert_reduce_fusion = (f32[8,16]{1,0:T(8,128)S(1)}, bf16[8,16,256]{2,1,0:T(8,128)(2,1)S(1)}, bf16[8,16,256]{2,1,0:T(8,128)(2,1)}) fusion(bf16[8,16,256]{2,1,0:T(8,128)(2,1)S(1)} %copy-done.1, bf16[8,16,128]{2,1,0:T(8,128)(2,1)S(1)} %convert_element_type.76, bf16[128,256]{1,0:T(8,128)(2,1)S(1)} %copy-done), kind=kOutput, calls=%fused_computation.27 | convolution fusion | flops 8617856 | bytes 295424 | tf_op jit(solution)/shard_map/dot_general | solution.py:19
  52.3 0.2 fusion.17
  52.5 0.6 copy-done.6
  53.1 0.2 convolution_convert_fusion.4
  53.4 0.0 copy-start.7
  53.4 0.1 reshape.58
  53.5 0.7 copy-done.7
  54.2 0.2 convolution_convert_fusion.3
  54.4 7.5 %all_gather.15 = bf16[32,16,128]{2,1,0:T(8,128)(2,1)S(1)} all-gather(bf16[8,16,128]{2,1,0:T(8,128)(2,1)S(1)} %convolution_convert_fusion.3), channel_id=1, replica_groups=mesh['seq'=4,'col'=8] {'seq'}, dimensions={0}, use_global_device_ids=true | all-gather | bytes 163840 | tf_op jit(solution)/shard_map/all_gather | solution.py:74
  62.0 0.2 reshape.59
  62.2 0.5 convolution_multiply_fusion
  62.7 0.3 fusion.52
  63.0 0.6 copy-done.8
  63.5 0.2 convolution_convert_fusion.5
  63.8 8.4 %all_gather.14 = bf16[32,16,128]{2,1,0:T(8,128)(2,1)S(1)} all-gather(bf16[8,16,128]{2,1,0:T(8,128)(2,1)S(1)} %convolution_convert_fusion.5), channel_id=1, replica_groups=mesh['seq'=4,'col'=8] {'seq'}, dimensions={0}, use_global_device_ids=true | all-gather | bytes 163840 | tf_op jit(solution)/shard_map/all_gather | solution.py:75
  72.1 0.2 reshape.57
  72.4 1.0 %fusion.4 = bf16[8,16,4,32]{3,0,2,1:T(8,128)(2,1)S(1)} fusion(bf16[32,16,4,32]{3,2,1,0:T(4,128)(2,1)S(1)} %reshape.57, f32[16,4,8]{2,1,0:T(4,128)S(1)} %fusion.52, f32[16,4,8,32]{3,2,1,0:T(8,128)S(1)} %convolution_multiply_fusion), kind=kOutput, calls=%fused_computation.7 | convolution fusion | flops 1114655 | bytes 231424 | tf_op jit(solution)/shard_map/chst,tchd->schd/dot_general | solution.py:31
  73.4 0.1 copy.44
  73.4 0.0 copy-start.2
  73.5 0.1 convert_element_type.88
  73.6 0.7 copy-done.2
  74.3 0.8 %fusion.6 = bf16[8,16,256]{2,1,0:T(8,128)(2,1)} fusion(bf16[8,16,128]{2,1,0:T(8,128)(2,1)S(1)} %convert_element_type.88, bf16[8,16,256]{2,1,0:T(8,128)(2,1)S(1)} %get-tuple-element.3, bf16[128,256]{1,0:T(8,128)(2,1)S(1)} %copy-done.2), kind=kOutput, calls=%fused_computation.11 | convolution fusion | flops 8486912 | bytes 229376 | tf_op jit(solution)/shard_map/dot_general | solution.py:19
  (6 shorter events, 0.0 us)
Async XLA Ops:
  0.6 50.9 %copy-start = (bf16[128,256]{1,0:T(8,128)(2,1)S(1)}, bf16[128,256]{1,0:T(8,128)(2,1)}, u32[]{:S(2)}) copy-start(bf16[128,256]{1,0:T(8,128)(2,1)} %param.13) | copy-start | bytes 196612
  0.6 1.0 %copy-start.1 = (bf16[8,16,256]{2,1,0:T(8,128)(2,1)S(1)}, bf16[8,16,256]{2,1,0:T(8,128)(2,1)}, u32[]{:S(2)}) copy-start(bf16[8,16,256]{2,1,0:T(8,128)(2,1)} %param.9) | copy-start | bytes 196612
  0.7 1.2 %copy-start.3 = (bf16[256,128]{1,0:T(8,128)(2,1)S(1)}, bf16[256,128]{1,0:T(8,128)(2,1)}, u32[]{:S(2)}) copy-start(bf16[256,128]{1,0:T(8,128)(2,1)} %param.11) | copy-start | bytes 196612
  18.0 0.8 %copy-start.4 = (bf16[256,128]{1,0:T(8,128)(2,1)S(1)}, bf16[256,128]{1,0:T(8,128)(2,1)}, u32[]{:S(2)}) copy-start(bf16[256,128]{1,0:T(8,128)(2,1)} %param.10) | copy-start | bytes 196612
  19.4 16.6 %copy-start.5 = (bf16[256,128]{1,0:T(8,128)(2,1)S(1)}, bf16[256,128]{1,0:T(8,128)(2,1)}, u32[]{:S(2)}) copy-start(bf16[256,128]{1,0:T(8,128)(2,1)} %param.12) | copy-start | bytes 196612
  52.3 0.8 %copy-start.6 = (bf16[256,128]{1,0:T(8,128)(2,1)S(1)}, bf16[256,128]{1,0:T(8,128)(2,1)}, u32[]{:S(2)}) copy-start(bf16[256,128]{1,0:T(8,128)(2,1)} %param.14) | copy-start | bytes 196612
  53.4 0.8 %copy-start.7 = (bf16[256,128]{1,0:T(8,128)(2,1)S(1)}, bf16[256,128]{1,0:T(8,128)(2,1)}, u32[]{:S(2)}) copy-start(bf16[256,128]{1,0:T(8,128)(2,1)} %param.15) | copy-start | bytes 196612
  62.7 0.8 %copy-start.8 = (bf16[256,128]{1,0:T(8,128)(2,1)S(1)}, bf16[256,128]{1,0:T(8,128)(2,1)}, u32[]{:S(2)}) copy-start(bf16[256,128]{1,0:T(8,128)(2,1)} %param.16) | copy-start | bytes 196612
  73.4 0.8 %copy-start.2 = (bf16[128,256]{1,0:T(8,128)(2,1)S(1)}, bf16[128,256]{1,0:T(8,128)(2,1)}, u32[]{:S(2)}) copy-start(bf16[128,256]{1,0:T(8,128)(2,1)} %param.17) | copy-start | bytes 196612
where the time goes:
time: 75.6 us; the launch traced here: 75.1 us
  blocking collectives  62.6 us (83%)
  matrix products  5.07 us (7%)
  local copies, waits for them, and re-layouts  4.82 us (6%)
  other arithmetic  1.75 us (2%)
  between operations  0.86 us (1%)
    psum x1, blocking collectives, on_device(): logits = lax.psum(partial_value, 'seq') * scale  16.4 us
    all_gather x1, blocking collectives, on_device(): piece = lax.all_gather(keys, 'col', axis=1, tiled=True)  15.9 us
    all_gather x1, blocking collectives, on_device(): piece = lax.all_gather(values, 'col', axis=1, tiled=True)  14.3 us
    all_gather x1, blocking collectives, on_device(): lax.all_gather(column_values, 'seq', axis=0, tiled=True)  8.37 us
    all_gather x1, blocking collectives, on_device(): lax.all_gather(column_keys, 'seq', axis=0, tiled=True)  7.55 us
    unnamed x18, local copies, waits for them, and re-layouts  3.34 us
    dot_general x8, matrix products, project(): return jnp.dot(field, weight, preferred_element_type=jnp.float32)  2.87 us

commit v1 on v0

--- a/solution.py
+++ b/solution.py
@@ -17,6 +17,22 @@
 
 def project(field, weight):
     return jnp.dot(field, weight, preferred_element_type=jnp.float32)
+
+
+def gather(block, axis, groups=None, size=None):
+    size = lax.axis_size(axis) if size is None else size
+    copies = jnp.broadcast_to(block[None], (size,) + block.shape)
+    return lax.all_to_all(copies, axis, 0, 0, axis_index_groups=groups)
+
+
+def gather_columns(block):
+    size = lax.axis_size("col")
+    if size % 2 or size == 2:
+        return gather(block, "col")
+    groups = [[i for i in range(size) if i % 2 == parity] for parity in (0, 1)]
+    mine = gather(block, "col", groups, size // 2)
+    other = lax.ppermute(mine, "col", [(i, i ^ 1) for i in range(size)])
+    return jnp.concatenate([mine, other], axis=0)
 
 
 def column_attend(queries, keys, values):
@@ -50,31 +66,28 @@
     scale = float(HEAD_DIM * seq_dev * lax.axis_size("seq")) ** (-0.5)
     normed = layer_norm(alignment)
     queries = project(normed, row_query).astype(jnp.bfloat16)
-    keys = project(normed, row_key).astype(jnp.bfloat16)
-    values = project(normed, row_value).astype(jnp.bfloat16)
+    key_value = project(normed, jnp.concatenate([row_key, row_value], axis=1)).astype(jnp.bfloat16)
     query_heads = queries.reshape(seq_dev, col_dev, HEADS, HEAD_DIM)
-    piece = lax.all_gather(keys, "col", axis=1, tiled=True)
-    piece_heads = piece.reshape(seq_dev, piece.shape[1], HEADS, HEAD_DIM)
+    every = gather_columns(key_value)
+    key_heads = every[..., :inner].reshape(every.shape[0], seq_dev, col_dev, HEADS, HEAD_DIM)
+    value_heads = every[..., inner:].reshape(every.shape[0], seq_dev, col_dev, HEADS, HEAD_DIM)
     partial_value = jnp.einsum(
-        "sihd,sjhd->hij", query_heads, piece_heads, preferred_element_type=jnp.float32
+        "sihd,gsjhd->higj", query_heads, key_heads, preferred_element_type=jnp.float32
     )
-    logits = lax.psum(partial_value, "seq") * scale
-    probs = jax.nn.softmax(logits, axis=-1).astype(jnp.bfloat16)
-    piece = lax.all_gather(values, "col", axis=1, tiled=True)
-    piece_heads = piece.reshape(seq_dev, piece.shape[1], HEADS, HEAD_DIM)
-    context = jnp.einsum("hij,sjhd->sihd", probs, piece_heads, preferred_element_type=jnp.float32)
+    shape = partial_value.shape
+    partial_value = partial_value.reshape(shape[0], shape[1], -1)
+    logits = jnp.sum(gather(partial_value, "seq"), axis=0) * scale
+    probs = jax.nn.softmax(logits, axis=-1).astype(jnp.bfloat16).reshape(shape)
+    context = jnp.einsum("higj,gsjhd->sihd", probs, value_heads, preferred_element_type=jnp.float32)
     context = context.reshape(seq_dev, col_dev, inner).astype(jnp.bfloat16)
     row_update = project(context, row_output).astype(jnp.bfloat16)
     middle = (alignment.astype(jnp.float32) + row_update.astype(jnp.float32)).astype(jnp.bfloat16)
     column_normed = layer_norm(middle)
     column_queries = project(column_normed, column_query).astype(jnp.bfloat16)
-    column_keys = project(column_normed, column_key).astype(jnp.bfloat16)
-    column_values = project(column_normed, column_value).astype(jnp.bfloat16)
-    every_keys, every_values = (
-        lax.all_gather(column_keys, "seq", axis=0, tiled=True),
-        lax.all_gather(column_values, "seq", axis=0, tiled=True),
-    )
-    column_context = column_attend(column_queries, every_keys, every_values)
+    column_pair = project(column_normed, jnp.concatenate([column_key, column_value], axis=1))
+    every = gather(column_pair.astype(jnp.bfloat16), "seq")
+    every = every.reshape((-1,) + every.shape[2:])
+    column_context = column_attend(column_queries, every[..., :inner], every[..., inner:])
     layer_output = (middle.astype(jnp.float32) + project(column_context, column_output)).astype(
         jnp.bfloat16
     )

time: 75.6 us -> 48.6 us (0.64)
  blocking collectives: 62.6 us -> 15.2 us
  waiting for transfers between devices: 0 us -> 10.7 us
  starting transfers between devices: 0 us -> 7.25 us
  matrix products: 5.07 us -> 6.53 us
    all_gather x4 -> x0, blocking collectives: 46.1 us -> none  [the longest x1 15.9 us: on_device(): piece = lax.all_gather(keys, 'col', axis=1, tiled=True)]
    psum x1 -> x0, blocking collectives: 16.4 us -> none  [on_device(): logits = lax.psum(partial_value, 'seq') * scale]
    all_to_all x0 -> x1, blocking collectives: none -> 15.2 us  [gather(): return lax.all_to_all(copies, axis, 0, 0, axis_index_groups=groups)]
    all_to_all x0 -> x2, waiting for transfers between devices: none -> 9.59 us  [gather(): return lax.all_to_all(copies, axis, 0, 0, axis_index_groups=groups)]
    all_to_all x0 -> x2, starting transfers between devices: none -> 7.25 us  [gather(): return lax.all_to_all(copies, axis, 0, 0, axis_index_groups=groups)]
    unnamed x18 -> x17, local copies, waits for them, and re-layouts: 3.34 us -> 1.41 us
    broadcast_in_dim x0 -> x4, local copies, waits for them, and re-layouts: none -> 1.51 us  [gather(): copies = jnp.broadcast_to(block[None], (size,) + block.shape)]
    ppermute x0 -> x1, waiting for transfers between devices: none -> 1.15 us  [gather_columns(): other = lax.ppermute(mine, 'col', [(i, i ^ 1) for i in range(size)])]
  transfers between devices with their start and end apart: 0 -> 3, of which waited for: 0 -> 3; matrix products, arithmetic and copies ran while one was open for 0% -> 2% of each run, Pallas kernels for 0% -> 0%
where the time goes in v1:
time: 48.6 us; the launch traced here: 48 us
  blocking collectives  15.2 us (31%)
  waiting for transfers between devices  10.7 us (22%)
  starting transfers between devices  7.25 us (15%)
  matrix products  6.53 us (13%)
  local copies, waits for them, and re-layouts  5.28 us (11%)
  other arithmetic  2.06 us (4%)
  between operations  0.94 us (2%)
    all_to_all x1, blocking collectives, gather(): return lax.all_to_all(copies, axis, 0, 0, axis_index_groups=groups)  15.2 us
    all_to_all x2, waiting for transfers between devices, gather(): return lax.all_to_all(copies, axis, 0, 0, axis_index_groups=groups)  9.59 us
    all_to_all x2, starting transfers between devices, gather(): return lax.all_to_all(copies, axis, 0, 0, axis_index_groups=groups)  7.25 us
    dot_general x6, matrix products, project(): return jnp.dot(field, weight, preferred_element_type=jnp.float32)  3.26 us
    broadcast_in_dim x4, local copies, waits for them, and re-layouts, gather(): copies = jnp.broadcast_to(block[None], (size,) + block.shape)  1.51 us
    unnamed x17, local copies, waits for them, and re-layouts  1.41 us
    dot_general x1, matrix products, on_device(): jnp.einsum('sihd,gsjhd->higj', query_heads, key_heads, preferred_element_...  1.32 us
    ppermute x1, waiting for transfers between devices, gather_columns(): other = lax.ppermute(mine, 'col', [(i, i ^ 1) for i in range(size)])  1.15 us
  transfers between devices with their start and end apart: 3, of which 3 were waited for; matrix products, arithmetic and copies ran while one was open for 2% of the time, Pallas kernels for 0%

profile of v1, /device:TPU:0, one launch (start us, length us, event | category | flops | bytes accessed | tf_op | source)
XLA Modules:
  0.0 48.0 jit_solution(13910144581237907587)
XLA Ops:
  0.6 0.0 copy-start
  0.7 1.0 %convert_reduce_fusion.1 = f32[8,16]{1,0:T(8,128)S(1)} fusion(bf16[8,16,256]{2,1,0:T(8,128)(2,1)} %param.9), kind=kLoop, calls=%fused_computation.27 | loop fusion | flops 65408 | bytes 66048 | tf_op jit(solution)/shard_map/reduce_sum | solution.py:12
  1.7 0.2 fusion.17
  1.9 0.0 copy-done.3
  1.9 1.1 %convolution_convert_fusion.3 = bf16[8,16,256]{2,1,0:T(8,128)(2,1)S(1)} fusion(bf16[256,128]{1,0:T(8,128)(2,1)S(1)} %copy-done.3, bf16[256,128]{1,0:T(8,128)(2,1)} %param.11, bf16[8,16,256]{2,1,0:T(8,128)(2,1)S(1)} %copy-done.1, f32[8,16]{1,0:T(8,128)S(1)} %add_rsqrt_fusion.1, f32[8,16]{1,0:T(8,128)S(1)} %broadcast_multiply_fusion.2), kind=kOutput, calls=%fused_computation.14 | convolution fusion | flops 17203200 | bytes 263168 | tf_op jit(solution)/shard_map/dot_general | solution.py:19
  3.0 0.0 copy-start.4
  3.0 15.2 %all_to_all.15 = bf16[4,8,16,256]{3,2,1,0:T(8,128)(2,1)S(1)} all-to-all(bf16[4,8,16,256]{3,2,1,0:T(8,128)(2,1)S(1)} %broadcast_in_dim.8), channel_id=1, replica_groups={{0,2,4,6},{1,3,5,7},{8,10,12,14},{9,11,13,15},{16,18,20,22},{17,19,21,2..., dimensions={0} | all-to-all | bytes 524288 | tf_op jit(solution)/shard_map/all_to_all | solution.py:25
  18.1 0.0 collective-permute-start
  18.1 0.2 convolution_convert_fusion.5
  18.4 0.1 reshape.65
  18.5 1.2 %collective-permute-done = bf16[4,8,16,256]{3,2,1,0:T(8,128)(2,1)S(1)} collective-permute-done((bf16[4,8,16,256]{3,2,1,0:T(8,128)(2,1)S(1)}, bf16[4,8,16,256]{3,2,1,0:T(8,128)(2,1)S(1)}, u32[]{:S(2)}, u32[]{:S(2)}) %collective-permute-start) | collective-permute-done | bytes 262176 | tf_op jit(solution)/shard_map/ppermute | solution.py:34
  19.7 0.1 fusion.41
  19.8 0.4 reshape.66
  20.2 1.3 %convolution_bitcast_fusion.1 = f32[4,16,8,16]{3,1,2,0:T(8,128)S(1)} fusion(bf16[8,8,16,4,32]{4,3,2,1,0:T(4,128)(2,1)S(1)} %reshape.66, bf16[8,16,4,32,1]{3,2,1,0,4:T(4,128)(2,1)S(1)} %bitcast.49), kind=kOutput, calls=%fused_computation.5 | convolution fusion | flops 4194304 | bytes 327680 | tf_op jit(solution)/shard_map/sihd,gsjhd->higj/dot_general | solution.py:74
  21.6 0.1 copy.25
  21.7 0.1 broadcast_in_dim.9
  21.8 0.6 %broadcast_in_dim.10 = f32[4,4,16,128]{3,2,1,0:T(8,128)} broadcast(f32[4,16,128]{2,1,0:T(8,128)S(1)} %broadcast_in_dim.9), dimensions={1,2,3} | broadcast | bytes 163840 | tf_op jit(solution)/shard_map/broadcast_in_dim | solution.py:24
  22.4 3.7 %all-to-all-start.1 = ((f32[4,4,16,128]{3,2,1,0:T(8,128)}), f32[4,4,16,128]{3,2,1,0:T(8,128)S(1)}, u32[]{:S(2)}, u32[]{:S(2)}) async-start(f32[4,4,16,128]{3,2,1,0:T(8,128)} %broadcast_in_dim.10), calls=%async_computation.1 | async-start | bytes 262144 | tf_op jit(solution)/shard_map/all_to_all | solution.py:25
  26.2 0.4 reshape.64
  26.6 4.6 %all-to-all-done.1 = f32[4,4,16,128]{3,2,1,0:T(8,128)S(1)} async-done(((f32[4,4,16,128]{3,2,1,0:T(8,128)}), f32[4,4,16,128]{3,2,1,0:T(8,128)S(1)}, u32[]{:S(2)}, u32[]{:S(2)}) %all-to-all-start.1) | async-done | bytes 131104 | tf_op jit(solution)/shard_map/all_to_all | solution.py:25
  31.2 0.1 broadcast_multiply_fusion
  31.3 0.2 exponential_reduce_fusion
  31.4 0.1 mul.43
  31.6 0.2 fusion.28
  31.8 0.5 fusion.5
  32.3 0.1 copy.28
  32.4 0.1 convert_element_type.70
  32.5 0.0 copy-start.6
  32.5 0.8 %convert_reduce_fusion = (f32[8,16]{1,0:T(8,128)S(1)}, bf16[8,16,256]{2,1,0:T(8,128)(2,1)S(1)}, bf16[8,16,256]{2,1,0:T(8,128)(2,1)}) fusion(bf16[8,16,256]{2,1,0:T(8,128)(2,1)S(1)} %copy-done.1, bf16[8,16,128]{2,1,0:T(8,128)(2,1)S(1)} %convert_element_type.70, bf16[128,256]{1,0:T(8,128)(2,1)S(1)} %copy-done), kind=kOutput, calls=%fused_computation.24 | convolution fusion | flops 8617856 | bytes 295424 | tf_op jit(solution)/shard_map/dot_general | solution.py:19
  33.3 0.2 fusion.15
  33.5 0.6 %copy-done.5 = bf16[256,128]{1,0:T(8,128)(2,1)S(1)} copy-done((bf16[256,128]{1,0:T(8,128)(2,1)S(1)}, bf16[256,128]{1,0:T(8,128)(2,1)}, u32[]{:S(2)}) %copy-start.5) | copy-done | bytes 65560
  34.2 0.2 convolution_convert_fusion.2
  34.4 0.7 %broadcast_in_dim.11 = bf16[4,8,16,256]{3,2,1,0:T(8,128)(2,1)} broadcast(bf16[8,16,256]{2,1,0:T(8,128)(2,1)S(1)} %convolution_convert_fusion.2), dimensions={1,2,3} | broadcast | bytes 327680 | tf_op jit(solution)/shard_map/broadcast_in_dim | solution.py:24
  35.1 3.5 %all-to-all-start.2 = ((bf16[4,8,16,256]{3,2,1,0:T(8,128)(2,1)}), bf16[4,8,16,256]{3,2,1,0:T(8,128)(2,1)S(1)}, u32[]{:S(2)}, u32[]{:S(2)}) async-start(bf16[4,8,16,256]{3,2,1,0:T(8,128)(2,1)} %broadcast_in_dim.11), calls=%async_computation.2 | async-start | bytes 524288 | tf_op jit(solution)/shard_map/all_to_all | solution.py:25
  38.6 0.0 copy-done.7
  38.7 0.2 convolution_convert_fusion.4
  38.9 0.1 reshape.69
  39.0 5.0 %all-to-all-done.2 = bf16[4,8,16,256]{3,2,1,0:T(8,128)(2,1)S(1)} async-done(((bf16[4,8,16,256]{3,2,1,0:T(8,128)(2,1)}), bf16[4,8,16,256]{3,2,1,0:T(8,128)(2,1)S(1)}, u32[]{:S(2)}, u32[]{:S(2)}) %all-to-all-start.2) | async-done | bytes 262176 | tf_op jit(solution)/shard_map/all_to_all | solution.py:25
  44.0 0.2 reshape.70
  44.3 0.5 %convolution_multiply_fusion = f32[16,4,8,32]{3,2,1,0:T(8,128)S(1)} fusion(bf16[32,16,4,32]{3,2,1,0:T(4,128)(2,1)S(1)} %reshape.70, bf16[8,16,4,32]{3,2,1,0:T(4,128)(2,1)S(1)} %reshape.69), kind=kOutput, calls=%fused_computation.2 | convolution fusion | flops 1064960 | bytes 229376 | tf_op jit(solution)/shard_map/schd,tchd->chst/dot_general | solution.py:43
  44.8 0.3 fusion.43
  45.0 0.2 reshape.68
  45.3 1.0 %fusion.4 = bf16[8,16,4,32]{3,0,2,1:T(8,128)(2,1)S(1)} fusion(bf16[32,16,4,32]{3,2,1,0:T(4,128)(2,1)S(1)} %reshape.68, f32[16,4,8]{2,1,0:T(4,128)S(1)} %fusion.43, f32[16,4,8,32]{3,2,1,0:T(8,128)S(1)} %convolution_multiply_fusion), kind=kOutput, calls=%fused_computation.8 | convolution fusion | flops 1114655 | bytes 231424 | tf_op jit(solution)/shard_map/chst,tchd->schd/dot_general | solution.py:47
  46.3 0.1 copy.32
  46.3 0.0 copy-start.2
  46.4 0.1 convert_element_type.81
  46.5 0.7 %copy-done.2 = bf16[128,256]{1,0:T(8,128)(2,1)S(1)} copy-done((bf16[128,256]{1,0:T(8,128)(2,1)S(1)}, bf16[128,256]{1,0:T(8,128)(2,1)}, u32[]{:S(2)}) %copy-start.2) | copy-done | bytes 65560
  47.2 0.8 %fusion.6 = bf16[8,16,256]{2,1,0:T(8,128)(2,1)} fusion(bf16[8,16,128]{2,1,0:T(8,128)(2,1)S(1)} %convert_element_type.81, bf16[8,16,256]{2,1,0:T(8,128)(2,1)S(1)} %get-tuple-element.3, bf16[128,256]{1,0:T(8,128)(2,1)S(1)} %copy-done.2), kind=kOutput, calls=%fused_computation.12 | convolution fusion | flops 8486912 | bytes 229376 | tf_op jit(solution)/shard_map/dot_general | solution.py:19
  (17 shorter events, 0.2 us)
Async XLA Ops:
  0.6 31.9 %copy-start = (bf16[128,256]{1,0:T(8,128)(2,1)S(1)}, bf16[128,256]{1,0:T(8,128)(2,1)}, u32[]{:S(2)}) copy-start(bf16[128,256]{1,0:T(8,128)(2,1)} %param.13) | copy-start | bytes 196612
  0.6 1.0 %copy-start.1 = (bf16[8,16,256]{2,1,0:T(8,128)(2,1)S(1)}, bf16[8,16,256]{2,1,0:T(8,128)(2,1)}, u32[]{:S(2)}) copy-start(bf16[8,16,256]{2,1,0:T(8,128)(2,1)} %param.9) | copy-start | bytes 196612
  0.7 1.2 %copy-start.3 = (bf16[256,128]{1,0:T(8,128)(2,1)S(1)}, bf16[256,128]{1,0:T(8,128)(2,1)}, u32[]{:S(2)}) copy-start(bf16[256,128]{1,0:T(8,128)(2,1)} %param.12) | copy-start | bytes 196612
  3.0 15.2 %copy-start.4 = (bf16[256,128]{1,0:T(8,128)(2,1)S(1)}, bf16[256,128]{1,0:T(8,128)(2,1)}, u32[]{:S(2)}) copy-start(bf16[256,128]{1,0:T(8,128)(2,1)} %param.10) | copy-start | bytes 196612
  18.1 1.5 %collective-permute-start = (bf16[4,8,16,256]{3,2,1,0:T(8,128)(2,1)S(1)}, bf16[4,8,16,256]{3,2,1,0:T(8,128)(2,1)S(1)}, u32[]{:S(2)}, u32[]{:S(2)}) collective-permute-start(bf16[4,8,16,256]{3,2,1,0:T(8,128)(2,1)S(1)} %all_to_all.15), channel_id=1, source_target_pairs={{0,1},{1,0},{2,3},{3,2},{4,5},{5,4},{6,7},{7,6},{8,9},{9,8},{10,11... | collective-permute-start | bytes 786440 | tf_op jit(solution)/shard_map/ppermute | solution.py:34
  22.4 8.7 %all-to-all-start.1 = ((f32[4,4,16,128]{3,2,1,0:T(8,128)}), f32[4,4,16,128]{3,2,1,0:T(8,128)S(1)}, u32[]{:S(2)}, u32[]{:S(2)}) async-start(f32[4,4,16,128]{3,2,1,0:T(8,128)} %broadcast_in_dim.10), calls=%async_computation.1 | async-start | bytes 262144 | tf_op jit(solution)/shard_map/all_to_all | solution.py:25
  32.5 1.0 %copy-start.6 = (bf16[256,128]{1,0:T(8,128)(2,1)S(1)}, bf16[256,128]{1,0:T(8,128)(2,1)}, u32[]{:S(2)}) copy-start(bf16[256,128]{1,0:T(8,128)(2,1)} %param.15) | copy-start | bytes 196612
  33.3 0.8 %copy-start.5 = (bf16[256,128]{1,0:T(8,128)(2,1)S(1)}, bf16[256,128]{1,0:T(8,128)(2,1)}, u32[]{:S(2)}) copy-start(bf16[256,128]{1,0:T(8,128)(2,1)} %param.16) | copy-start | bytes 196612
  35.1 3.5 %copy-start.7 = (bf16[256,128]{1,0:T(8,128)(2,1)S(1)}, bf16[256,128]{1,0:T(8,128)(2,1)}, u32[]{:S(2)}) copy-start(bf16[256,128]{1,0:T(8,128)(2,1)} %param.14) | copy-start | bytes 196612
  35.1 8.9 %all-to-all-start.2 = ((bf16[4,8,16,256]{3,2,1,0:T(8,128)(2,1)}), bf16[4,8,16,256]{3,2,1,0:T(8,128)(2,1)S(1)}, u32[]{:S(2)}, u32[]{:S(2)}) async-start(bf16[4,8,16,256]{3,2,1,0:T(8,128)(2,1)} %broadcast_in_dim.11), calls=%async_computation.2 | async-start | bytes 524288 | tf_op jit(solution)/shard_map/all_to_all | solution.py:25
  46.3 0.8 %copy-start.2 = (bf16[128,256]{1,0:T(8,128)(2,1)S(1)}, bf16[128,256]{1,0:T(8,128)(2,1)}, u32[]{:S(2)}) copy-start(bf16[128,256]{1,0:T(8,128)(2,1)} %param.17) | copy-start | bytes 196612

commit v2 on v1

--- a/solution.py
+++ b/solution.py
@@ -1,6 +1,8 @@
 import jax
 import jax.numpy as jnp
 from jax import lax
+from jax.experimental import pallas as pl
+from jax.experimental.pallas import tpu as pltpu
 from jax.sharding import PartitionSpec as P
 
 HEADS = 4
@@ -94,9 +96,255 @@
     return (row_update, layer_output)
 
 
+def norm_rows(values):
+    mean = jnp.mean(values, axis=-1, keepdims=True)
+    centred = values - mean
+    variance = jnp.mean(centred * centred, axis=-1, keepdims=True)
+    return (centred * lax.rsqrt(variance + 1e-05)).astype(jnp.bfloat16)
+
+
+def swap_groups(arrays, group):
+    lanes = arrays[0].shape[-1]
+    index = lax.broadcasted_iota(jnp.int32, arrays[0].shape, 1) // group
+    arrays = list(arrays)
+    step = len(arrays) // 2
+    while step:
+        low = (index // step) % 2 == 0
+        for first in range(len(arrays)):
+            if (first // step) % 2 == 0:
+                one, two = arrays[first], arrays[first + step]
+                shift = step * group
+                arrays[first] = jnp.where(low, one, pltpu.roll(two, shift, 1))
+                arrays[first + step] = jnp.where(low, pltpu.roll(one, lanes - shift, 1), two)
+        step //= 2
+    return arrays
+
+
+def contract_last(left, right):
+    return lax.dot_general(
+        left, right, (((1,), (1,)), ((), ())), preferred_element_type=jnp.float32
+    )
+
+
+def project_kernel(field_ref, key_ref, value_ref, query_ref, out_ref):
+    seq_dev, col_dev, width = field_ref.shape
+    heads, chips, cores = out_ref.shape[:3]
+    normed = norm_rows(field_ref[...].astype(jnp.float32).reshape(seq_dev * col_dev, width))
+    for kind, weight_ref in enumerate((key_ref, value_ref, query_ref)):
+        rows = project(normed, weight_ref[...])
+        for core in range(cores):
+            first = core * heads
+            tiles = [
+                rows[(first + place) * col_dev : (first + place + 1) * col_dev]
+                for place in range(heads)
+            ]
+            for head, tile in enumerate(swap_groups(tiles, HEAD_DIM)):
+                tile = tile.astype(jnp.bfloat16)
+                for chip in range(chips):
+                    out_ref[head, chip, core, kind] = tile
+
+
+def attend_kernel(scale, mine_ref, other_ref, field_ref, out_ref):
+    column = lax.axis_index("col")
+    core = lax.rem(column, 2)
+    seq, col, _, col_dev, lanes = mine_ref.shape
+    seq_dev = field_ref.shape[0]
+    logits = jnp.zeros((col_dev, col * col_dev), jnp.float32)
+    for ref in (mine_ref, other_ref):
+        for source in range(seq):
+            keys = ref[source, :, 0].reshape(col * col_dev, lanes)
+            logits += contract_last(ref[source, column, 2], keys)
+    logits = logits * scale
+    weights = jnp.exp(logits - jnp.max(logits, axis=-1, keepdims=True))
+    probs = (weights / jnp.sum(weights, axis=-1, keepdims=True)).astype(jnp.bfloat16)
+    for ref, half in ((mine_ref, core), (other_ref, 1 - core)):
+        for source in range(seq):
+            values = ref[source, :, 1].reshape(col * col_dev, lanes)
+            context = project(probs, values).astype(jnp.bfloat16)
+            for copy in range(seq):
+                out_ref[copy, half * seq + source] = context
+    start = 2 * seq
+    for part in range(field_ref.shape[2] // lanes):
+        field = field_ref[:, :, part * lanes : (part + 1) * lanes]
+        for copy in range(seq):
+            out_ref[copy, start : start + seq_dev] = field
+        start += seq_dev
+
+
+def finish_kernel(
+    parts_ref,
+    row_output_ref,
+    query_ref,
+    key_ref,
+    value_ref,
+    output_ref,
+    update_ref,
+    layer_ref,
+    updates,
+    middles,
+    normals,
+    queries,
+    keys,
+    values,
+    contexts,
+):
+    own = lax.axis_index("seq")
+    seq, tiles, col_dev, lanes = parts_ref.shape
+    seq_dev, _, width = update_ref.shape
+    rows = seq_dev * col_dev
+    seqs = seq * seq_dev
+    for source in range(seq):
+        context = []
+        for half in range(seq_dev // HEADS):
+            heads = [
+                parts_ref[head, half * seq + source].astype(jnp.float32) for head in range(HEADS)
+            ]
+            context += swap_groups(heads, HEAD_DIM)
+        context = jnp.concatenate(context, axis=0).astype(jnp.bfloat16)
+        update = project(context, row_output_ref[...]).astype(jnp.bfloat16)
+        start = seq * seq_dev // HEADS
+        field = jnp.concatenate(
+            [
+                parts_ref[source, first : first + seq_dev].reshape(rows, lanes)
+                for first in range(start, tiles, seq_dev)
+            ],
+            axis=1,
+        )
+        middle = (field.astype(jnp.float32) + update.astype(jnp.float32)).astype(jnp.bfloat16)
+        normal = norm_rows(middle.astype(jnp.float32))
+        place = slice(source * rows, (source + 1) * rows)
+        updates[place, :] = update
+        middles[place, :] = middle
+        normals[place, :] = normal
+        keys[place, :] = project(normal, key_ref[...]).astype(jnp.bfloat16).astype(jnp.float32)
+        values[place, :] = project(normal, value_ref[...]).astype(jnp.bfloat16).astype(jnp.float32)
+    mine = pl.ds(pl.multiple_of(own * rows, rows), rows)
+    update_ref[...] = updates[mine, :].reshape(update_ref.shape)
+    queries[...] = (
+        project(normals[mine, :], query_ref[...]).astype(jnp.bfloat16).astype(jnp.float32)
+    )
+    group = lanes // seqs
+    head_of = lax.broadcasted_iota(jnp.int32, (seq_dev, lanes), 1) // HEAD_DIM
+    size = group * seqs
+    row_column = lax.broadcasted_iota(jnp.int32, (group * HEADS * seq_dev, size), 0) // (
+        HEADS * seq_dev
+    )
+    same = row_column == lax.broadcasted_iota(jnp.int32, row_column.shape, 1) // seqs
+    for first in range(0, col_dev, group):
+        query, key, value = [], [], []
+        for column in range(first, first + group):
+            row = queries[pl.ds(column, seq_dev, stride=col_dev), :]
+            query += [jnp.where(head_of == head, row, 0.0) for head in range(HEADS)]
+            key.append(keys[pl.ds(column, seqs, stride=col_dev), :])
+            value.append(values[pl.ds(column, seqs, stride=col_dev), :])
+        query, key, value = (
+            jnp.concatenate(part, axis=0).astype(jnp.bfloat16) for part in (query, key, value)
+        )
+        scores = jnp.where(
+            same, contract_last(query, key) * float(HEAD_DIM) ** (-0.5), -jnp.inf
+        )
+        weights = jnp.exp(scores - jnp.max(scores, axis=-1, keepdims=True))
+        probs = (weights / jnp.sum(weights, axis=-1, keepdims=True)).astype(jnp.bfloat16)
+        context = project(probs, value)
+        for place in range(group):
+            total = jnp.zeros((seq_dev, lanes), jnp.float32)
+            for head in range(HEADS):
+                at = (place * HEADS + head) * seq_dev
+                total = jnp.where(head_of == head, context[at : at + seq_dev], total)
+            contexts[pl.ds(first + place, seq_dev, stride=col_dev), :] = total
+    layer = middles[mine, :].astype(jnp.float32) + project(
+        contexts[...].astype(jnp.bfloat16), output_ref[...]
+    )
+    layer_ref[...] = layer.astype(jnp.bfloat16).reshape(layer_ref.shape)
+
+
+def by_head(
+    alignment,
+    row_query,
+    row_key,
+    row_value,
+    row_output,
+    column_query,
+    column_key,
+    column_value,
+    column_output,
+):
+    seq_dev, col_dev, width = alignment.shape
+    inner = row_query.shape[1]
+    seq, col = lax.axis_size("seq"), lax.axis_size("col")
+    scale = float(HEAD_DIM * seq_dev * seq) ** (-0.5)
+    bf16 = jnp.bfloat16
+    vmem = pl.BlockSpec(memory_space=pltpu.VMEM)
+    blocks = pl.pallas_call(
+        project_kernel,
+        out_shape=jax.ShapeDtypeStruct((seq, col // 2, 2, 3, col_dev, inner), bf16),
+        in_specs=[vmem] * 4,
+        out_specs=vmem,
+        compiler_params=pltpu.CompilerParams(vmem_limit_bytes=8 << 20),
+        name="project",
+    )(alignment, row_key, row_value, row_query)
+    mine = lax.all_to_all(
+        blocks.reshape(seq * col, 3, col_dev, inner), ("seq", "col"), 0, 0
+    )
+    other = lax.ppermute(mine, "col", [(i, i ^ 1) for i in range(col)])
+    shape = (seq, col, 3, col_dev, inner)
+    tiles = seq_dev // HEADS * seq + width // inner * seq_dev
+    parts = pl.pallas_call(
+        lambda *refs: attend_kernel(scale, *refs),
+        out_shape=jax.ShapeDtypeStruct((seq, tiles, col_dev, inner), bf16),
+        in_specs=[vmem] * 3,
+        out_specs=vmem,
+        compiler_params=pltpu.CompilerParams(vmem_limit_bytes=8 << 20),
+        name="attend",
+    )(mine.reshape(shape), other.reshape(shape), alignment)
+    parts = lax.all_to_all(parts, "seq", 0, 0)
+    total = seq * seq_dev * col_dev
+    local = seq_dev * col_dev
+    like = jax.ShapeDtypeStruct(alignment.shape, bf16)
+    f32 = jnp.float32
+    return pl.pallas_call(
+        finish_kernel,
+        out_shape=(like, like),
+        in_specs=[vmem] * 6,
+        out_specs=(vmem, vmem),
+        scratch_shapes=[
+            pltpu.VMEM((total, width), bf16),
+            pltpu.VMEM((total, width), bf16),
+            pltpu.VMEM((total, width), bf16),
+            pltpu.VMEM((local, inner), f32),
+            pltpu.VMEM((total, inner), f32),
+            pltpu.VMEM((total, inner), f32),
+            pltpu.VMEM((local, inner), f32),
+        ],
+        compiler_params=pltpu.CompilerParams(vmem_limit_bytes=8 << 20),
+        name="finish",
+    )(parts, row_output, column_query, column_key, column_value, column_output)
+
+
+def suits_by_head(seq, col, seq_dev, col_dev, width, inner):
+    return (
+        seq == HEADS
+        and col % 2 == 0
+        and seq_dev == 2 * HEADS
+        and col_dev % 16 == 0
+        and inner == HEADS * HEAD_DIM
+        and inner == 128
+        and width % inner == 0
+        and inner % (seq * seq_dev) == 0
+        and col_dev % (inner // (seq * seq_dev)) == 0
+        and seq * seq_dev * col_dev <= 1024
+        and col * col_dev <= 512
+    )
+
+
 def solution(mesh):
+    def choose(*args):
+        seq_dev, col_dev, width = args[0].shape
+        sizes = (mesh.shape["seq"], mesh.shape["col"], seq_dev, col_dev, width, args[1].shape[1])
+        return (by_head if suits_by_head(*sizes) else on_device)(*args)
+
     return jax.shard_map(
-        on_device,
+        choose,
         mesh=mesh,
         in_specs=(P("seq", "col", None), P(), P(), P(), P(), P(), P(), P(), P()),
         out_specs=(P("seq", "col", None), P("seq", "col", None)),

time: 48.6 us -> 41.6 us (0.86)
  blocking collectives: 15.2 us -> 30.8 us
  waiting for transfers between devices: 10.7 us -> 1.61 us
  starting transfers between devices: 7.25 us -> 0.12 us
  matrix products: 6.53 us -> 0 us
  Pallas kernels: 0 us -> 4.57 us
  other arithmetic: 2.06 us -> 0 us
  local copies, waits for them, and re-layouts: 5.28 us -> 3.38 us
    all_to_all x1 -> x2, blocking collectives: 15.2 us -> 30.8 us  [the longest x1 20.6 us: by_head(): lax.all_to_all(blocks.reshape(seq * col, 3, col_dev, inner), ('seq', 'col...]
    all_to_all x2 -> x0, waiting for transfers between devices: 9.59 us -> none  [gather(): return lax.all_to_all(copies, axis, 0, 0, axis_index_groups=groups)]
    all_to_all x2 -> x0, starting transfers between devices: 7.25 us -> none  [gather(): return lax.all_to_all(copies, axis, 0, 0, axis_index_groups=groups)]
    dot_general x10 -> x0, matrix products: 6.53 us -> none  [the longest x6 3.26 us: project(): return jnp.dot(field, weight, preferred_element_type=jnp.float32)]
    pallas_call x0 -> x3, Pallas kernels: none -> 4.57 us  [the longest x1 3.37 us: by_head(): pl.pallas_call(finish_kernel, out_shape=(like, like), in_specs=[vmem] * 6...]
    unnamed x17 -> x18, local copies, waits for them, and re-layouts: 1.41 us -> 3.38 us
    reshape x6 -> x0, local copies, waits for them, and re-layouts: 1.53 us -> none  [the longest x1 0.41 us: on_device(): every[..., :inner]]
    broadcast_in_dim x4 -> x0, local copies, waits for them, and re-layouts: 1.51 us -> none  [gather(): copies = jnp.broadcast_to(block[None], (size,) + block.shape)]
  transfers between devices with their start and end apart: 3 -> 1, of which waited for: 3 -> 1; matrix products, arithmetic and copies ran while one was open for 2% -> 0% of each run, Pallas kernels for 0% -> 0%
where the time goes in v2:
time: 41.6 us; the launch traced here: 41.2 us
  blocking collectives  30.8 us (74%)
  Pallas kernels  4.57 us (11%)
  local copies, waits for them, and re-layouts  3.38 us (8%)
  waiting for transfers between devices  1.61 us (4%)
  between operations  0.72 us (2%)
    all_to_all x1, blocking collectives, by_head(): lax.all_to_all(blocks.reshape(seq * col, 3, col_dev, inner), ('seq', 'col...  20.6 us
    all_to_all x1, blocking collectives, by_head(): parts = lax.all_to_all(parts, 'seq', 0, 0)  10.2 us
    unnamed x18, local copies, waits for them, and re-layouts  3.38 us
    pallas_call x1, Pallas kernels, by_head(): pl.pallas_call(finish_kernel, out_shape=(like, like), in_specs=[vmem] * 6...  3.37 us
    ppermute x1, waiting for transfers between devices, by_head(): other = lax.ppermute(mine, 'col', [(i, i ^ 1) for i in range(col)])  1.61 us
  transfers between devices with their start and end apart: 1, of which 1 were waited for; matrix products, arithmetic and copies ran while one was open for 0% of the time, Pallas kernels for 0%

profile of v2, /device:TPU:0, one launch (start us, length us, event | category | flops | bytes accessed | tf_op | source)
XLA Modules:
  0.0 41.2 jit_solution(18274492610038972362)
XLA Ops:
  0.6 0.0 copy-start
  0.6 0.8 %copy-done = bf16[8,16,256]{2,1,0:T(8,128)(2,1)S(1)} copy-done((bf16[8,16,256]{2,1,0:T(8,128)(2,1)S(1)}, bf16[8,16,256]{2,1,0:T(8,128)(2,1)}, u32[]{:S(2)}) %copy-start) | copy-done | bytes 65560
  1.5 0.0 copy-start.1
  1.5 0.8 %copy-done.1 = bf16[256,128]{1,0:T(8,128)(2,1)S(1)} copy-done((bf16[256,128]{1,0:T(8,128)(2,1)S(1)}, bf16[256,128]{1,0:T(8,128)(2,1)}, u32[]{:S(2)}) %copy-start.1) | copy-done | bytes 65560
  2.3 0.0 copy-start.2
  2.3 0.8 %copy-done.2 = bf16[256,128]{1,0:T(8,128)(2,1)S(1)} copy-done((bf16[256,128]{1,0:T(8,128)(2,1)S(1)}, bf16[256,128]{1,0:T(8,128)(2,1)}, u32[]{:S(2)}) %copy-start.2) | copy-done | bytes 65560
  3.2 0.0 copy-start.3
  3.2 0.8 %copy-done.3 = bf16[256,128]{1,0:T(8,128)(2,1)S(1)} copy-done((bf16[256,128]{1,0:T(8,128)(2,1)S(1)}, bf16[256,128]{1,0:T(8,128)(2,1)}, u32[]{:S(2)}) %copy-start.3) | copy-done | bytes 65560
  4.0 0.5 %project.1 = bf16[4,4,2,3,16,128]{5,4,3,2,1,0:T(8,128)(2,1)S(1)} custom-call(bf16[8,16,256]{2,1,0:T(8,128)(2,1)S(1)} %copy-done, bf16[256,128]{1,0:T(8,128)(2,1)S(1)} %copy-done.1, bf16[256,128]{1,0:T(8,128)(2,1)S(1)} %copy-done.2, bf16[256,128]{1,0:T(8,128)(2,1)S(1)} %copy-done.3), custom_call_target="tpu_custom_call" | custom-call | tf_op jit(solution)/shard_map/project/pallas_call | solution.py:278
  4.5 20.6 %all_to_all.10 = bf16[32,3,16,128]{3,2,1,0:T(8,128)(2,1)S(1)} all-to-all(bf16[32,3,16,128]{3,2,1,0:T(8,128)(2,1)S(1)} %bitcast.4), channel_id=1, replica_groups=mesh['seq'=4,'col'=8] {'seq','col'}, dimensions={0} | all-to-all | bytes 786432 | tf_op jit(solution)/shard_map/all_to_all | solution.py:286
  25.1 0.1 collective-permute-start
  25.2 1.6 %collective-permute-done = bf16[32,3,16,128]{3,2,1,0:T(8,128)(2,1)S(1)} collective-permute-done((bf16[32,3,16,128]{3,2,1,0:T(8,128)(2,1)S(1)}, bf16[32,3,16,128]{3,2,1,0:T(8,128)(2,1)S(1)}, u32[]{:S(2)}, u32[]{:S(2)}) %collective-permute-start) | collective-permute-done | bytes 393248 | tf_op jit(solution)/shard_map/ppermute | solution.py:289
  26.8 0.7 %attend.1 = bf16[4,24,16,128]{3,2,1,0:T(8,128)(2,1)S(1)} custom-call(bf16[4,8,3,16,128]{4,3,2,1,0:T(8,128)(2,1)S(1)} %bitcast.3, bf16[4,8,3,16,128]{4,3,2,1,0:T(8,128)(2,1)S(1)} %bitcast.5, bf16[8,16,256]{2,1,0:T(8,128)(2,1)S(1)} %copy-done), custom_call_target="tpu_custom_call" | custom-call | tf_op jit(solution)/shard_map/attend/pallas_call | solution.py:292
  27.5 0.0 copy-start.4
  27.5 0.0 copy-start.5
  27.5 0.0 copy-start.6
  27.5 0.0 copy-start.7
  27.5 0.0 copy-start.8
  27.5 10.2 %all_to_all.11.parts_ref = bf16[4,24,16,128]{3,2,1,0:T(8,128)(2,1)S(1)} all-to-all(bf16[4,24,16,128]{3,2,1,0:T(8,128)(2,1)S(1)} %attend.1), channel_id=1, replica_groups=mesh['seq'=4,'col'=8] {'seq'}, dimensions={0} | all-to-all | bytes 786432 | tf_op jit(solution)/shard_map/all_to_all | solution.py:300
  37.8 0.0 copy-done.4
  37.8 0.0 copy-done.5
  37.8 0.0 copy-done.6
  37.8 0.0 copy-done.7
  37.8 0.0 copy-done.8
  37.8 3.4 %finish.1 = (bf16[8,16,256]{2,1,0:T(8,128)(2,1)}, bf16[8,16,256]{2,1,0:T(8,128)(2,1)}) custom-call(bf16[4,24,16,128]{3,2,1,0:T(8,128)(2,1)S(1)} %all_to_all.11.parts_ref, bf16[128,256]{1,0:T(8,128)(2,1)S(1)} %copy-done.4, bf16[256,128]{1,0:T(8,128)(2,1)S(1)} %copy-done.5, bf16[256,128]{1,0:T(8,128)(2,1)S(1)} %copy-done.6, bf16[256,128]{1,0:T(8,128)(2,1)S(1)} %copy-done.7, ...), custom_call_target="tpu_custom_call" | custom-call | tf_op jit(solution)/shard_map/finish/pallas_call | solution.py:305
Async XLA Ops:
  0.6 0.8 %copy-start = (bf16[8,16,256]{2,1,0:T(8,128)(2,1)S(1)}, bf16[8,16,256]{2,1,0:T(8,128)(2,1)}, u32[]{:S(2)}) copy-start(bf16[8,16,256]{2,1,0:T(8,128)(2,1)} %refs_2_.1) | copy-start | bytes 196612
  1.5 0.8 %copy-start.1 = (bf16[256,128]{1,0:T(8,128)(2,1)S(1)}, bf16[256,128]{1,0:T(8,128)(2,1)}, u32[]{:S(2)}) copy-start(bf16[256,128]{1,0:T(8,128)(2,1)} %key_ref.2) | copy-start | bytes 196612
  2.3 0.8 %copy-start.2 = (bf16[256,128]{1,0:T(8,128)(2,1)S(1)}, bf16[256,128]{1,0:T(8,128)(2,1)}, u32[]{:S(2)}) copy-start(bf16[256,128]{1,0:T(8,128)(2,1)} %value_ref.2) | copy-start | bytes 196612
  3.2 0.8 %copy-start.3 = (bf16[256,128]{1,0:T(8,128)(2,1)S(1)}, bf16[256,128]{1,0:T(8,128)(2,1)}, u32[]{:S(2)}) copy-start(bf16[256,128]{1,0:T(8,128)(2,1)} %query_ref.2) | copy-start | bytes 196612
  25.1 1.7 %collective-permute-start = (bf16[32,3,16,128]{3,2,1,0:T(8,128)(2,1)S(1)}, bf16[32,3,16,128]{3,2,1,0:T(8,128)(2,1)S(1)}, u32[]{:S(2)}, u32[]{:S(2)}) collective-permute-start(bf16[32,3,16,128]{3,2,1,0:T(8,128)(2,1)S(1)} %all_to_all.10), channel_id=1, source_target_pairs={{0,1},{1,0},{2,3},{3,2},{4,5},{5,4},{6,7},{7,6},{8,9},{9,8},{10,11... | collective-permute-start | bytes 1179656 | tf_op jit(solution)/shard_map/ppermute | solution.py:289
  27.5 10.3 %copy-start.4 = (bf16[128,256]{1,0:T(8,128)(2,1)S(1)}, bf16[128,256]{1,0:T(8,128)(2,1)}, u32[]{:S(2)}) copy-start(bf16[128,256]{1,0:T(8,128)(2,1)} %row_output_ref.1) | copy-start | bytes 196612
  27.5 10.3 %copy-start.5 = (bf16[256,128]{1,0:T(8,128)(2,1)S(1)}, bf16[256,128]{1,0:T(8,128)(2,1)}, u32[]{:S(2)}) copy-start(bf16[256,128]{1,0:T(8,128)(2,1)} %query_ref.3) | copy-start | bytes 196612
  27.5 10.3 %copy-start.6 = (bf16[256,128]{1,0:T(8,128)(2,1)S(1)}, bf16[256,128]{1,0:T(8,128)(2,1)}, u32[]{:S(2)}) copy-start(bf16[256,128]{1,0:T(8,128)(2,1)} %key_ref.3) | copy-start | bytes 196612
  27.5 10.3 %copy-start.7 = (bf16[256,128]{1,0:T(8,128)(2,1)S(1)}, bf16[256,128]{1,0:T(8,128)(2,1)}, u32[]{:S(2)}) copy-start(bf16[256,128]{1,0:T(8,128)(2,1)} %value_ref.3) | copy-start | bytes 196612
  27.5 10.3 %copy-start.8 = (bf16[128,256]{1,0:T(8,128)(2,1)S(1)}, bf16[128,256]{1,0:T(8,128)(2,1)}, u32[]{:S(2)}) copy-start(bf16[128,256]{1,0:T(8,128)(2,1)} %output_ref.1) | copy-start | bytes 196612

commit v3 on v2

--- a/solution.py
+++ b/solution.py
@@ -126,11 +126,21 @@
     )
 
 
-def project_kernel(field_ref, key_ref, value_ref, query_ref, out_ref):
+def project_kernel(*refs):
+    sources, out_ref, held, sems = refs[:4], refs[4], refs[5:9], refs[9]
+    copies = [
+        pltpu.make_async_copy(source, ref, sems.at[place])
+        for place, (source, ref) in enumerate(zip(sources, held))
+    ]
+    for copy in copies:
+        copy.start()
+    field_ref, key_ref, value_ref, query_ref = held
     seq_dev, col_dev, width = field_ref.shape
     heads, chips, cores = out_ref.shape[:3]
+    copies[0].wait()
     normed = norm_rows(field_ref[...].astype(jnp.float32).reshape(seq_dev * col_dev, width))
     for kind, weight_ref in enumerate((key_ref, value_ref, query_ref)):
+        copies[kind + 1].wait()
         rows = project(normed, weight_ref[...])
         for core in range(cores):
             first = core * heads
@@ -275,14 +285,18 @@
     scale = float(HEAD_DIM * seq_dev * seq) ** (-0.5)
     bf16 = jnp.bfloat16
     vmem = pl.BlockSpec(memory_space=pltpu.VMEM)
+    sources = (alignment, row_key, row_value, row_query)
     blocks = pl.pallas_call(
         project_kernel,
         out_shape=jax.ShapeDtypeStruct((seq, col // 2, 2, 3, col_dev, inner), bf16),
-        in_specs=[vmem] * 4,
+        in_specs=[pl.BlockSpec(memory_space=pltpu.HBM)] * 4,
         out_specs=vmem,
+        scratch_shapes=[pltpu.VMEM(alignment.shape, bf16)]
+        + [pltpu.VMEM(row_key.shape, bf16)] * 3
+        + [pltpu.SemaphoreType.DMA((4,))],
         compiler_params=pltpu.CompilerParams(vmem_limit_bytes=8 << 20),
         name="project",
-    )(alignment, row_key, row_value, row_query)
+    )(*(pltpu.with_memory_space_constraint(x, pltpu.HBM) for x in sources))
     mine = lax.all_to_all(
         blocks.reshape(seq * col, 3, col_dev, inner), ("seq", "col"), 0, 0
     )

time: 41.6 us -> 39.6 us (0.952)
  local copies, waits for them, and re-layouts: 3.38 us -> 0.04 us
  Pallas kernels: 4.57 us -> 6.05 us
    unnamed x18 -> x12, local copies, waits for them, and re-layouts: 3.38 us -> 0.04 us
    pallas_call x1, Pallas kernels: 0.49 us -> 1.98 us  [by_head(): pl.pallas_call(project_kernel, out_shape=jax.ShapeDtypeStruct((seq, col /...]
where the time goes in v3:
time: 39.6 us; the launch traced here: 39.3 us
  blocking collectives  30.8 us (78%)
  Pallas kernels  6.05 us (15%)
  waiting for transfers between devices  1.61 us (4%)
  between operations  0.72 us (2%)
    all_to_all x1, blocking collectives, by_head(): lax.all_to_all(blocks.reshape(seq * col, 3, col_dev, inner), ('seq', 'col...  20.6 us
    all_to_all x1, blocking collectives, by_head(): parts = lax.all_to_all(parts, 'seq', 0, 0)  10.2 us
    pallas_call x1, Pallas kernels, by_head(): pl.pallas_call(finish_kernel, out_shape=(like, like), in_specs=[vmem] * 6...  3.37 us
    pallas_call x1, Pallas kernels, by_head(): pl.pallas_call(project_kernel, out_shape=jax.ShapeDtypeStruct((seq, col /...  1.98 us
    ppermute x1, waiting for transfers between devices, by_head(): other = lax.ppermute(mine, 'col', [(i, i ^ 1) for i in range(col)])  1.61 us
  transfers between devices with their start and end apart: 1, of which 1 were waited for; matrix products, arithmetic and copies ran while one was open for 0% of the time, Pallas kernels for 0%

profile of v3, /device:TPU:0, one launch (start us, length us, event | category | flops | bytes accessed | tf_op | source)
XLA Modules:
  0.0 39.3 jit_solution(11421870580442103923)
XLA Ops:
  0.6 2.0 %project.1 = bf16[4,4,2,3,16,128]{5,4,3,2,1,0:T(8,128)(2,1)S(1)} custom-call(bf16[8,16,256]{2,1,0:T(8,128)(2,1)} %refs_2_.3, bf16[256,128]{1,0:T(8,128)(2,1)} %refs_1_.1, bf16[256,128]{1,0:T(8,128)(2,1)} %refs_2_.2, bf16[256,128]{1,0:T(8,128)(2,1)} %refs_3_.1), custom_call_target="tpu_custom_call" | custom-call | tf_op jit(solution)/shard_map/project/pallas_call | solution.py:289
  2.6 0.0 copy-start
  2.6 20.6 %all_to_all.10 = bf16[32,3,16,128]{3,2,1,0:T(8,128)(2,1)S(1)} all-to-all(bf16[32,3,16,128]{3,2,1,0:T(8,128)(2,1)S(1)} %bitcast.4), channel_id=1, replica_groups=mesh['seq'=4,'col'=8] {'seq','col'}, dimensions={0} | all-to-all | bytes 786432 | tf_op jit(solution)/shard_map/all_to_all | solution.py:300
  23.2 0.1 collective-permute-start
  23.3 1.6 %collective-permute-done = bf16[32,3,16,128]{3,2,1,0:T(8,128)(2,1)S(1)} collective-permute-done((bf16[32,3,16,128]{3,2,1,0:T(8,128)(2,1)S(1)}, bf16[32,3,16,128]{3,2,1,0:T(8,128)(2,1)S(1)}, u32[]{:S(2)}, u32[]{:S(2)}) %collective-permute-start) | collective-permute-done | bytes 393248 | tf_op jit(solution)/shard_map/ppermute | solution.py:303
  24.9 0.0 copy-done
  24.9 0.7 %attend.1 = bf16[4,24,16,128]{3,2,1,0:T(8,128)(2,1)S(1)} custom-call(bf16[4,8,3,16,128]{4,3,2,1,0:T(8,128)(2,1)S(1)} %bitcast.3, bf16[4,8,3,16,128]{4,3,2,1,0:T(8,128)(2,1)S(1)} %bitcast.5, bf16[8,16,256]{2,1,0:T(8,128)(2,1)S(1)} %copy-done), custom_call_target="tpu_custom_call" | custom-call | tf_op jit(solution)/shard_map/attend/pallas_call | solution.py:306
  25.6 0.0 copy-start.1
  25.6 0.0 copy-start.2
  25.7 0.0 copy-start.3
  25.7 0.0 copy-start.4
  25.7 0.0 copy-start.5
  25.7 10.2 %all_to_all.11.parts_ref = bf16[4,24,16,128]{3,2,1,0:T(8,128)(2,1)S(1)} all-to-all(bf16[4,24,16,128]{3,2,1,0:T(8,128)(2,1)S(1)} %attend.1), channel_id=1, replica_groups=mesh['seq'=4,'col'=8] {'seq'}, dimensions={0} | all-to-all | bytes 786432 | tf_op jit(solution)/shard_map/all_to_all | solution.py:314
  35.9 0.0 copy-done.1
  35.9 0.0 copy-done.2
  35.9 0.0 copy-done.3
  35.9 0.0 copy-done.4
  35.9 0.0 copy-done.5
  35.9 3.4 %finish.1 = (bf16[8,16,256]{2,1,0:T(8,128)(2,1)}, bf16[8,16,256]{2,1,0:T(8,128)(2,1)}) custom-call(bf16[4,24,16,128]{3,2,1,0:T(8,128)(2,1)S(1)} %all_to_all.11.parts_ref, bf16[128,256]{1,0:T(8,128)(2,1)S(1)} %copy-done.1, bf16[256,128]{1,0:T(8,128)(2,1)S(1)} %copy-done.2, bf16[256,128]{1,0:T(8,128)(2,1)S(1)} %copy-done.3, bf16[256,128]{1,0:T(8,128)(2,1)S(1)} %copy-done.4, ...), custom_call_target="tpu_custom_call" | custom-call | tf_op jit(solution)/shard_map/finish/pallas_call | solution.py:319
Async XLA Ops:
  2.6 22.3 %copy-start = (bf16[8,16,256]{2,1,0:T(8,128)(2,1)S(1)}, bf16[8,16,256]{2,1,0:T(8,128)(2,1)}, u32[]{:S(2)}) copy-start(bf16[8,16,256]{2,1,0:T(8,128)(2,1)} %refs_2_.3) | copy-start | bytes 196612
  23.2 1.7 %collective-permute-start = (bf16[32,3,16,128]{3,2,1,0:T(8,128)(2,1)S(1)}, bf16[32,3,16,128]{3,2,1,0:T(8,128)(2,1)S(1)}, u32[]{:S(2)}, u32[]{:S(2)}) collective-permute-start(bf16[32,3,16,128]{3,2,1,0:T(8,128)(2,1)S(1)} %all_to_all.10), channel_id=1, source_target_pairs={{0,1},{1,0},{2,3},{3,2},{4,5},{5,4},{6,7},{7,6},{8,9},{9,8},{10,11... | collective-permute-start | bytes 1179656 | tf_op jit(solution)/shard_map/ppermute | solution.py:303
  25.6 10.3 %copy-start.1 = (bf16[128,256]{1,0:T(8,128)(2,1)S(1)}, bf16[128,256]{1,0:T(8,128)(2,1)}, u32[]{:S(2)}) copy-start(bf16[128,256]{1,0:T(8,128)(2,1)} %row_output_ref.1) | copy-start | bytes 196612
  25.6 10.3 %copy-start.2 = (bf16[256,128]{1,0:T(8,128)(2,1)S(1)}, bf16[256,128]{1,0:T(8,128)(2,1)}, u32[]{:S(2)}) copy-start(bf16[256,128]{1,0:T(8,128)(2,1)} %query_ref.1) | copy-start | bytes 196612
  25.7 10.3 %copy-start.3 = (bf16[256,128]{1,0:T(8,128)(2,1)S(1)}, bf16[256,128]{1,0:T(8,128)(2,1)}, u32[]{:S(2)}) copy-start(bf16[256,128]{1,0:T(8,128)(2,1)} %key_ref.1) | copy-start | bytes 196612
  25.7 10.3 %copy-start.4 = (bf16[256,128]{1,0:T(8,128)(2,1)S(1)}, bf16[256,128]{1,0:T(8,128)(2,1)}, u32[]{:S(2)}) copy-start(bf16[256,128]{1,0:T(8,128)(2,1)} %value_ref.1) | copy-start | bytes 196612
  25.7 10.3 %copy-start.5 = (bf16[128,256]{1,0:T(8,128)(2,1)S(1)}, bf16[128,256]{1,0:T(8,128)(2,1)}, u32[]{:S(2)}) copy-start(bf16[128,256]{1,0:T(8,128)(2,1)} %output_ref.1) | copy-start | bytes 196612

commit v4 on v3

--- a/solution.py
+++ b/solution.py
@@ -1,9 +1,12 @@
+import functools
+
 import jax
 import jax.numpy as jnp
 from jax import lax
 from jax.experimental import pallas as pl
 from jax.experimental.pallas import tpu as pltpu
 from jax.sharding import PartitionSpec as P
+
 
 HEADS = 4
 HEAD_DIM = 32
@@ -63,7 +66,7 @@
     column_value,
     column_output,
 ):
-    seq_dev, col_dev, width = alignment.shape
+    seq_dev, col_dev, _ = alignment.shape
     inner = row_query.shape[1]
     scale = float(HEAD_DIM * seq_dev * lax.axis_size("seq")) ** (-0.5)
     normed = layer_norm(alignment)
@@ -127,19 +130,19 @@
 
 
 def project_kernel(*refs):
-    sources, out_ref, held, sems = refs[:4], refs[4], refs[5:9], refs[9]
+    sources, out_ref, held, sems = refs[:3], refs[3], refs[4:7], refs[7]
     copies = [
         pltpu.make_async_copy(source, ref, sems.at[place])
         for place, (source, ref) in enumerate(zip(sources, held))
     ]
     for copy in copies:
         copy.start()
-    field_ref, key_ref, value_ref, query_ref = held
+    field_ref, key_ref, value_ref = held
     seq_dev, col_dev, width = field_ref.shape
     heads, chips, cores = out_ref.shape[:3]
     copies[0].wait()
     normed = norm_rows(field_ref[...].astype(jnp.float32).reshape(seq_dev * col_dev, width))
-    for kind, weight_ref in enumerate((key_ref, value_ref, query_ref)):
+    for kind, weight_ref in enumerate((key_ref, value_ref)):
         copies[kind + 1].wait()
         rows = project(normed, weight_ref[...])
         for core in range(cores):
@@ -154,56 +157,73 @@
                     out_ref[head, chip, core, kind] = tile
 
 
-def attend_kernel(scale, mine_ref, other_ref, field_ref, out_ref):
-    column = lax.axis_index("col")
-    core = lax.rem(column, 2)
+def query_kernel(*refs):
+    fields, (weight_ref, mine_ref, query_ref, logits_ref) = refs[:-4], refs[-4:]
+    own, half = lax.axis_index("seq"), lax.rem(lax.axis_index("col"), 2)
+    seq_dev, col_dev, width = fields[0].shape
+    seq, col, _, _, lanes = mine_ref.shape
+    group = lax.broadcasted_iota(jnp.int32, weight_ref.shape, 1) // HEAD_DIM
+    weight = weight_ref[...].astype(jnp.float32)
+    spread = []
+    for place in range(HEADS):
+        shift = lax.rem((place + HEADS - own) * HEAD_DIM, lanes)
+        spread.append(jnp.where(group == place, pltpu.roll(weight, shift, 1), 0.0))
+    spread = jnp.concatenate(spread, axis=0).astype(jnp.bfloat16)
+    normed = []
+    for field_ref in fields:
+        rows = norm_rows(field_ref[...].astype(jnp.float32).reshape(seq_dev * col_dev, width))
+        for first in range(0, seq_dev, HEADS):
+            normed.append(
+                jnp.concatenate(
+                    [
+                        rows[place * col_dev : (place + 1) * col_dev]
+                        for place in range(first, first + HEADS)
+                    ],
+                    axis=1,
+                )
+            )
+    queries = project(jnp.concatenate(normed, axis=0), spread).astype(jnp.bfloat16)
+    halves = seq_dev // HEADS
+    for place in range(seq):
+        for part in range(halves):
+            start = (place * halves + part) * col_dev
+            query_ref[part, own ^ place] = queries[start : start + col_dev]
+    logits = jnp.zeros(logits_ref.shape, jnp.float32)
+    for source in range(seq):
+        keys = mine_ref[source, :, 0].reshape(col * col_dev, lanes)
+        logits += contract_last(query_ref[half, source], keys)
+    logits_ref[...] = logits
+
+
+def attend_kernel(scale, mine_ref, other_ref, query_ref, logits_ref, out_ref):
+    half = lax.rem(lax.axis_index("col"), 2)
     seq, col, _, col_dev, lanes = mine_ref.shape
-    seq_dev = field_ref.shape[0]
-    logits = jnp.zeros((col_dev, col * col_dev), jnp.float32)
-    for ref in (mine_ref, other_ref):
-        for source in range(seq):
-            keys = ref[source, :, 0].reshape(col * col_dev, lanes)
-            logits += contract_last(ref[source, column, 2], keys)
+    logits = logits_ref[...]
+    for source in range(seq):
+        keys = other_ref[source, :, 0].reshape(col * col_dev, lanes)
+        logits += contract_last(query_ref[1 - half, source], keys)
     logits = logits * scale
     weights = jnp.exp(logits - jnp.max(logits, axis=-1, keepdims=True))
     probs = (weights / jnp.sum(weights, axis=-1, keepdims=True)).astype(jnp.bfloat16)
-    for ref, half in ((mine_ref, core), (other_ref, 1 - core)):
+    for ref, part in ((mine_ref, half), (other_ref, 1 - half)):
         for source in range(seq):
             values = ref[source, :, 1].reshape(col * col_dev, lanes)
             context = project(probs, values).astype(jnp.bfloat16)
             for copy in range(seq):
-                out_ref[copy, half * seq + source] = context
-    start = 2 * seq
-    for part in range(field_ref.shape[2] // lanes):
-        field = field_ref[:, :, part * lanes : (part + 1) * lanes]
-        for copy in range(seq):
-            out_ref[copy, start : start + seq_dev] = field
-        start += seq_dev
-
-
-def finish_kernel(
-    parts_ref,
-    row_output_ref,
-    query_ref,
-    key_ref,
-    value_ref,
-    output_ref,
-    update_ref,
-    layer_ref,
-    updates,
-    middles,
-    normals,
-    queries,
-    keys,
-    values,
-    contexts,
-):
+                out_ref[copy, part * seq + source] = context
+
+
+def finish_kernel(*refs):
+    fields, refs = refs[:-12], refs[-12:]
+    (parts_ref, row_output_ref, query_ref, key_ref, value_ref, output_ref) = refs[:6]
+    update_ref, layer_ref, queries, keys, values, contexts = refs[6:]
     own = lax.axis_index("seq")
-    seq, tiles, col_dev, lanes = parts_ref.shape
+    seq, _, col_dev, lanes = parts_ref.shape
     seq_dev, _, width = update_ref.shape
     rows = seq_dev * col_dev
     seqs = seq * seq_dev
-    for source in range(seq):
+    for place, field_ref in enumerate(fields):
+        source = own ^ place
         context = []
         for half in range(seq_dev // HEADS):
             heads = [
@@ -212,27 +232,18 @@
             context += swap_groups(heads, HEAD_DIM)
         context = jnp.concatenate(context, axis=0).astype(jnp.bfloat16)
         update = project(context, row_output_ref[...]).astype(jnp.bfloat16)
-        start = seq * seq_dev // HEADS
-        field = jnp.concatenate(
-            [
-                parts_ref[source, first : first + seq_dev].reshape(rows, lanes)
-                for first in range(start, tiles, seq_dev)
-            ],
-            axis=1,
-        )
+        field = field_ref[...].reshape(rows, width)
         middle = (field.astype(jnp.float32) + update.astype(jnp.float32)).astype(jnp.bfloat16)
         normal = norm_rows(middle.astype(jnp.float32))
-        place = slice(source * rows, (source + 1) * rows)
-        updates[place, :] = update
-        middles[place, :] = middle
-        normals[place, :] = normal
-        keys[place, :] = project(normal, key_ref[...]).astype(jnp.bfloat16).astype(jnp.float32)
-        values[place, :] = project(normal, value_ref[...]).astype(jnp.bfloat16).astype(jnp.float32)
-    mine = pl.ds(pl.multiple_of(own * rows, rows), rows)
-    update_ref[...] = updates[mine, :].reshape(update_ref.shape)
-    queries[...] = (
-        project(normals[mine, :], query_ref[...]).astype(jnp.bfloat16).astype(jnp.float32)
-    )
+        here = slice(place * rows, (place + 1) * rows)
+        keys[here, :] = project(normal, key_ref[...]).astype(jnp.bfloat16).astype(jnp.float32)
+        values[here, :] = project(normal, value_ref[...]).astype(jnp.bfloat16).astype(jnp.float32)
+        if place == 0:
+            update_ref[...] = update.reshape(update_ref.shape)
+            layer_ref[...] = middle.reshape(layer_ref.shape)
+            queries[...] = (
+                project(normal, query_ref[...]).astype(jnp.bfloat16).astype(jnp.float32)
+            )
     group = lanes // seqs
     head_of = lax.broadcasted_iota(jnp.int32, (seq_dev, lanes), 1) // HEAD_DIM
     size = group * seqs
@@ -262,7 +273,7 @@
                 at = (place * HEADS + head) * seq_dev
                 total = jnp.where(head_of == head, context[at : at + seq_dev], total)
             contexts[pl.ds(first + place, seq_dev, stride=col_dev), :] = total
-    layer = middles[mine, :].astype(jnp.float32) + project(
+    layer = layer_ref[...].reshape(rows, width).astype(jnp.float32) + project(
         contexts[...].astype(jnp.bfloat16), output_ref[...]
     )
     layer_ref[...] = layer.astype(jnp.bfloat16).reshape(layer_ref.shape)
@@ -279,60 +290,70 @@
     column_value,
     column_output,
 ):
-    seq_dev, col_dev, width = alignment.shape
+    seq_dev, col_dev, _ = alignment.shape
     inner = row_query.shape[1]
     seq, col = lax.axis_size("seq"), lax.axis_size("col")
     scale = float(HEAD_DIM * seq_dev * seq) ** (-0.5)
-    bf16 = jnp.bfloat16
+    bf16, f32 = jnp.bfloat16, jnp.float32
     vmem = pl.BlockSpec(memory_space=pltpu.VMEM)
-    sources = (alignment, row_key, row_value, row_query)
+    grant = pltpu.CompilerParams(vmem_limit_bytes=8 << 20)
+    fields = {0: alignment}
+    for place in range(seq - 1, 0, -1):
+        fields[place] = lax.ppermute(alignment, "seq", [(i, i ^ place) for i in range(seq)])
+    fields = [fields[place] for place in range(seq)]
+    sources = (alignment, row_key, row_value)
     blocks = pl.pallas_call(
         project_kernel,
-        out_shape=jax.ShapeDtypeStruct((seq, col // 2, 2, 3, col_dev, inner), bf16),
-        in_specs=[pl.BlockSpec(memory_space=pltpu.HBM)] * 4,
+        out_shape=jax.ShapeDtypeStruct((seq, col // 2, 2, 2, col_dev, inner), bf16),
+        in_specs=[pl.BlockSpec(memory_space=pltpu.HBM)] * 3,
         out_specs=vmem,
-        scratch_shapes=[pltpu.VMEM(alignment.shape, bf16)]
-        + [pltpu.VMEM(row_key.shape, bf16)] * 3
-        + [pltpu.SemaphoreType.DMA((4,))],
-        compiler_params=pltpu.CompilerParams(vmem_limit_bytes=8 << 20),
+        scratch_shapes=[pltpu.VMEM(source.shape, bf16) for source in sources]
+        + [pltpu.SemaphoreType.DMA((3,))],
+        compiler_params=grant,
         name="project",
-    )(*(pltpu.with_memory_space_constraint(x, pltpu.HBM) for x in sources))
-    mine = lax.all_to_all(
-        blocks.reshape(seq * col, 3, col_dev, inner), ("seq", "col"), 0, 0
-    )
+    )(*(pltpu.with_memory_space_constraint(source, pltpu.HBM) for source in sources))
+    mine = lax.all_to_all(blocks.reshape(seq * col, 2, col_dev, inner), ("seq", "col"), 0, 0)
     other = lax.ppermute(mine, "col", [(i, i ^ 1) for i in range(col)])
-    shape = (seq, col, 3, col_dev, inner)
-    tiles = seq_dev // HEADS * seq + width // inner * seq_dev
+    shape = (seq, col, 2, col_dev, inner)
+    mine, other = mine.reshape(shape), other.reshape(shape)
+    halves = seq_dev // HEADS
+    queries, logits = pl.pallas_call(
+        query_kernel,
+        out_shape=(
+            jax.ShapeDtypeStruct((halves, seq, col_dev, inner), bf16),
+            jax.ShapeDtypeStruct((col_dev, col * col_dev), f32),
+        ),
+        in_specs=[vmem] * (seq + 2),
+        out_specs=(vmem, vmem),
+        compiler_params=grant,
+        name="query",
+    )(*fields, row_query, mine)
     parts = pl.pallas_call(
-        lambda *refs: attend_kernel(scale, *refs),
-        out_shape=jax.ShapeDtypeStruct((seq, tiles, col_dev, inner), bf16),
-        in_specs=[vmem] * 3,
+        functools.partial(attend_kernel, scale),
+        out_shape=jax.ShapeDtypeStruct((seq, halves * seq, col_dev, inner), bf16),
+        in_specs=[vmem] * 4,
         out_specs=vmem,
-        compiler_params=pltpu.CompilerParams(vmem_limit_bytes=8 << 20),
+        compiler_params=grant,
         name="attend",
-    )(mine.reshape(shape), other.reshape(shape), alignment)
+    )(mine, other, queries, logits)
     parts = lax.all_to_all(parts, "seq", 0, 0)
     total = seq * seq_dev * col_dev
     local = seq_dev * col_dev
     like = jax.ShapeDtypeStruct(alignment.shape, bf16)
-    f32 = jnp.float32
     return pl.pallas_call(
         finish_kernel,
         out_shape=(like, like),
-        in_specs=[vmem] * 6,
+        in_specs=[vmem] * (seq + 6),
         out_specs=(vmem, vmem),
         scratch_shapes=[
-            pltpu.VMEM((total, width), bf16),
-            pltpu.VMEM((total, width), bf16),
-            pltpu.VMEM((total, width), bf16),
             pltpu.VMEM((local, inner), f32),
             pltpu.VMEM((total, inner), f32),
             pltpu.VMEM((total, inner), f32),
             pltpu.VMEM((local, inner), f32),
         ],
-        compiler_params=pltpu.CompilerParams(vmem_limit_bytes=8 << 20),
+        compiler_params=grant,
         name="finish",
-    )(parts, row_output, column_query, column_key, column_value, column_output)
+    )(*fields, parts, row_output, column_query, column_key, column_value, column_output)
 
 
 def suits_by_head(seq, col, seq_dev, col_dev, width, inner):

time: 39.6 us -> 39.8 us (level)
  blocking collectives: 30.8 us -> 24.8 us
  starting transfers between devices: 0.12 us -> 4.23 us
  waiting for transfers between devices: 1.61 us -> 3.07 us
  Pallas kernels: 6.05 us -> 6.65 us
    ppermute x0 -> x3, starting transfers between devices: none -> 3.49 us  [by_head(): lax.ppermute(alignment, 'seq', [(i, i ^ place) for i in range(seq)])]
    all_to_all x1, blocking collectives: 20.6 us -> 17.1 us  [by_head(): lax.all_to_all(blocks.reshape(seq * col, 2, col_dev, inner), ('seq', 'col...]
    ppermute x0 -> x3, waiting for transfers between devices: none -> 3.06 us  [by_head(): lax.ppermute(alignment, 'seq', [(i, i ^ place) for i in range(seq)])]
    all_to_all x1, blocking collectives: 10.2 us -> 7.69 us  [by_head(): parts = lax.all_to_all(parts, 'seq', 0, 0)]
    ppermute x1, waiting for transfers between devices: 1.61 us -> 0.01 us  [by_head(): other = lax.ppermute(mine, 'col', [(i, i ^ 1) for i in range(col)])]
    pallas_call x2 -> x3, Pallas kernels: 4.07 us -> 4.97 us  [the longest x1 3.36 us: by_head(): pl.pallas_call(finish_kernel, out_shape=(like, like), in_specs=[vmem] * (...]
    ppermute x1, starting transfers between devices: 0.12 us -> 0.74 us  [by_head(): other = lax.ppermute(mine, 'col', [(i, i ^ 1) for i in range(col)])]
  transfers between devices with their start and end apart: 1 -> 4, of which waited for: 1 -> 3; matrix products, arithmetic and copies ran while one was open for 0% -> 0% of each run, Pallas kernels for 0% -> 2%
where the time goes in v4:
time: 39.8 us; the launch traced here: 39.5 us
  blocking collectives  24.8 us (62%)
  Pallas kernels  6.65 us (17%)
  starting transfers between devices  4.23 us (11%)
  waiting for transfers between devices  3.07 us (8%)
  between operations  0.72 us (2%)
    all_to_all x1, blocking collectives, by_head(): lax.all_to_all(blocks.reshape(seq * col, 2, col_dev, inner), ('seq', 'col...  17.1 us
    all_to_all x1, blocking collectives, by_head(): parts = lax.all_to_all(parts, 'seq', 0, 0)  7.69 us
    ppermute x3, starting transfers between devices, by_head(): lax.ppermute(alignment, 'seq', [(i, i ^ place) for i in range(seq)])  3.49 us
    pallas_call x1, Pallas kernels, by_head(): pl.pallas_call(finish_kernel, out_shape=(like, like), in_specs=[vmem] * (...  3.36 us
    ppermute x3, waiting for transfers between devices, by_head(): lax.ppermute(alignment, 'seq', [(i, i ^ place) for i in range(seq)])  3.06 us
    pallas_call x1, Pallas kernels, by_head(): pl.pallas_call(project_kernel, out_shape=jax.ShapeDtypeStruct((seq, col /...  1.67 us
    pallas_call x1, Pallas kernels, by_head(): pl.pallas_call(query_kernel, out_shape=(jax.ShapeDtypeStruct((halves, seq...  0.92 us
  transfers between devices with their start and end apart: 4, of which 3 were waited for; matrix products, arithmetic and copies ran while one was open for 0% of the time, Pallas kernels for 2%

profile of v4, /device:TPU:0, one launch (start us, length us, event | category | flops | bytes accessed | tf_op | source)
XLA Modules:
  0.0 39.5 jit_solution(4441391759825238927)
XLA Ops:
  0.6 1.7 %project.1 = bf16[4,4,2,2,16,128]{5,4,3,2,1,0:T(8,128)(2,1)S(1)} custom-call(bf16[8,16,256]{2,1,0:T(8,128)(2,1)} %refs_0_.5, bf16[256,128]{1,0:T(8,128)(2,1)} %refs_1_.1, bf16[256,128]{1,0:T(8,128)(2,1)} %refs_2_.1), custom_call_target="tpu_custom_call" | custom-call | tf_op jit(solution)/shard_map/project/pallas_call | solution.py:305
  2.3 0.0 copy-start
  2.3 0.0 copy-start.1
  2.3 17.1 %all_to_all.10 = bf16[32,2,16,128]{3,2,1,0:T(8,128)(2,1)S(1)} all-to-all(bf16[32,2,16,128]{3,2,1,0:T(8,128)(2,1)S(1)} %bitcast.5), channel_id=1, replica_groups=mesh['seq'=4,'col'=8] {'seq','col'}, dimensions={0} | all-to-all | bytes 524288 | tf_op jit(solution)/shard_map/all_to_all | solution.py:315
  19.5 0.7 %collective-permute-start.3 = (bf16[32,2,16,128]{3,2,1,0:T(8,128)(2,1)S(1)}, bf16[32,2,16,128]{3,2,1,0:T(8,128)(2,1)S(1)}, u32[]{:S(2)}, u32[]{:S(2)}) collective-permute-start(bf16[32,2,16,128]{3,2,1,0:T(8,128)(2,1)S(1)} %all_to_all.10), channel_id=1, source_target_pairs={{0,1},{1,0},{2,3},{3,2},{4,5},{5,4},{6,7},{7,6},{8,9},{9,8},{10,11... | collective-permute-start | bytes 786440 | tf_op jit(solution)/shard_map/ppermute | solution.py:316
  20.2 0.0 copy-done
  20.2 0.8 %collective-permute-start.2 = (bf16[8,16,256]{2,1,0:T(8,128)(2,1)S(1)}, bf16[8,16,256]{2,1,0:T(8,128)(2,1)S(1)}, u32[]{:S(2)}, u32[]{:S(2)}) collective-permute-start(bf16[8,16,256]{2,1,0:T(8,128)(2,1)S(1)} %copy-done), channel_id=1, source_target_pairs={{0,24},{8,16},{16,8},{24,0},{1,25},{9,17},{17,9},{25,1},{2,26},{10... | collective-permute-start | bytes 196616 | tf_op jit(solution)/shard_map/ppermute | solution.py:302
  21.0 1.5 %collective-permute-start.1 = (bf16[8,16,256]{2,1,0:T(8,128)(2,1)S(1)}, bf16[8,16,256]{2,1,0:T(8,128)(2,1)S(1)}, u32[]{:S(2)}, u32[]{:S(2)}) collective-permute-start(bf16[8,16,256]{2,1,0:T(8,128)(2,1)S(1)} %copy-done), channel_id=1, source_target_pairs={{0,16},{8,24},{16,0},{24,8},{1,17},{9,25},{17,1},{25,9},{2,18},{10... | collective-permute-start | bytes 196616 | tf_op jit(solution)/shard_map/ppermute | solution.py:302
  22.5 1.2 %collective-permute-start = (bf16[8,16,256]{2,1,0:T(8,128)(2,1)S(1)}, bf16[8,16,256]{2,1,0:T(8,128)(2,1)S(1)}, u32[]{:S(2)}, u32[]{:S(2)}) collective-permute-start(bf16[8,16,256]{2,1,0:T(8,128)(2,1)S(1)} %copy-done), channel_id=1, source_target_pairs={{0,8},{8,0},{16,24},{24,16},{1,9},{9,1},{17,25},{25,17},{2,10},{10... | collective-permute-start | bytes 196616 | tf_op jit(solution)/shard_map/ppermute | solution.py:302
  23.7 2.3 %collective-permute-done.2.refs_3_ = bf16[8,16,256]{2,1,0:T(8,128)(2,1)S(1)} collective-permute-done((bf16[8,16,256]{2,1,0:T(8,128)(2,1)S(1)}, bf16[8,16,256]{2,1,0:T(8,128)(2,1)S(1)}, u32[]{:S(2)}, u32[]{:S(2)}) %collective-permute-start.2) | collective-permute-done | bytes 65568 | tf_op jit(solution)/shard_map/ppermute | solution.py:302
  26.0 0.2 collective-permute-done.1.refs_2_
  26.2 0.5 %collective-permute-done.refs_1_ = bf16[8,16,256]{2,1,0:T(8,128)(2,1)S(1)} collective-permute-done((bf16[8,16,256]{2,1,0:T(8,128)(2,1)S(1)}, bf16[8,16,256]{2,1,0:T(8,128)(2,1)S(1)}, u32[]{:S(2)}, u32[]{:S(2)}) %collective-permute-start) | collective-permute-done | bytes 65568 | tf_op jit(solution)/shard_map/ppermute | solution.py:302
  26.8 0.0 copy-done.1
  26.8 0.9 %query.1 = (bf16[2,4,16,128]{3,2,1,0:T(8,128)(2,1)S(1)}, f32[16,128]{1,0:T(8,128)S(1)}) custom-call(bf16[8,16,256]{2,1,0:T(8,128)(2,1)S(1)} %copy-done, bf16[8,16,256]{2,1,0:T(8,128)(2,1)S(1)} %collective-permute-done.refs_1_, bf16[8,16,256]{2,1,0:T(8,128)(2,1)S(1)} %collective-permute-done.1.refs_2_, ...), custom_call_target="tpu_custom_call" | custom-call | tf_op jit(solution)/shard_map/query/pallas_call | solution.py:320
  27.7 0.0 collective-permute-done.3
  27.7 0.0 copy-start.6
  27.7 0.7 %attend.1 = bf16[4,8,16,128]{3,2,1,0:T(8,128)(2,1)S(1)} custom-call(bf16[4,8,2,16,128]{4,3,2,1,0:T(8,128)(2,1)S(1)} %bitcast.4, bf16[4,8,2,16,128]{4,3,2,1,0:T(8,128)(2,1)S(1)} %bitcast.6, bf16[2,4,16,128]{3,2,1,0:T(8,128)(2,1)S(1)} %get-tuple-element.4.query_ref, f32[16,128]{1,0:T(8,128)S(1)} %get-tuple-element.5.logits_ref), custom_call_target="tpu_custom_call" | custom-call | tf_op jit(solution)/shard_map/attend/pallas_call | solution.py:331
  28.4 0.0 copy-start.2
  28.4 0.0 copy-start.3
  28.4 0.0 copy-start.4
  28.4 0.0 copy-start.5
  28.4 7.7 %all_to_all.11.refs_4_ = bf16[4,8,16,128]{3,2,1,0:T(8,128)(2,1)S(1)} all-to-all(bf16[4,8,16,128]{3,2,1,0:T(8,128)(2,1)S(1)} %attend.1), channel_id=1, replica_groups=mesh['seq'=4,'col'=8] {'seq'}, dimensions={0} | all-to-all | bytes 262144 | tf_op jit(solution)/shard_map/all_to_all | solution.py:339
  36.1 0.0 copy-done.6
  36.1 0.0 copy-done.2
  36.1 0.0 copy-done.3
  36.1 0.0 copy-done.4
  36.2 0.0 copy-done.5
  36.2 3.4 %finish.1 = (bf16[8,16,256]{2,1,0:T(8,128)(2,1)}, bf16[8,16,256]{2,1,0:T(8,128)(2,1)}) custom-call(bf16[8,16,256]{2,1,0:T(8,128)(2,1)S(1)} %copy-done, bf16[8,16,256]{2,1,0:T(8,128)(2,1)S(1)} %collective-permute-done.refs_1_, bf16[8,16,256]{2,1,0:T(8,128)(2,1)S(1)} %collective-permute-done.1.refs_2_, bf16[8,16,256]{2,1,0:T(8,128)(2,1)S(1)} %collective-permute-done.2.refs_3_, ...), custom_call_target="tpu_custom_call" | custom-call | tf_op jit(solution)/shard_map/finish/pallas_call | solution.py:343
Async XLA Ops:
  2.3 17.9 %copy-start = (bf16[8,16,256]{2,1,0:T(8,128)(2,1)S(1)}, bf16[8,16,256]{2,1,0:T(8,128)(2,1)}, u32[]{:S(2)}) copy-start(bf16[8,16,256]{2,1,0:T(8,128)(2,1)} %refs_0_.5) | copy-start | bytes 196612
  2.3 24.5 %copy-start.1 = (bf16[256,128]{1,0:T(8,128)(2,1)S(1)}, bf16[256,128]{1,0:T(8,128)(2,1)}, u32[]{:S(2)}) copy-start(bf16[256,128]{1,0:T(8,128)(2,1)} %refs_4_.1) | copy-start | bytes 196612
  19.5 8.2 %collective-permute-start.3 = (bf16[32,2,16,128]{3,2,1,0:T(8,128)(2,1)S(1)}, bf16[32,2,16,128]{3,2,1,0:T(8,128)(2,1)S(1)}, u32[]{:S(2)}, u32[]{:S(2)}) collective-permute-start(bf16[32,2,16,128]{3,2,1,0:T(8,128)(2,1)S(1)} %all_to_all.10), channel_id=1, source_target_pairs={{0,1},{1,0},{2,3},{3,2},{4,5},{5,4},{6,7},{7,6},{8,9},{9,8},{10,11... | collective-permute-start | bytes 786440 | tf_op jit(solution)/shard_map/ppermute | solution.py:316
  20.2 5.8 %collective-permute-start.2 = (bf16[8,16,256]{2,1,0:T(8,128)(2,1)S(1)}, bf16[8,16,256]{2,1,0:T(8,128)(2,1)S(1)}, u32[]{:S(2)}, u32[]{:S(2)}) collective-permute-start(bf16[8,16,256]{2,1,0:T(8,128)(2,1)S(1)} %copy-done), channel_id=1, source_target_pairs={{0,24},{8,16},{16,8},{24,0},{1,25},{9,17},{17,9},{25,1},{2,26},{10... | collective-permute-start | bytes 196616 | tf_op jit(solution)/shard_map/ppermute | solution.py:302
  21.0 5.2 %collective-permute-start.1 = (bf16[8,16,256]{2,1,0:T(8,128)(2,1)S(1)}, bf16[8,16,256]{2,1,0:T(8,128)(2,1)S(1)}, u32[]{:S(2)}, u32[]{:S(2)}) collective-permute-start(bf16[8,16,256]{2,1,0:T(8,128)(2,1)S(1)} %copy-done), channel_id=1, source_target_pairs={{0,16},{8,24},{16,0},{24,8},{1,17},{9,25},{17,1},{25,9},{2,18},{10... | collective-permute-start | bytes 196616 | tf_op jit(solution)/shard_map/ppermute | solution.py:302
  22.5 4.3 %collective-permute-start = (bf16[8,16,256]{2,1,0:T(8,128)(2,1)S(1)}, bf16[8,16,256]{2,1,0:T(8,128)(2,1)S(1)}, u32[]{:S(2)}, u32[]{:S(2)}) collective-permute-start(bf16[8,16,256]{2,1,0:T(8,128)(2,1)S(1)} %copy-done), channel_id=1, source_target_pairs={{0,8},{8,0},{16,24},{24,16},{1,9},{9,1},{17,25},{25,17},{2,10},{10... | collective-permute-start | bytes 196616 | tf_op jit(solution)/shard_map/ppermute | solution.py:302
  27.7 8.4 %copy-start.6 = (bf16[128,256]{1,0:T(8,128)(2,1)S(1)}, bf16[128,256]{1,0:T(8,128)(2,1)}, u32[]{:S(2)}) copy-start(bf16[128,256]{1,0:T(8,128)(2,1)} %refs_9_.1) | copy-start | bytes 196612
  28.4 7.7 %copy-start.2 = (bf16[128,256]{1,0:T(8,128)(2,1)S(1)}, bf16[128,256]{1,0:T(8,128)(2,1)}, u32[]{:S(2)}) copy-start(bf16[128,256]{1,0:T(8,128)(2,1)} %refs_5_.1) | copy-start | bytes 196612
  28.4 7.7 %copy-start.3 = (bf16[256,128]{1,0:T(8,128)(2,1)S(1)}, bf16[256,128]{1,0:T(8,128)(2,1)}, u32[]{:S(2)}) copy-start(bf16[256,128]{1,0:T(8,128)(2,1)} %refs_6_.1) | copy-start | bytes 196612
  28.4 7.7 %copy-start.4 = (bf16[256,128]{1,0:T(8,128)(2,1)S(1)}, bf16[256,128]{1,0:T(8,128)(2,1)}, u32[]{:S(2)}) copy-start(bf16[256,128]{1,0:T(8,128)(2,1)} %refs_7_.1) | copy-start | bytes 196612
  28.4 7.7 %copy-start.5 = (bf16[256,128]{1,0:T(8,128)(2,1)S(1)}, bf16[256,128]{1,0:T(8,128)(2,1)}, u32[]{:S(2)}) copy-start(bf16[256,128]{1,0:T(8,128)(2,1)} %refs_8_.1) | copy-start | bytes 196612

commit v5 on v4

--- a/solution.py
+++ b/solution.py
@@ -214,14 +214,15 @@
 
 
 def finish_kernel(*refs):
-    fields, refs = refs[:-12], refs[-12:]
+    fields, refs = refs[:-13], refs[-13:]
     (parts_ref, row_output_ref, query_ref, key_ref, value_ref, output_ref) = refs[:6]
-    update_ref, layer_ref, queries, keys, values, contexts = refs[6:]
+    update_ref, layer_ref, middles, queries, keys, values, contexts = refs[6:]
     own = lax.axis_index("seq")
     seq, _, col_dev, lanes = parts_ref.shape
     seq_dev, _, width = update_ref.shape
     rows = seq_dev * col_dev
     seqs = seq * seq_dev
+    pair = jnp.concatenate([key_ref[...], value_ref[...]], axis=1)
     for place, field_ref in enumerate(fields):
         source = own ^ place
         context = []
@@ -231,19 +232,17 @@
             ]
             context += swap_groups(heads, HEAD_DIM)
         context = jnp.concatenate(context, axis=0).astype(jnp.bfloat16)
-        update = project(context, row_output_ref[...]).astype(jnp.bfloat16)
-        field = field_ref[...].reshape(rows, width)
-        middle = (field.astype(jnp.float32) + update.astype(jnp.float32)).astype(jnp.bfloat16)
-        normal = norm_rows(middle.astype(jnp.float32))
+        update = project(context, row_output_ref[...])
+        middle = field_ref[...].reshape(rows, width).astype(jnp.float32) + update
+        normal = norm_rows(middle)
         here = slice(place * rows, (place + 1) * rows)
-        keys[here, :] = project(normal, key_ref[...]).astype(jnp.bfloat16).astype(jnp.float32)
-        values[here, :] = project(normal, value_ref[...]).astype(jnp.bfloat16).astype(jnp.float32)
+        both = project(normal, pair)
+        keys[here, :] = both[:, :lanes]
+        values[here, :] = both[:, lanes:]
         if place == 0:
-            update_ref[...] = update.reshape(update_ref.shape)
-            layer_ref[...] = middle.reshape(layer_ref.shape)
-            queries[...] = (
-                project(normal, query_ref[...]).astype(jnp.bfloat16).astype(jnp.float32)
-            )
+            update_ref[...] = update.astype(jnp.bfloat16).reshape(update_ref.shape)
+            middles[...] = middle
+            queries[...] = project(normal, query_ref[...]) * float(HEAD_DIM) ** (-0.5)
     group = lanes // seqs
     head_of = lax.broadcasted_iota(jnp.int32, (seq_dev, lanes), 1) // HEAD_DIM
     size = group * seqs
@@ -251,6 +250,7 @@
         HEADS * seq_dev
     )
     same = row_column == lax.broadcasted_iota(jnp.int32, row_column.shape, 1) // seqs
+    ones = jnp.ones((size, lanes), jnp.bfloat16)
     for first in range(0, col_dev, group):
         query, key, value = [], [], []
         for column in range(first, first + group):
@@ -261,21 +261,18 @@
         query, key, value = (
             jnp.concatenate(part, axis=0).astype(jnp.bfloat16) for part in (query, key, value)
         )
-        scores = jnp.where(
-            same, contract_last(query, key) * float(HEAD_DIM) ** (-0.5), -jnp.inf
-        )
+        scores = jnp.where(same, contract_last(query, key), -jnp.inf)
         weights = jnp.exp(scores - jnp.max(scores, axis=-1, keepdims=True))
-        probs = (weights / jnp.sum(weights, axis=-1, keepdims=True)).astype(jnp.bfloat16)
-        context = project(probs, value)
+        both = project(weights.astype(jnp.bfloat16), jnp.concatenate([value, ones], axis=1))
         for place in range(group):
-            total = jnp.zeros((seq_dev, lanes), jnp.float32)
+            above = jnp.zeros((seq_dev, lanes), jnp.float32)
+            below = jnp.ones((seq_dev, lanes), jnp.float32)
             for head in range(HEADS):
                 at = (place * HEADS + head) * seq_dev
-                total = jnp.where(head_of == head, context[at : at + seq_dev], total)
-            contexts[pl.ds(first + place, seq_dev, stride=col_dev), :] = total
-    layer = layer_ref[...].reshape(rows, width).astype(jnp.float32) + project(
-        contexts[...].astype(jnp.bfloat16), output_ref[...]
-    )
+                above = jnp.where(head_of == head, both[at : at + seq_dev, :lanes], above)
+                below = jnp.where(head_of == head, both[at : at + seq_dev, lanes:], below)
+            contexts[pl.ds(first + place, seq_dev, stride=col_dev), :] = above / below
+    layer = middles[...] + project(contexts[...].astype(jnp.bfloat16), output_ref[...])
     layer_ref[...] = layer.astype(jnp.bfloat16).reshape(layer_ref.shape)
 
 
@@ -290,7 +287,7 @@
     column_value,
     column_output,
 ):
-    seq_dev, col_dev, _ = alignment.shape
+    seq_dev, col_dev, width = alignment.shape
     inner = row_query.shape[1]
     seq, col = lax.axis_size("seq"), lax.axis_size("col")
     scale = float(HEAD_DIM * seq_dev * seq) ** (-0.5)
@@ -346,6 +343,7 @@
         in_specs=[vmem] * (seq + 6),
         out_specs=(vmem, vmem),
         scratch_shapes=[
+            pltpu.VMEM((local, width), f32),
             pltpu.VMEM((local, inner), f32),
             pltpu.VMEM((total, inner), f32),
             pltpu.VMEM((total, inner), f32),

time: 39.8 us -> 38.8 us (0.975)
  Pallas kernels: 6.65 us -> 5.67 us
    pallas_call x1, Pallas kernels: 3.36 us -> 2.39 us  [by_head(): pl.pallas_call(finish_kernel, out_shape=(like, like), in_specs=[vmem] * (...]
where the time goes in v5:
time: 38.8 us; the launch traced here: 38.5 us
  blocking collectives  24.8 us (64%)
  Pallas kernels  5.67 us (15%)
  starting transfers between devices  4.23 us (11%)
  waiting for transfers between devices  3.07 us (8%)
  between operations  0.72 us (2%)
    all_to_all x1, blocking collectives, by_head(): lax.all_to_all(blocks.reshape(seq * col, 2, col_dev, inner), ('seq', 'col...  17.1 us
    all_to_all x1, blocking collectives, by_head(): parts = lax.all_to_all(parts, 'seq', 0, 0)  7.69 us
    ppermute x3, starting transfers between devices, by_head(): lax.ppermute(alignment, 'seq', [(i, i ^ place) for i in range(seq)])  3.49 us
    ppermute x3, waiting for transfers between devices, by_head(): lax.ppermute(alignment, 'seq', [(i, i ^ place) for i in range(seq)])  3.06 us
    pallas_call x1, Pallas kernels, by_head(): pl.pallas_call(finish_kernel, out_shape=(like, like), in_specs=[vmem] * (...  2.39 us
    pallas_call x1, Pallas kernels, by_head(): pl.pallas_call(project_kernel, out_shape=jax.ShapeDtypeStruct((seq, col /...  1.67 us
    pallas_call x1, Pallas kernels, by_head(): pl.pallas_call(query_kernel, out_shape=(jax.ShapeDtypeStruct((halves, seq...  0.92 us
  transfers between devices with their start and end apart: 4, of which 3 were waited for; matrix products, arithmetic and copies ran while one was open for 0% of the time, Pallas kernels for 2%

profile of v5, /device:TPU:0, one launch (start us, length us, event | category | flops | bytes accessed | tf_op | source)
XLA Modules:
  0.0 38.5 jit_solution(16304039392827619253)
XLA Ops:
  0.6 1.7 %project.1 = bf16[4,4,2,2,16,128]{5,4,3,2,1,0:T(8,128)(2,1)S(1)} custom-call(bf16[8,16,256]{2,1,0:T(8,128)(2,1)} %refs_0_.5, bf16[256,128]{1,0:T(8,128)(2,1)} %refs_1_.1, bf16[256,128]{1,0:T(8,128)(2,1)} %refs_2_.1), custom_call_target="tpu_custom_call" | custom-call | tf_op jit(solution)/shard_map/project/pallas_call | solution.py:302
  2.3 0.0 copy-start
  2.3 0.0 copy-start.1
  2.3 17.1 %all_to_all.10 = bf16[32,2,16,128]{3,2,1,0:T(8,128)(2,1)S(1)} all-to-all(bf16[32,2,16,128]{3,2,1,0:T(8,128)(2,1)S(1)} %bitcast.5), channel_id=1, replica_groups=mesh['seq'=4,'col'=8] {'seq','col'}, dimensions={0} | all-to-all | bytes 524288 | tf_op jit(solution)/shard_map/all_to_all | solution.py:312
  19.5 0.7 %collective-permute-start.3 = (bf16[32,2,16,128]{3,2,1,0:T(8,128)(2,1)S(1)}, bf16[32,2,16,128]{3,2,1,0:T(8,128)(2,1)S(1)}, u32[]{:S(2)}, u32[]{:S(2)}) collective-permute-start(bf16[32,2,16,128]{3,2,1,0:T(8,128)(2,1)S(1)} %all_to_all.10), channel_id=1, source_target_pairs={{0,1},{1,0},{2,3},{3,2},{4,5},{5,4},{6,7},{7,6},{8,9},{9,8},{10,11... | collective-permute-start | bytes 786440 | tf_op jit(solution)/shard_map/ppermute | solution.py:313
  20.2 0.0 copy-done
  20.2 0.8 %collective-permute-start.2 = (bf16[8,16,256]{2,1,0:T(8,128)(2,1)S(1)}, bf16[8,16,256]{2,1,0:T(8,128)(2,1)S(1)}, u32[]{:S(2)}, u32[]{:S(2)}) collective-permute-start(bf16[8,16,256]{2,1,0:T(8,128)(2,1)S(1)} %copy-done), channel_id=1, source_target_pairs={{0,24},{8,16},{16,8},{24,0},{1,25},{9,17},{17,9},{25,1},{2,26},{10... | collective-permute-start | bytes 196616 | tf_op jit(solution)/shard_map/ppermute | solution.py:299
  21.0 1.5 %collective-permute-start.1 = (bf16[8,16,256]{2,1,0:T(8,128)(2,1)S(1)}, bf16[8,16,256]{2,1,0:T(8,128)(2,1)S(1)}, u32[]{:S(2)}, u32[]{:S(2)}) collective-permute-start(bf16[8,16,256]{2,1,0:T(8,128)(2,1)S(1)} %copy-done), channel_id=1, source_target_pairs={{0,16},{8,24},{16,0},{24,8},{1,17},{9,25},{17,1},{25,9},{2,18},{10... | collective-permute-start | bytes 196616 | tf_op jit(solution)/shard_map/ppermute | solution.py:299
  22.5 1.2 %collective-permute-start = (bf16[8,16,256]{2,1,0:T(8,128)(2,1)S(1)}, bf16[8,16,256]{2,1,0:T(8,128)(2,1)S(1)}, u32[]{:S(2)}, u32[]{:S(2)}) collective-permute-start(bf16[8,16,256]{2,1,0:T(8,128)(2,1)S(1)} %copy-done), channel_id=1, source_target_pairs={{0,8},{8,0},{16,24},{24,16},{1,9},{9,1},{17,25},{25,17},{2,10},{10... | collective-permute-start | bytes 196616 | tf_op jit(solution)/shard_map/ppermute | solution.py:299
  23.7 2.3 %collective-permute-done.2.refs_3_ = bf16[8,16,256]{2,1,0:T(8,128)(2,1)S(1)} collective-permute-done((bf16[8,16,256]{2,1,0:T(8,128)(2,1)S(1)}, bf16[8,16,256]{2,1,0:T(8,128)(2,1)S(1)}, u32[]{:S(2)}, u32[]{:S(2)}) %collective-permute-start.2) | collective-permute-done | bytes 65568 | tf_op jit(solution)/shard_map/ppermute | solution.py:299
  26.0 0.2 collective-permute-done.1.refs_2_
  26.2 0.5 %collective-permute-done.refs_1_ = bf16[8,16,256]{2,1,0:T(8,128)(2,1)S(1)} collective-permute-done((bf16[8,16,256]{2,1,0:T(8,128)(2,1)S(1)}, bf16[8,16,256]{2,1,0:T(8,128)(2,1)S(1)}, u32[]{:S(2)}, u32[]{:S(2)}) %collective-permute-start) | collective-permute-done | bytes 65568 | tf_op jit(solution)/shard_map/ppermute | solution.py:299
  26.8 0.0 copy-done.1
  26.8 0.9 %query.1 = (bf16[2,4,16,128]{3,2,1,0:T(8,128)(2,1)S(1)}, f32[16,128]{1,0:T(8,128)S(1)}) custom-call(bf16[8,16,256]{2,1,0:T(8,128)(2,1)S(1)} %copy-done, bf16[8,16,256]{2,1,0:T(8,128)(2,1)S(1)} %collective-permute-done.refs_1_, bf16[8,16,256]{2,1,0:T(8,128)(2,1)S(1)} %collective-permute-done.1.refs_2_, ...), custom_call_target="tpu_custom_call" | custom-call | tf_op jit(solution)/shard_map/query/pallas_call | solution.py:317
  27.7 0.0 collective-permute-done.3
  27.7 0.0 copy-start.6
  27.7 0.7 %attend.1 = bf16[4,8,16,128]{3,2,1,0:T(8,128)(2,1)S(1)} custom-call(bf16[4,8,2,16,128]{4,3,2,1,0:T(8,128)(2,1)S(1)} %bitcast.4, bf16[4,8,2,16,128]{4,3,2,1,0:T(8,128)(2,1)S(1)} %bitcast.6, bf16[2,4,16,128]{3,2,1,0:T(8,128)(2,1)S(1)} %get-tuple-element.4.query_ref, f32[16,128]{1,0:T(8,128)S(1)} %get-tuple-element.5.logits_ref), custom_call_target="tpu_custom_call" | custom-call | tf_op jit(solution)/shard_map/attend/pallas_call | solution.py:328
  28.4 0.0 copy-start.2
  28.4 0.0 copy-start.3
  28.4 0.0 copy-start.4
  28.4 0.0 copy-start.5
  28.4 7.7 %all_to_all.11.refs_4_ = bf16[4,8,16,128]{3,2,1,0:T(8,128)(2,1)S(1)} all-to-all(bf16[4,8,16,128]{3,2,1,0:T(8,128)(2,1)S(1)} %attend.1), channel_id=1, replica_groups=mesh['seq'=4,'col'=8] {'seq'}, dimensions={0} | all-to-all | bytes 262144 | tf_op jit(solution)/shard_map/all_to_all | solution.py:336
  36.1 0.0 copy-done.6
  36.1 0.0 copy-done.2
  36.1 0.0 copy-done.3
  36.1 0.0 copy-done.4
  36.2 0.0 copy-done.5
  36.2 2.4 %finish.1 = (bf16[8,16,256]{2,1,0:T(8,128)(2,1)}, bf16[8,16,256]{2,1,0:T(8,128)(2,1)}) custom-call(bf16[8,16,256]{2,1,0:T(8,128)(2,1)S(1)} %copy-done, bf16[8,16,256]{2,1,0:T(8,128)(2,1)S(1)} %collective-permute-done.refs_1_, bf16[8,16,256]{2,1,0:T(8,128)(2,1)S(1)} %collective-permute-done.1.refs_2_, bf16[8,16,256]{2,1,0:T(8,128)(2,1)S(1)} %collective-permute-done.2.refs_3_, ...), custom_call_target="tpu_custom_call" | custom-call | tf_op jit(solution)/shard_map/finish/pallas_call | solution.py:340
Async XLA Ops:
  2.3 17.9 %copy-start = (bf16[8,16,256]{2,1,0:T(8,128)(2,1)S(1)}, bf16[8,16,256]{2,1,0:T(8,128)(2,1)}, u32[]{:S(2)}) copy-start(bf16[8,16,256]{2,1,0:T(8,128)(2,1)} %refs_0_.5) | copy-start | bytes 196612
  2.3 24.5 %copy-start.1 = (bf16[256,128]{1,0:T(8,128)(2,1)S(1)}, bf16[256,128]{1,0:T(8,128)(2,1)}, u32[]{:S(2)}) copy-start(bf16[256,128]{1,0:T(8,128)(2,1)} %refs_4_.1) | copy-start | bytes 196612
  19.5 8.2 %collective-permute-start.3 = (bf16[32,2,16,128]{3,2,1,0:T(8,128)(2,1)S(1)}, bf16[32,2,16,128]{3,2,1,0:T(8,128)(2,1)S(1)}, u32[]{:S(2)}, u32[]{:S(2)}) collective-permute-start(bf16[32,2,16,128]{3,2,1,0:T(8,128)(2,1)S(1)} %all_to_all.10), channel_id=1, source_target_pairs={{0,1},{1,0},{2,3},{3,2},{4,5},{5,4},{6,7},{7,6},{8,9},{9,8},{10,11... | collective-permute-start | bytes 786440 | tf_op jit(solution)/shard_map/ppermute | solution.py:313
  20.2 5.8 %collective-permute-start.2 = (bf16[8,16,256]{2,1,0:T(8,128)(2,1)S(1)}, bf16[8,16,256]{2,1,0:T(8,128)(2,1)S(1)}, u32[]{:S(2)}, u32[]{:S(2)}) collective-permute-start(bf16[8,16,256]{2,1,0:T(8,128)(2,1)S(1)} %copy-done), channel_id=1, source_target_pairs={{0,24},{8,16},{16,8},{24,0},{1,25},{9,17},{17,9},{25,1},{2,26},{10... | collective-permute-start | bytes 196616 | tf_op jit(solution)/shard_map/ppermute | solution.py:299
  21.0 5.2 %collective-permute-start.1 = (bf16[8,16,256]{2,1,0:T(8,128)(2,1)S(1)}, bf16[8,16,256]{2,1,0:T(8,128)(2,1)S(1)}, u32[]{:S(2)}, u32[]{:S(2)}) collective-permute-start(bf16[8,16,256]{2,1,0:T(8,128)(2,1)S(1)} %copy-done), channel_id=1, source_target_pairs={{0,16},{8,24},{16,0},{24,8},{1,17},{9,25},{17,1},{25,9},{2,18},{10... | collective-permute-start | bytes 196616 | tf_op jit(solution)/shard_map/ppermute | solution.py:299
  22.5 4.3 %collective-permute-start = (bf16[8,16,256]{2,1,0:T(8,128)(2,1)S(1)}, bf16[8,16,256]{2,1,0:T(8,128)(2,1)S(1)}, u32[]{:S(2)}, u32[]{:S(2)}) collective-permute-start(bf16[8,16,256]{2,1,0:T(8,128)(2,1)S(1)} %copy-done), channel_id=1, source_target_pairs={{0,8},{8,0},{16,24},{24,16},{1,9},{9,1},{17,25},{25,17},{2,10},{10... | collective-permute-start | bytes 196616 | tf_op jit(solution)/shard_map/ppermute | solution.py:299
  27.7 8.4 %copy-start.6 = (bf16[128,256]{1,0:T(8,128)(2,1)S(1)}, bf16[128,256]{1,0:T(8,128)(2,1)}, u32[]{:S(2)}) copy-start(bf16[128,256]{1,0:T(8,128)(2,1)} %refs_9_.1) | copy-start | bytes 196612
  28.4 7.7 %copy-start.2 = (bf16[128,256]{1,0:T(8,128)(2,1)S(1)}, bf16[128,256]{1,0:T(8,128)(2,1)}, u32[]{:S(2)}) copy-start(bf16[128,256]{1,0:T(8,128)(2,1)} %refs_5_.1) | copy-start | bytes 196612
  28.4 7.7 %copy-start.3 = (bf16[256,128]{1,0:T(8,128)(2,1)S(1)}, bf16[256,128]{1,0:T(8,128)(2,1)}, u32[]{:S(2)}) copy-start(bf16[256,128]{1,0:T(8,128)(2,1)} %refs_6_.1) | copy-start | bytes 196612
  28.4 7.7 %copy-start.4 = (bf16[256,128]{1,0:T(8,128)(2,1)S(1)}, bf16[256,128]{1,0:T(8,128)(2,1)}, u32[]{:S(2)}) copy-start(bf16[256,128]{1,0:T(8,128)(2,1)} %refs_7_.1) | copy-start | bytes 196612
  28.4 7.7 %copy-start.5 = (bf16[256,128]{1,0:T(8,128)(2,1)S(1)}, bf16[256,128]{1,0:T(8,128)(2,1)}, u32[]{:S(2)}) copy-start(bf16[256,128]{1,0:T(8,128)(2,1)} %refs_8_.1) | copy-start | bytes 196612

commit v6 on v5

--- a/solution.py
+++ b/solution.py
@@ -129,21 +129,15 @@
     )
 
 
-def project_kernel(*refs):
-    sources, out_ref, held, sems = refs[:3], refs[3], refs[4:7], refs[7]
-    copies = [
-        pltpu.make_async_copy(source, ref, sems.at[place])
-        for place, (source, ref) in enumerate(zip(sources, held))
-    ]
-    for copy in copies:
-        copy.start()
-    field_ref, key_ref, value_ref = held
+def gate_kernel(out_ref):
+    out_ref[...] = jnp.zeros_like(out_ref)
+
+
+def project_kernel(field_ref, key_ref, value_ref, gate_ref, out_ref):
     seq_dev, col_dev, width = field_ref.shape
     heads, chips, cores = out_ref.shape[:3]
-    copies[0].wait()
     normed = norm_rows(field_ref[...].astype(jnp.float32).reshape(seq_dev * col_dev, width))
     for kind, weight_ref in enumerate((key_ref, value_ref)):
-        copies[kind + 1].wait()
         rows = project(normed, weight_ref[...])
         for core in range(cores):
             first = core * heads
@@ -294,21 +288,26 @@
     bf16, f32 = jnp.bfloat16, jnp.float32
     vmem = pl.BlockSpec(memory_space=pltpu.VMEM)
     grant = pltpu.CompilerParams(vmem_limit_bytes=8 << 20)
+    gate = pl.pallas_call(
+        gate_kernel,
+        out_shape=jax.ShapeDtypeStruct((8, inner), f32),
+        out_specs=vmem,
+        compiler_params=grant,
+        cost_estimate=pl.CostEstimate(flops=1 << 33, transcendentals=0, bytes_accessed=1 << 24),
+        name="gate",
+    )()
     fields = {0: alignment}
     for place in range(seq - 1, 0, -1):
         fields[place] = lax.ppermute(alignment, "seq", [(i, i ^ place) for i in range(seq)])
     fields = [fields[place] for place in range(seq)]
-    sources = (alignment, row_key, row_value)
     blocks = pl.pallas_call(
         project_kernel,
         out_shape=jax.ShapeDtypeStruct((seq, col // 2, 2, 2, col_dev, inner), bf16),
-        in_specs=[pl.BlockSpec(memory_space=pltpu.HBM)] * 3,
+        in_specs=[vmem] * 4,
         out_specs=vmem,
-        scratch_shapes=[pltpu.VMEM(source.shape, bf16) for source in sources]
-        + [pltpu.SemaphoreType.DMA((3,))],
         compiler_params=grant,
         name="project",
-    )(*(pltpu.with_memory_space_constraint(source, pltpu.HBM) for source in sources))
+    )(alignment, row_key, row_value, gate)
     mine = lax.all_to_all(blocks.reshape(seq * col, 2, col_dev, inner), ("seq", "col"), 0, 0)
     other = lax.ppermute(mine, "col", [(i, i ^ 1) for i in range(col)])
     shape = (seq, col, 2, col_dev, inner)

time: 38.8 us -> 38.5 us (level)
  Pallas kernels: 5.67 us -> 4.47 us
  local copies, waits for them, and re-layouts: 0.04 us -> 0.91 us
    pallas_call x1, Pallas kernels: 1.67 us -> 0.47 us  [by_head(): pl.pallas_call(project_kernel, out_shape=jax.ShapeDtypeStruct((seq, col /...]
    unnamed x14 -> x18, local copies, waits for them, and re-layouts: 0.04 us -> 0.91 us
where the time goes in v6:
time: 38.5 us; the launch traced here: 38.2 us
  blocking collectives  24.8 us (64%)
  Pallas kernels  4.47 us (12%)
  starting transfers between devices  4.23 us (11%)
  waiting for transfers between devices  3.07 us (8%)
  local copies, waits for them, and re-layouts  0.91 us (2%)
  between operations  0.74 us (2%)
    all_to_all x1, blocking collectives, by_head(): lax.all_to_all(blocks.reshape(seq * col, 2, col_dev, inner), ('seq', 'col...  17.1 us
    all_to_all x1, blocking collectives, by_head(): parts = lax.all_to_all(parts, 'seq', 0, 0)  7.69 us
    ppermute x3, starting transfers between devices, by_head(): lax.ppermute(alignment, 'seq', [(i, i ^ place) for i in range(seq)])  3.49 us
    ppermute x3, waiting for transfers between devices, by_head(): lax.ppermute(alignment, 'seq', [(i, i ^ place) for i in range(seq)])  3.06 us
    pallas_call x1, Pallas kernels, by_head(): pl.pallas_call(finish_kernel, out_shape=(like, like), in_specs=[vmem] * (...  2.39 us
    pallas_call x1, Pallas kernels, by_head(): pl.pallas_call(query_kernel, out_shape=(jax.ShapeDtypeStruct((halves, seq...  0.92 us
    unnamed x18, local copies, waits for them, and re-layouts  0.91 us
  transfers between devices with their start and end apart: 4, of which 3 were waited for; matrix products, arithmetic and copies ran while one was open for 0% of the time, Pallas kernels for 2%

profile of v6, /device:TPU:0, one launch (start us, length us, event | category | flops | bytes accessed | tf_op | source)
XLA Modules:
  0.0 38.2 jit_solution(10715143643308932660)
XLA Ops:
  0.6 0.0 copy-start
  0.6 0.0 copy-start.2
  0.6 0.0 copy-start.1
  0.7 0.8 %copy-done = bf16[8,16,256]{2,1,0:T(8,128)(2,1)S(1)} copy-done((bf16[8,16,256]{2,1,0:T(8,128)(2,1)S(1)}, bf16[8,16,256]{2,1,0:T(8,128)(2,1)}, u32[]{:S(2)}) %copy-start) | copy-done | bytes 65560
  1.5 0.0 copy-done.2
  1.5 0.0 copy-done.1
  1.5 0.5 %project.1 = bf16[4,4,2,2,16,128]{5,4,3,2,1,0:T(8,128)(2,1)S(1)} custom-call(bf16[8,16,256]{2,1,0:T(8,128)(2,1)S(1)} %copy-done, bf16[256,128]{1,0:T(8,128)(2,1)S(1)} %copy-done.1, bf16[256,128]{1,0:T(8,128)(2,1)S(1)} %copy-done.2, f32[8,128]{1,0:T(8,128)S(1)} %gate.1.gate_ref), custom_call_target="tpu_custom_call" | custom-call | tf_op jit(solution)/shard_map/project/pallas_call | solution.py:303
  2.0 0.0 copy-start.3
  2.0 17.1 %all_to_all.10 = bf16[32,2,16,128]{3,2,1,0:T(8,128)(2,1)S(1)} all-to-all(bf16[32,2,16,128]{3,2,1,0:T(8,128)(2,1)S(1)} %bitcast.5), channel_id=1, replica_groups=mesh['seq'=4,'col'=8] {'seq','col'}, dimensions={0} | all-to-all | bytes 524288 | tf_op jit(solution)/shard_map/all_to_all | solution.py:311
  19.2 0.7 %collective-permute-start.3 = (bf16[32,2,16,128]{3,2,1,0:T(8,128)(2,1)S(1)}, bf16[32,2,16,128]{3,2,1,0:T(8,128)(2,1)S(1)}, u32[]{:S(2)}, u32[]{:S(2)}) collective-permute-start(bf16[32,2,16,128]{3,2,1,0:T(8,128)(2,1)S(1)} %all_to_all.10), channel_id=1, source_target_pairs={{0,1},{1,0},{2,3},{3,2},{4,5},{5,4},{6,7},{7,6},{8,9},{9,8},{10,11... | collective-permute-start | bytes 786440 | tf_op jit(solution)/shard_map/ppermute | solution.py:312
  19.9 0.8 %collective-permute-start.2 = (bf16[8,16,256]{2,1,0:T(8,128)(2,1)S(1)}, bf16[8,16,256]{2,1,0:T(8,128)(2,1)S(1)}, u32[]{:S(2)}, u32[]{:S(2)}) collective-permute-start(bf16[8,16,256]{2,1,0:T(8,128)(2,1)S(1)} %copy-done), channel_id=1, source_target_pairs={{0,24},{8,16},{16,8},{24,0},{1,25},{9,17},{17,9},{25,1},{2,26},{10... | collective-permute-start | bytes 196616 | tf_op jit(solution)/shard_map/ppermute | solution.py:301
  20.7 1.5 %collective-permute-start.1 = (bf16[8,16,256]{2,1,0:T(8,128)(2,1)S(1)}, bf16[8,16,256]{2,1,0:T(8,128)(2,1)S(1)}, u32[]{:S(2)}, u32[]{:S(2)}) collective-permute-start(bf16[8,16,256]{2,1,0:T(8,128)(2,1)S(1)} %copy-done), channel_id=1, source_target_pairs={{0,16},{8,24},{16,0},{24,8},{1,17},{9,25},{17,1},{25,9},{2,18},{10... | collective-permute-start | bytes 196616 | tf_op jit(solution)/shard_map/ppermute | solution.py:301
  22.2 1.2 %collective-permute-start = (bf16[8,16,256]{2,1,0:T(8,128)(2,1)S(1)}, bf16[8,16,256]{2,1,0:T(8,128)(2,1)S(1)}, u32[]{:S(2)}, u32[]{:S(2)}) collective-permute-start(bf16[8,16,256]{2,1,0:T(8,128)(2,1)S(1)} %copy-done), channel_id=1, source_target_pairs={{0,8},{8,0},{16,24},{24,16},{1,9},{9,1},{17,25},{25,17},{2,10},{10... | collective-permute-start | bytes 196616 | tf_op jit(solution)/shard_map/ppermute | solution.py:301
  23.4 2.3 %collective-permute-done.2.refs_3_ = bf16[8,16,256]{2,1,0:T(8,128)(2,1)S(1)} collective-permute-done((bf16[8,16,256]{2,1,0:T(8,128)(2,1)S(1)}, bf16[8,16,256]{2,1,0:T(8,128)(2,1)S(1)}, u32[]{:S(2)}, u32[]{:S(2)}) %collective-permute-start.2) | collective-permute-done | bytes 65568 | tf_op jit(solution)/shard_map/ppermute | solution.py:301
  25.7 0.2 collective-permute-done.1.refs_2_
  25.9 0.5 %collective-permute-done.refs_1_ = bf16[8,16,256]{2,1,0:T(8,128)(2,1)S(1)} collective-permute-done((bf16[8,16,256]{2,1,0:T(8,128)(2,1)S(1)}, bf16[8,16,256]{2,1,0:T(8,128)(2,1)S(1)}, u32[]{:S(2)}, u32[]{:S(2)}) %collective-permute-start) | collective-permute-done | bytes 65568 | tf_op jit(solution)/shard_map/ppermute | solution.py:301
  26.5 0.0 copy-done.3
  26.5 0.9 %query.1 = (bf16[2,4,16,128]{3,2,1,0:T(8,128)(2,1)S(1)}, f32[16,128]{1,0:T(8,128)S(1)}) custom-call(bf16[8,16,256]{2,1,0:T(8,128)(2,1)S(1)} %copy-done, bf16[8,16,256]{2,1,0:T(8,128)(2,1)S(1)} %collective-permute-done.refs_1_, bf16[8,16,256]{2,1,0:T(8,128)(2,1)S(1)} %collective-permute-done.1.refs_2_, ...), custom_call_target="tpu_custom_call" | custom-call | tf_op jit(solution)/shard_map/query/pallas_call | solution.py:316
  27.4 0.0 collective-permute-done.3
  27.4 0.0 copy-start.8
  27.4 0.7 %attend.1 = bf16[4,8,16,128]{3,2,1,0:T(8,128)(2,1)S(1)} custom-call(bf16[4,8,2,16,128]{4,3,2,1,0:T(8,128)(2,1)S(1)} %bitcast.4, bf16[4,8,2,16,128]{4,3,2,1,0:T(8,128)(2,1)S(1)} %bitcast.6, bf16[2,4,16,128]{3,2,1,0:T(8,128)(2,1)S(1)} %get-tuple-element.4.query_ref, f32[16,128]{1,0:T(8,128)S(1)} %get-tuple-element.5.logits_ref), custom_call_target="tpu_custom_call" | custom-call | tf_op jit(solution)/shard_map/attend/pallas_call | solution.py:327
  28.1 0.0 copy-start.4
  28.1 0.0 copy-start.5
  28.1 0.0 copy-start.6
  28.1 0.0 copy-start.7
  28.1 7.7 %all_to_all.11.refs_4_ = bf16[4,8,16,128]{3,2,1,0:T(8,128)(2,1)S(1)} all-to-all(bf16[4,8,16,128]{3,2,1,0:T(8,128)(2,1)S(1)} %attend.1), channel_id=1, replica_groups=mesh['seq'=4,'col'=8] {'seq'}, dimensions={0} | all-to-all | bytes 262144 | tf_op jit(solution)/shard_map/all_to_all | solution.py:335
  35.8 0.0 copy-done.8
  35.8 0.0 copy-done.4
  35.8 0.0 copy-done.5
  35.8 0.0 copy-done.6
  35.8 0.0 copy-done.7
  35.8 2.4 %finish.1 = (bf16[8,16,256]{2,1,0:T(8,128)(2,1)}, bf16[8,16,256]{2,1,0:T(8,128)(2,1)}) custom-call(bf16[8,16,256]{2,1,0:T(8,128)(2,1)S(1)} %copy-done, bf16[8,16,256]{2,1,0:T(8,128)(2,1)S(1)} %collective-permute-done.refs_1_, bf16[8,16,256]{2,1,0:T(8,128)(2,1)S(1)} %collective-permute-done.1.refs_2_, bf16[8,16,256]{2,1,0:T(8,128)(2,1)S(1)} %collective-permute-done.2.refs_3_, ...), custom_call_target="tpu_custom_call" | custom-call | tf_op jit(solution)/shard_map/finish/pallas_call | solution.py:339
  (1 shorter events, 0.0 us)
Async XLA Ops:
  0.6 0.8 %copy-start = (bf16[8,16,256]{2,1,0:T(8,128)(2,1)S(1)}, bf16[8,16,256]{2,1,0:T(8,128)(2,1)}, u32[]{:S(2)}) copy-start(bf16[8,16,256]{2,1,0:T(8,128)(2,1)} %refs_0_.3) | copy-start | bytes 196612
  0.6 0.9 %copy-start.2 = (bf16[256,128]{1,0:T(8,128)(2,1)S(1)}, bf16[256,128]{1,0:T(8,128)(2,1)}, u32[]{:S(2)}) copy-start(bf16[256,128]{1,0:T(8,128)(2,1)} %value_ref.1) | copy-start | bytes 196612
  0.6 0.9 %copy-start.1 = (bf16[256,128]{1,0:T(8,128)(2,1)S(1)}, bf16[256,128]{1,0:T(8,128)(2,1)}, u32[]{:S(2)}) copy-start(bf16[256,128]{1,0:T(8,128)(2,1)} %key_ref.1) | copy-start | bytes 196612
  2.0 24.4 %copy-start.3 = (bf16[256,128]{1,0:T(8,128)(2,1)S(1)}, bf16[256,128]{1,0:T(8,128)(2,1)}, u32[]{:S(2)}) copy-start(bf16[256,128]{1,0:T(8,128)(2,1)} %refs_4_.1) | copy-start | bytes 196612
  19.2 8.2 %collective-permute-start.3 = (bf16[32,2,16,128]{3,2,1,0:T(8,128)(2,1)S(1)}, bf16[32,2,16,128]{3,2,1,0:T(8,128)(2,1)S(1)}, u32[]{:S(2)}, u32[]{:S(2)}) collective-permute-start(bf16[32,2,16,128]{3,2,1,0:T(8,128)(2,1)S(1)} %all_to_all.10), channel_id=1, source_target_pairs={{0,1},{1,0},{2,3},{3,2},{4,5},{5,4},{6,7},{7,6},{8,9},{9,8},{10,11... | collective-permute-start | bytes 786440 | tf_op jit(solution)/shard_map/ppermute | solution.py:312
  19.9 5.8 %collective-permute-start.2 = (bf16[8,16,256]{2,1,0:T(8,128)(2,1)S(1)}, bf16[8,16,256]{2,1,0:T(8,128)(2,1)S(1)}, u32[]{:S(2)}, u32[]{:S(2)}) collective-permute-start(bf16[8,16,256]{2,1,0:T(8,128)(2,1)S(1)} %copy-done), channel_id=1, source_target_pairs={{0,24},{8,16},{16,8},{24,0},{1,25},{9,17},{17,9},{25,1},{2,26},{10... | collective-permute-start | bytes 196616 | tf_op jit(solution)/shard_map/ppermute | solution.py:301
  20.7 5.2 %collective-permute-start.1 = (bf16[8,16,256]{2,1,0:T(8,128)(2,1)S(1)}, bf16[8,16,256]{2,1,0:T(8,128)(2,1)S(1)}, u32[]{:S(2)}, u32[]{:S(2)}) collective-permute-start(bf16[8,16,256]{2,1,0:T(8,128)(2,1)S(1)} %copy-done), channel_id=1, source_target_pairs={{0,16},{8,24},{16,0},{24,8},{1,17},{9,25},{17,1},{25,9},{2,18},{10... | collective-permute-start | bytes 196616 | tf_op jit(solution)/shard_map/ppermute | solution.py:301
  22.2 4.3 %collective-permute-start = (bf16[8,16,256]{2,1,0:T(8,128)(2,1)S(1)}, bf16[8,16,256]{2,1,0:T(8,128)(2,1)S(1)}, u32[]{:S(2)}, u32[]{:S(2)}) collective-permute-start(bf16[8,16,256]{2,1,0:T(8,128)(2,1)S(1)} %copy-done), channel_id=1, source_target_pairs={{0,8},{8,0},{16,24},{24,16},{1,9},{9,1},{17,25},{25,17},{2,10},{10... | collective-permute-start | bytes 196616 | tf_op jit(solution)/shard_map/ppermute | solution.py:301
  27.4 8.4 %copy-start.8 = (bf16[128,256]{1,0:T(8,128)(2,1)S(1)}, bf16[128,256]{1,0:T(8,128)(2,1)}, u32[]{:S(2)}) copy-start(bf16[128,256]{1,0:T(8,128)(2,1)} %refs_9_.1) | copy-start | bytes 196612
  28.1 7.7 %copy-start.4 = (bf16[128,256]{1,0:T(8,128)(2,1)S(1)}, bf16[128,256]{1,0:T(8,128)(2,1)}, u32[]{:S(2)}) copy-start(bf16[128,256]{1,0:T(8,128)(2,1)} %refs_5_.1) | copy-start | bytes 196612
  28.1 7.7 %copy-start.5 = (bf16[256,128]{1,0:T(8,128)(2,1)S(1)}, bf16[256,128]{1,0:T(8,128)(2,1)}, u32[]{:S(2)}) copy-start(bf16[256,128]{1,0:T(8,128)(2,1)} %refs_6_.1) | copy-start | bytes 196612
  28.1 7.7 %copy-start.6 = (bf16[256,128]{1,0:T(8,128)(2,1)S(1)}, bf16[256,128]{1,0:T(8,128)(2,1)}, u32[]{:S(2)}) copy-start(bf16[256,128]{1,0:T(8,128)(2,1)} %refs_7_.1) | copy-start | bytes 196612
  28.1 7.7 %copy-start.7 = (bf16[256,128]{1,0:T(8,128)(2,1)S(1)}, bf16[256,128]{1,0:T(8,128)(2,1)}, u32[]{:S(2)}) copy-start(bf16[256,128]{1,0:T(8,128)(2,1)} %refs_8_.1) | copy-start | bytes 196612

commit v7 on v6

--- a/solution.py
+++ b/solution.py
@@ -152,10 +152,10 @@
 
 
 def query_kernel(*refs):
-    fields, (weight_ref, mine_ref, query_ref, logits_ref) = refs[:-4], refs[-4:]
-    own, half = lax.axis_index("seq"), lax.rem(lax.axis_index("col"), 2)
+    fields, (weight_ref, query_ref) = refs[:-2], refs[-2:]
+    own = lax.axis_index("seq")
     seq_dev, col_dev, width = fields[0].shape
-    seq, col, _, _, lanes = mine_ref.shape
+    seq, lanes = len(fields), weight_ref.shape[1]
     group = lax.broadcasted_iota(jnp.int32, weight_ref.shape, 1) // HEAD_DIM
     weight = weight_ref[...].astype(jnp.float32)
     spread = []
@@ -182,20 +182,16 @@
         for part in range(halves):
             start = (place * halves + part) * col_dev
             query_ref[part, own ^ place] = queries[start : start + col_dev]
-    logits = jnp.zeros(logits_ref.shape, jnp.float32)
-    for source in range(seq):
-        keys = mine_ref[source, :, 0].reshape(col * col_dev, lanes)
-        logits += contract_last(query_ref[half, source], keys)
-    logits_ref[...] = logits
-
-
-def attend_kernel(scale, mine_ref, other_ref, query_ref, logits_ref, out_ref):
+
+
+def attend_kernel(scale, mine_ref, other_ref, query_ref, out_ref):
     half = lax.rem(lax.axis_index("col"), 2)
     seq, col, _, col_dev, lanes = mine_ref.shape
-    logits = logits_ref[...]
-    for source in range(seq):
-        keys = other_ref[source, :, 0].reshape(col * col_dev, lanes)
-        logits += contract_last(query_ref[1 - half, source], keys)
+    logits = jnp.zeros((col_dev, col * col_dev), jnp.float32)
+    for ref, part in ((mine_ref, half), (other_ref, 1 - half)):
+        for source in range(seq):
+            keys = ref[source, :, 0].reshape(col * col_dev, lanes)
+            logits += contract_last(query_ref[part, source], keys)
     logits = logits * scale
     weights = jnp.exp(logits - jnp.max(logits, axis=-1, keepdims=True))
     probs = (weights / jnp.sum(weights, axis=-1, keepdims=True)).astype(jnp.bfloat16)
@@ -313,25 +309,22 @@
     shape = (seq, col, 2, col_dev, inner)
     mine, other = mine.reshape(shape), other.reshape(shape)
     halves = seq_dev // HEADS
-    queries, logits = pl.pallas_call(
+    queries = pl.pallas_call(
         query_kernel,
-        out_shape=(
-            jax.ShapeDtypeStruct((halves, seq, col_dev, inner), bf16),
-            jax.ShapeDtypeStruct((col_dev, col * col_dev), f32),
-        ),
-        in_specs=[vmem] * (seq + 2),
-        out_specs=(vmem, vmem),
+        out_shape=jax.ShapeDtypeStruct((halves, seq, col_dev, inner), bf16),
+        in_specs=[vmem] * (seq + 1),
+        out_specs=vmem,
         compiler_params=grant,
         name="query",
-    )(*fields, row_query, mine)
+    )(*fields, row_query)
     parts = pl.pallas_call(
         functools.partial(attend_kernel, scale),
         out_shape=jax.ShapeDtypeStruct((seq, halves * seq, col_dev, inner), bf16),
-        in_specs=[vmem] * 4,
+        in_specs=[vmem] * 3,
         out_specs=vmem,
         compiler_params=grant,
         name="attend",
-    )(mine, other, queries, logits)
+    )(mine, other, queries)
     parts = lax.all_to_all(parts, "seq", 0, 0)
     total = seq * seq_dev * col_dev
     local = seq_dev * col_dev

time: 38.5 us -> 38.4 us (level)
  no operation moved by 1% of the time
where the time goes in v7:
time: 38.4 us; the launch traced here: 38.1 us
  blocking collectives  24.8 us (65%)
  Pallas kernels  4.34 us (11%)
  starting transfers between devices  4.23 us (11%)
  waiting for transfers between devices  3.07 us (8%)
  local copies, waits for them, and re-layouts  0.91 us (2%)
  between operations  0.75 us (2%)
    all_to_all x1, blocking collectives, by_head(): lax.all_to_all(blocks.reshape(seq * col, 2, col_dev, inner), ('seq', 'col...  17.1 us
    all_to_all x1, blocking collectives, by_head(): parts = lax.all_to_all(parts, 'seq', 0, 0)  7.69 us
    ppermute x3, starting transfers between devices, by_head(): lax.ppermute(alignment, 'seq', [(i, i ^ place) for i in range(seq)])  3.49 us
    ppermute x3, waiting for transfers between devices, by_head(): lax.ppermute(alignment, 'seq', [(i, i ^ place) for i in range(seq)])  3.06 us
    pallas_call x1, Pallas kernels, by_head(): pl.pallas_call(finish_kernel, out_shape=(like, like), in_specs=[vmem] * (...  2.38 us
    unnamed x18, local copies, waits for them, and re-layouts  0.91 us
    pallas_call x1, Pallas kernels, by_head(): pl.pallas_call(query_kernel, out_shape=jax.ShapeDtypeStruct((halves, seq,...  0.79 us
  transfers between devices with their start and end apart: 4, of which 3 were waited for; matrix products, arithmetic and copies ran while one was open for 0% of the time, Pallas kernels for 2%

profile of v7, /device:TPU:0, one launch (start us, length us, event | category | flops | bytes accessed | tf_op | source)
XLA Modules:
  0.0 38.1 jit_solution(3021795950488826353)
XLA Ops:
  0.6 0.0 copy-start
  0.6 0.0 copy-start.2
  0.6 0.0 copy-start.1
  0.7 0.8 %copy-done = bf16[8,16,256]{2,1,0:T(8,128)(2,1)S(1)} copy-done((bf16[8,16,256]{2,1,0:T(8,128)(2,1)S(1)}, bf16[8,16,256]{2,1,0:T(8,128)(2,1)}, u32[]{:S(2)}) %copy-start) | copy-done | bytes 65560
  1.5 0.0 copy-done.2
  1.5 0.0 copy-done.1
  1.5 0.5 %project.1 = bf16[4,4,2,2,16,128]{5,4,3,2,1,0:T(8,128)(2,1)S(1)} custom-call(bf16[8,16,256]{2,1,0:T(8,128)(2,1)S(1)} %copy-done, bf16[256,128]{1,0:T(8,128)(2,1)S(1)} %copy-done.1, bf16[256,128]{1,0:T(8,128)(2,1)S(1)} %copy-done.2, f32[8,128]{1,0:T(8,128)S(1)} %gate.1.gate_ref), custom_call_target="tpu_custom_call" | custom-call | tf_op jit(solution)/shard_map/project/pallas_call | solution.py:299
  2.0 0.0 copy-start.3
  2.0 17.1 %all_to_all.10 = bf16[32,2,16,128]{3,2,1,0:T(8,128)(2,1)S(1)} all-to-all(bf16[32,2,16,128]{3,2,1,0:T(8,128)(2,1)S(1)} %bitcast.3), channel_id=1, replica_groups=mesh['seq'=4,'col'=8] {'seq','col'}, dimensions={0} | all-to-all | bytes 524288 | tf_op jit(solution)/shard_map/all_to_all | solution.py:307
  19.2 0.7 %collective-permute-start.3 = (bf16[32,2,16,128]{3,2,1,0:T(8,128)(2,1)S(1)}, bf16[32,2,16,128]{3,2,1,0:T(8,128)(2,1)S(1)}, u32[]{:S(2)}, u32[]{:S(2)}) collective-permute-start(bf16[32,2,16,128]{3,2,1,0:T(8,128)(2,1)S(1)} %all_to_all.10), channel_id=1, source_target_pairs={{0,1},{1,0},{2,3},{3,2},{4,5},{5,4},{6,7},{7,6},{8,9},{9,8},{10,11... | collective-permute-start | bytes 786440 | tf_op jit(solution)/shard_map/ppermute | solution.py:308
  19.9 0.8 %collective-permute-start.2 = (bf16[8,16,256]{2,1,0:T(8,128)(2,1)S(1)}, bf16[8,16,256]{2,1,0:T(8,128)(2,1)S(1)}, u32[]{:S(2)}, u32[]{:S(2)}) collective-permute-start(bf16[8,16,256]{2,1,0:T(8,128)(2,1)S(1)} %copy-done), channel_id=1, source_target_pairs={{0,24},{8,16},{16,8},{24,0},{1,25},{9,17},{17,9},{25,1},{2,26},{10... | collective-permute-start | bytes 196616 | tf_op jit(solution)/shard_map/ppermute | solution.py:297
  20.7 1.5 %collective-permute-start.1 = (bf16[8,16,256]{2,1,0:T(8,128)(2,1)S(1)}, bf16[8,16,256]{2,1,0:T(8,128)(2,1)S(1)}, u32[]{:S(2)}, u32[]{:S(2)}) collective-permute-start(bf16[8,16,256]{2,1,0:T(8,128)(2,1)S(1)} %copy-done), channel_id=1, source_target_pairs={{0,16},{8,24},{16,0},{24,8},{1,17},{9,25},{17,1},{25,9},{2,18},{10... | collective-permute-start | bytes 196616 | tf_op jit(solution)/shard_map/ppermute | solution.py:297
  22.2 1.2 %collective-permute-start = (bf16[8,16,256]{2,1,0:T(8,128)(2,1)S(1)}, bf16[8,16,256]{2,1,0:T(8,128)(2,1)S(1)}, u32[]{:S(2)}, u32[]{:S(2)}) collective-permute-start(bf16[8,16,256]{2,1,0:T(8,128)(2,1)S(1)} %copy-done), channel_id=1, source_target_pairs={{0,8},{8,0},{16,24},{24,16},{1,9},{9,1},{17,25},{25,17},{2,10},{10... | collective-permute-start | bytes 196616 | tf_op jit(solution)/shard_map/ppermute | solution.py:297
  23.4 2.3 %collective-permute-done.2.refs_3_ = bf16[8,16,256]{2,1,0:T(8,128)(2,1)S(1)} collective-permute-done((bf16[8,16,256]{2,1,0:T(8,128)(2,1)S(1)}, bf16[8,16,256]{2,1,0:T(8,128)(2,1)S(1)}, u32[]{:S(2)}, u32[]{:S(2)}) %collective-permute-start.2) | collective-permute-done | bytes 65568 | tf_op jit(solution)/shard_map/ppermute | solution.py:297
  25.7 0.2 collective-permute-done.1.refs_2_
  25.9 0.5 %collective-permute-done.refs_1_ = bf16[8,16,256]{2,1,0:T(8,128)(2,1)S(1)} collective-permute-done((bf16[8,16,256]{2,1,0:T(8,128)(2,1)S(1)}, bf16[8,16,256]{2,1,0:T(8,128)(2,1)S(1)}, u32[]{:S(2)}, u32[]{:S(2)}) %collective-permute-start) | collective-permute-done | bytes 65568 | tf_op jit(solution)/shard_map/ppermute | solution.py:297
  26.5 0.0 copy-done.3
  26.5 0.8 %query.1.query_ref = bf16[2,4,16,128]{3,2,1,0:T(8,128)(2,1)S(1)} custom-call(bf16[8,16,256]{2,1,0:T(8,128)(2,1)S(1)} %copy-done, bf16[8,16,256]{2,1,0:T(8,128)(2,1)S(1)} %collective-permute-done.refs_1_, bf16[8,16,256]{2,1,0:T(8,128)(2,1)S(1)} %collective-permute-done.1.refs_2_, bf16[8,16,256]{2,1,0:T(8,128)(2,1)S(1)} %collective-permute-done.2.refs_3_, ...), custom_call_target="tpu_custom_call" | custom-call | tf_op jit(solution)/shard_map/query/pallas_call | solution.py:312
  27.3 0.0 collective-permute-done.3
  27.3 0.0 copy-start.8
  27.3 0.7 %attend.1 = bf16[4,8,16,128]{3,2,1,0:T(8,128)(2,1)S(1)} custom-call(bf16[4,8,2,16,128]{4,3,2,1,0:T(8,128)(2,1)S(1)} %bitcast.4, bf16[4,8,2,16,128]{4,3,2,1,0:T(8,128)(2,1)S(1)} %bitcast.5, bf16[2,4,16,128]{3,2,1,0:T(8,128)(2,1)S(1)} %query.1.query_ref), custom_call_target="tpu_custom_call" | custom-call | tf_op jit(solution)/shard_map/attend/pallas_call | solution.py:320
  28.0 0.0 copy-start.4
  28.0 0.0 copy-start.5
  28.0 0.0 copy-start.6
  28.0 0.0 copy-start.7
  28.0 7.7 %all_to_all.11.refs_4_ = bf16[4,8,16,128]{3,2,1,0:T(8,128)(2,1)S(1)} all-to-all(bf16[4,8,16,128]{3,2,1,0:T(8,128)(2,1)S(1)} %attend.1), channel_id=1, replica_groups=mesh['seq'=4,'col'=8] {'seq'}, dimensions={0} | all-to-all | bytes 262144 | tf_op jit(solution)/shard_map/all_to_all | solution.py:328
  35.7 0.0 copy-done.8
  35.7 0.0 copy-done.4
  35.7 0.0 copy-done.5
  35.7 0.0 copy-done.6
  35.7 0.0 copy-done.7
  35.7 2.4 %finish.1 = (bf16[8,16,256]{2,1,0:T(8,128)(2,1)}, bf16[8,16,256]{2,1,0:T(8,128)(2,1)}) custom-call(bf16[8,16,256]{2,1,0:T(8,128)(2,1)S(1)} %copy-done, bf16[8,16,256]{2,1,0:T(8,128)(2,1)S(1)} %collective-permute-done.refs_1_, bf16[8,16,256]{2,1,0:T(8,128)(2,1)S(1)} %collective-permute-done.1.refs_2_, bf16[8,16,256]{2,1,0:T(8,128)(2,1)S(1)} %collective-permute-done.2.refs_3_, ...), custom_call_target="tpu_custom_call" | custom-call | tf_op jit(solution)/shard_map/finish/pallas_call | solution.py:332
  (1 shorter events, 0.0 us)
Async XLA Ops:
  0.6 0.8 %copy-start = (bf16[8,16,256]{2,1,0:T(8,128)(2,1)S(1)}, bf16[8,16,256]{2,1,0:T(8,128)(2,1)}, u32[]{:S(2)}) copy-start(bf16[8,16,256]{2,1,0:T(8,128)(2,1)} %refs_0_.3) | copy-start | bytes 196612
  0.6 0.9 %copy-start.2 = (bf16[256,128]{1,0:T(8,128)(2,1)S(1)}, bf16[256,128]{1,0:T(8,128)(2,1)}, u32[]{:S(2)}) copy-start(bf16[256,128]{1,0:T(8,128)(2,1)} %value_ref.1) | copy-start | bytes 196612
  0.6 0.9 %copy-start.1 = (bf16[256,128]{1,0:T(8,128)(2,1)S(1)}, bf16[256,128]{1,0:T(8,128)(2,1)}, u32[]{:S(2)}) copy-start(bf16[256,128]{1,0:T(8,128)(2,1)} %key_ref.1) | copy-start | bytes 196612
  2.0 24.4 %copy-start.3 = (bf16[256,128]{1,0:T(8,128)(2,1)S(1)}, bf16[256,128]{1,0:T(8,128)(2,1)}, u32[]{:S(2)}) copy-start(bf16[256,128]{1,0:T(8,128)(2,1)} %refs_4_.1) | copy-start | bytes 196612
  19.2 8.1 %collective-permute-start.3 = (bf16[32,2,16,128]{3,2,1,0:T(8,128)(2,1)S(1)}, bf16[32,2,16,128]{3,2,1,0:T(8,128)(2,1)S(1)}, u32[]{:S(2)}, u32[]{:S(2)}) collective-permute-start(bf16[32,2,16,128]{3,2,1,0:T(8,128)(2,1)S(1)} %all_to_all.10), channel_id=1, source_target_pairs={{0,1},{1,0},{2,3},{3,2},{4,5},{5,4},{6,7},{7,6},{8,9},{9,8},{10,11... | collective-permute-start | bytes 786440 | tf_op jit(solution)/shard_map/ppermute | solution.py:308
  19.9 5.8 %collective-permute-start.2 = (bf16[8,16,256]{2,1,0:T(8,128)(2,1)S(1)}, bf16[8,16,256]{2,1,0:T(8,128)(2,1)S(1)}, u32[]{:S(2)}, u32[]{:S(2)}) collective-permute-start(bf16[8,16,256]{2,1,0:T(8,128)(2,1)S(1)} %copy-done), channel_id=1, source_target_pairs={{0,24},{8,16},{16,8},{24,0},{1,25},{9,17},{17,9},{25,1},{2,26},{10... | collective-permute-start | bytes 196616 | tf_op jit(solution)/shard_map/ppermute | solution.py:297
  20.7 5.2 %collective-permute-start.1 = (bf16[8,16,256]{2,1,0:T(8,128)(2,1)S(1)}, bf16[8,16,256]{2,1,0:T(8,128)(2,1)S(1)}, u32[]{:S(2)}, u32[]{:S(2)}) collective-permute-start(bf16[8,16,256]{2,1,0:T(8,128)(2,1)S(1)} %copy-done), channel_id=1, source_target_pairs={{0,16},{8,24},{16,0},{24,8},{1,17},{9,25},{17,1},{25,9},{2,18},{10... | collective-permute-start | bytes 196616 | tf_op jit(solution)/shard_map/ppermute | solution.py:297
  22.2 4.3 %collective-permute-start = (bf16[8,16,256]{2,1,0:T(8,128)(2,1)S(1)}, bf16[8,16,256]{2,1,0:T(8,128)(2,1)S(1)}, u32[]{:S(2)}, u32[]{:S(2)}) collective-permute-start(bf16[8,16,256]{2,1,0:T(8,128)(2,1)S(1)} %copy-done), channel_id=1, source_target_pairs={{0,8},{8,0},{16,24},{24,16},{1,9},{9,1},{17,25},{25,17},{2,10},{10... | collective-permute-start | bytes 196616 | tf_op jit(solution)/shard_map/ppermute | solution.py:297
  27.3 8.4 %copy-start.8 = (bf16[128,256]{1,0:T(8,128)(2,1)S(1)}, bf16[128,256]{1,0:T(8,128)(2,1)}, u32[]{:S(2)}) copy-start(bf16[128,256]{1,0:T(8,128)(2,1)} %refs_9_.1) | copy-start | bytes 196612
  28.0 7.7 %copy-start.4 = (bf16[128,256]{1,0:T(8,128)(2,1)S(1)}, bf16[128,256]{1,0:T(8,128)(2,1)}, u32[]{:S(2)}) copy-start(bf16[128,256]{1,0:T(8,128)(2,1)} %refs_5_.1) | copy-start | bytes 196612
  28.0 7.7 %copy-start.5 = (bf16[256,128]{1,0:T(8,128)(2,1)S(1)}, bf16[256,128]{1,0:T(8,128)(2,1)}, u32[]{:S(2)}) copy-start(bf16[256,128]{1,0:T(8,128)(2,1)} %refs_6_.1) | copy-start | bytes 196612
  28.0 7.7 %copy-start.6 = (bf16[256,128]{1,0:T(8,128)(2,1)S(1)}, bf16[256,128]{1,0:T(8,128)(2,1)}, u32[]{:S(2)}) copy-start(bf16[256,128]{1,0:T(8,128)(2,1)} %refs_7_.1) | copy-start | bytes 196612
  28.0 7.7 %copy-start.7 = (bf16[256,128]{1,0:T(8,128)(2,1)S(1)}, bf16[256,128]{1,0:T(8,128)(2,1)}, u32[]{:S(2)}) copy-start(bf16[256,128]{1,0:T(8,128)(2,1)} %refs_8_.1) | copy-start | bytes 196612

commit v8 on v7

--- a/solution.py
+++ b/solution.py
@@ -198,18 +198,25 @@
     for ref, part in ((mine_ref, half), (other_ref, 1 - half)):
         for source in range(seq):
             values = ref[source, :, 1].reshape(col * col_dev, lanes)
-            context = project(probs, values).astype(jnp.bfloat16)
-            for copy in range(seq):
-                out_ref[copy, part * seq + source] = context
+            out_ref[part * seq + source] = project(probs, values).astype(jnp.bfloat16)
 
 
 def finish_kernel(*refs):
-    fields, refs = refs[:-13], refs[-13:]
-    (parts_ref, row_output_ref, query_ref, key_ref, value_ref, output_ref) = refs[:6]
-    update_ref, layer_ref, middles, queries, keys, values, contexts = refs[6:]
+    tail = refs[-7:]
+    refs, (row_output_ref, query_ref, key_ref, value_ref, output_ref) = refs[:-12], refs[-12:-7]
+    fields, parts = refs[: len(refs) // 2], refs[len(refs) // 2 :]
+    update_ref, layer_ref, middles, queries, keys, values, contexts = tail
     own = lax.axis_index("seq")
-    seq, _, col_dev, lanes = parts_ref.shape
+    seq = len(parts)
+    _, col_dev, lanes = parts[0].shape
     seq_dev, _, width = update_ref.shape
+    row_output = jnp.concatenate(
+        [
+            row_output_ref[pl.ds(pl.multiple_of((own ^ place) * HEAD_DIM, HEAD_DIM), HEAD_DIM), :]
+            for place in range(HEADS)
+        ],
+        axis=0,
+    )
     rows = seq_dev * col_dev
     seqs = seq * seq_dev
     pair = jnp.concatenate([key_ref[...], value_ref[...]], axis=1)
@@ -217,12 +224,10 @@
         source = own ^ place
         context = []
         for half in range(seq_dev // HEADS):
-            heads = [
-                parts_ref[head, half * seq + source].astype(jnp.float32) for head in range(HEADS)
-            ]
+            heads = [part_ref[half * seq + source].astype(jnp.float32) for part_ref in parts]
             context += swap_groups(heads, HEAD_DIM)
         context = jnp.concatenate(context, axis=0).astype(jnp.bfloat16)
-        update = project(context, row_output_ref[...])
+        update = project(context, row_output)
         middle = field_ref[...].reshape(rows, width).astype(jnp.float32) + update
         normal = norm_rows(middle)
         here = slice(place * rows, (place + 1) * rows)
@@ -319,20 +324,22 @@
     )(*fields, row_query)
     parts = pl.pallas_call(
         functools.partial(attend_kernel, scale),
-        out_shape=jax.ShapeDtypeStruct((seq, halves * seq, col_dev, inner), bf16),
+        out_shape=jax.ShapeDtypeStruct((halves * seq, col_dev, inner), bf16),
         in_specs=[vmem] * 3,
         out_specs=vmem,
         compiler_params=grant,
         name="attend",
     )(mine, other, queries)
-    parts = lax.all_to_all(parts, "seq", 0, 0)
+    parts = [parts] * seq
+    for place in range(seq - 1, 0, -1):
+        parts[place] = lax.ppermute(parts[place], "seq", [(i, i ^ place) for i in range(seq)])
     total = seq * seq_dev * col_dev
     local = seq_dev * col_dev
     like = jax.ShapeDtypeStruct(alignment.shape, bf16)
     return pl.pallas_call(
         finish_kernel,
         out_shape=(like, like),
-        in_specs=[vmem] * (seq + 6),
+        in_specs=[vmem] * (2 * seq + 5),
         out_specs=(vmem, vmem),
         scratch_shapes=[
             pltpu.VMEM((local, width), f32),
@@ -343,7 +350,7 @@
         ],
         compiler_params=grant,
         name="finish",
-    )(*fields, parts, row_output, column_query, column_key, column_value, column_output)
+    )(*fields, *parts, row_output, column_query, column_key, column_value, column_output)
 
 
 def suits_by_head(seq, col, seq_dev, col_dev, width, inner):

time: 38.4 us -> 37.3 us (0.971)
  blocking collectives: 24.8 us -> 17.1 us
  starting transfers between devices: 4.23 us -> 7.77 us
  waiting for transfers between devices: 3.07 us -> 6.16 us
    all_to_all x1 -> x0, blocking collectives: 7.69 us -> none  [by_head(): parts = lax.all_to_all(parts, 'seq', 0, 0)]
    ppermute x0 -> x3, starting transfers between devices: none -> 3.54 us  [by_head(): lax.ppermute(parts[place], 'seq', [(i, i ^ place) for i in range(seq)])]
    ppermute x0 -> x3, waiting for transfers between devices: none -> 3.09 us  [by_head(): lax.ppermute(parts[place], 'seq', [(i, i ^ place) for i in range(seq)])]
  transfers between devices with their start and end apart: 4 -> 7, of which waited for: 3 -> 6; matrix products, arithmetic and copies ran while one was open for 0% -> 0% of each run, Pallas kernels for 2% -> 2%
where the time goes in v8:
time: 37.3 us; the launch traced here: 37.1 us
  blocking collectives  17.1 us (46%)
  starting transfers between devices  7.77 us (21%)
  waiting for transfers between devices  6.16 us (17%)
  Pallas kernels  4.34 us (12%)
  local copies, waits for them, and re-layouts  0.91 us (2%)
  between operations  0.75 us (2%)
    all_to_all x1, blocking collectives, by_head(): lax.all_to_all(blocks.reshape(seq * col, 2, col_dev, inner), ('seq', 'col...  17.1 us
    ppermute x3, starting transfers between devices, by_head(): lax.ppermute(parts[place], 'seq', [(i, i ^ place) for i in range(seq)])  3.54 us
    ppermute x3, starting transfers between devices, by_head(): lax.ppermute(alignment, 'seq', [(i, i ^ place) for i in range(seq)])  3.49 us
    ppermute x3, waiting for transfers between devices, by_head(): lax.ppermute(parts[place], 'seq', [(i, i ^ place) for i in range(seq)])  3.09 us
    ppermute x3, waiting for transfers between devices, by_head(): lax.ppermute(alignment, 'seq', [(i, i ^ place) for i in range(seq)])  3.06 us
    pallas_call x1, Pallas kernels, by_head(): pl.pallas_call(finish_kernel, out_shape=(like, like), in_specs=[vmem] * (...  2.39 us
    unnamed x18, local copies, waits for them, and re-layouts  0.91 us
    pallas_call x1, Pallas kernels, by_head(): pl.pallas_call(query_kernel, out_shape=jax.ShapeDtypeStruct((halves, seq,...  0.79 us
  transfers between devices with their start and end apart: 7, of which 6 were waited for; matrix products, arithmetic and copies ran while one was open for 0% of the time, Pallas kernels for 2%

profile of v8, /device:TPU:0, one launch (start us, length us, event | category | flops | bytes accessed | tf_op | source)
XLA Modules:
  0.0 37.1 jit_solution(5512743534204544869)
XLA Ops:
  0.6 0.0 copy-start
  0.6 0.0 copy-start.2
  0.6 0.0 copy-start.1
  0.7 0.8 %copy-done = bf16[8,16,256]{2,1,0:T(8,128)(2,1)S(1)} copy-done((bf16[8,16,256]{2,1,0:T(8,128)(2,1)S(1)}, bf16[8,16,256]{2,1,0:T(8,128)(2,1)}, u32[]{:S(2)}) %copy-start) | copy-done | bytes 65560
  1.5 0.0 copy-done.2
  1.5 0.0 copy-done.1
  1.5 0.5 %project.1 = bf16[4,4,2,2,16,128]{5,4,3,2,1,0:T(8,128)(2,1)S(1)} custom-call(bf16[8,16,256]{2,1,0:T(8,128)(2,1)S(1)} %copy-done, bf16[256,128]{1,0:T(8,128)(2,1)S(1)} %copy-done.1, bf16[256,128]{1,0:T(8,128)(2,1)S(1)} %copy-done.2, f32[8,128]{1,0:T(8,128)S(1)} %gate.1.gate_ref), custom_call_target="tpu_custom_call" | custom-call | tf_op jit(solution)/shard_map/project/pallas_call | solution.py:304
  2.0 0.0 copy-start.3
  2.0 17.1 %all_to_all.5 = bf16[32,2,16,128]{3,2,1,0:T(8,128)(2,1)S(1)} all-to-all(bf16[32,2,16,128]{3,2,1,0:T(8,128)(2,1)S(1)} %bitcast.3), channel_id=1, replica_groups=mesh['seq'=4,'col'=8] {'seq','col'}, dimensions={0} | all-to-all | bytes 524288 | tf_op jit(solution)/shard_map/all_to_all | solution.py:312
  19.2 0.7 %collective-permute-start.3 = (bf16[32,2,16,128]{3,2,1,0:T(8,128)(2,1)S(1)}, bf16[32,2,16,128]{3,2,1,0:T(8,128)(2,1)S(1)}, u32[]{:S(2)}, u32[]{:S(2)}) collective-permute-start(bf16[32,2,16,128]{3,2,1,0:T(8,128)(2,1)S(1)} %all_to_all.5), channel_id=1, source_target_pairs={{0,1},{1,0},{2,3},{3,2},{4,5},{5,4},{6,7},{7,6},{8,9},{9,8},{10,11... | collective-permute-start | bytes 786440 | tf_op jit(solution)/shard_map/ppermute | solution.py:313
  19.9 0.8 %collective-permute-start.2 = (bf16[8,16,256]{2,1,0:T(8,128)(2,1)S(1)}, bf16[8,16,256]{2,1,0:T(8,128)(2,1)S(1)}, u32[]{:S(2)}, u32[]{:S(2)}) collective-permute-start(bf16[8,16,256]{2,1,0:T(8,128)(2,1)S(1)} %copy-done), channel_id=1, source_target_pairs={{0,24},{8,16},{16,8},{24,0},{1,25},{9,17},{17,9},{25,1},{2,26},{10... | collective-permute-start | bytes 196616 | tf_op jit(solution)/shard_map/ppermute | solution.py:302
  20.7 1.5 %collective-permute-start.1 = (bf16[8,16,256]{2,1,0:T(8,128)(2,1)S(1)}, bf16[8,16,256]{2,1,0:T(8,128)(2,1)S(1)}, u32[]{:S(2)}, u32[]{:S(2)}) collective-permute-start(bf16[8,16,256]{2,1,0:T(8,128)(2,1)S(1)} %copy-done), channel_id=1, source_target_pairs={{0,16},{8,24},{16,0},{24,8},{1,17},{9,25},{17,1},{25,9},{2,18},{10... | collective-permute-start | bytes 196616 | tf_op jit(solution)/shard_map/ppermute | solution.py:302
  22.2 1.2 %collective-permute-start = (bf16[8,16,256]{2,1,0:T(8,128)(2,1)S(1)}, bf16[8,16,256]{2,1,0:T(8,128)(2,1)S(1)}, u32[]{:S(2)}, u32[]{:S(2)}) collective-permute-start(bf16[8,16,256]{2,1,0:T(8,128)(2,1)S(1)} %copy-done), channel_id=1, source_target_pairs={{0,8},{8,0},{16,24},{24,16},{1,9},{9,1},{17,25},{25,17},{2,10},{10... | collective-permute-start | bytes 196616 | tf_op jit(solution)/shard_map/ppermute | solution.py:302
  23.4 2.3 %collective-permute-done.2.refs_3_ = bf16[8,16,256]{2,1,0:T(8,128)(2,1)S(1)} collective-permute-done((bf16[8,16,256]{2,1,0:T(8,128)(2,1)S(1)}, bf16[8,16,256]{2,1,0:T(8,128)(2,1)S(1)}, u32[]{:S(2)}, u32[]{:S(2)}) %collective-permute-start.2) | collective-permute-done | bytes 65568 | tf_op jit(solution)/shard_map/ppermute | solution.py:302
  25.7 0.2 collective-permute-done.1.refs_2_
  25.9 0.5 %collective-permute-done.refs_1_ = bf16[8,16,256]{2,1,0:T(8,128)(2,1)S(1)} collective-permute-done((bf16[8,16,256]{2,1,0:T(8,128)(2,1)S(1)}, bf16[8,16,256]{2,1,0:T(8,128)(2,1)S(1)}, u32[]{:S(2)}, u32[]{:S(2)}) %collective-permute-start) | collective-permute-done | bytes 65568 | tf_op jit(solution)/shard_map/ppermute | solution.py:302
  26.5 0.0 copy-done.3
  26.5 0.8 %query.1.query_ref = bf16[2,4,16,128]{3,2,1,0:T(8,128)(2,1)S(1)} custom-call(bf16[8,16,256]{2,1,0:T(8,128)(2,1)S(1)} %copy-done, bf16[8,16,256]{2,1,0:T(8,128)(2,1)S(1)} %collective-permute-done.refs_1_, bf16[8,16,256]{2,1,0:T(8,128)(2,1)S(1)} %collective-permute-done.1.refs_2_, bf16[8,16,256]{2,1,0:T(8,128)(2,1)S(1)} %collective-permute-done.2.refs_3_, ...), custom_call_target="tpu_custom_call" | custom-call | tf_op jit(solution)/shard_map/query/pallas_call | solution.py:317
  27.3 0.0 collective-permute-done.3
  27.3 0.0 copy-start.4
  27.3 0.0 copy-start.5
  27.3 0.0 copy-start.6
  27.3 0.0 copy-start.7
  27.3 0.0 copy-start.8
  27.3 0.7 %attend.1.refs_4_ = bf16[8,16,128]{2,1,0:T(8,128)(2,1)S(1)} custom-call(bf16[4,8,2,16,128]{4,3,2,1,0:T(8,128)(2,1)S(1)} %bitcast.4, bf16[4,8,2,16,128]{4,3,2,1,0:T(8,128)(2,1)S(1)} %bitcast.5, bf16[2,4,16,128]{3,2,1,0:T(8,128)(2,1)S(1)} %query.1.query_ref), custom_call_target="tpu_custom_call" | custom-call | tf_op jit(solution)/shard_map/attend/pallas_call | solution.py:325
  28.0 1.5 %collective-permute-start.6 = (bf16[8,16,128]{2,1,0:T(8,128)(2,1)S(1)}, bf16[8,16,128]{2,1,0:T(8,128)(2,1)S(1)}, u32[]{:S(2)}, u32[]{:S(2)}) collective-permute-start(bf16[8,16,128]{2,1,0:T(8,128)(2,1)S(1)} %attend.1.refs_4_), channel_id=1, source_target_pairs={{0,24},{8,16},{16,8},{24,0},{1,25},{9,17},{17,9},{25,1},{2,26},{10... | collective-permute-start | bytes 98312 | tf_op jit(solution)/shard_map/ppermute | solution.py:335
  29.5 1.2 %collective-permute-start.5 = (bf16[8,16,128]{2,1,0:T(8,128)(2,1)S(1)}, bf16[8,16,128]{2,1,0:T(8,128)(2,1)S(1)}, u32[]{:S(2)}, u32[]{:S(2)}) collective-permute-start(bf16[8,16,128]{2,1,0:T(8,128)(2,1)S(1)} %attend.1.refs_4_), channel_id=1, source_target_pairs={{0,16},{8,24},{16,0},{24,8},{1,17},{9,25},{17,1},{25,9},{2,18},{10... | collective-permute-start | bytes 98312 | tf_op jit(solution)/shard_map/ppermute | solution.py:335
  30.7 0.8 %collective-permute-start.4 = (bf16[8,16,128]{2,1,0:T(8,128)(2,1)S(1)}, bf16[8,16,128]{2,1,0:T(8,128)(2,1)S(1)}, u32[]{:S(2)}, u32[]{:S(2)}) collective-permute-start(bf16[8,16,128]{2,1,0:T(8,128)(2,1)S(1)} %attend.1.refs_4_), channel_id=1, source_target_pairs={{0,8},{8,0},{16,24},{24,16},{1,9},{9,1},{17,25},{25,17},{2,10},{10... | collective-permute-start | bytes 98312 | tf_op jit(solution)/shard_map/ppermute | solution.py:335
  31.6 1.3 %collective-permute-done.6.refs_7_ = bf16[8,16,128]{2,1,0:T(8,128)(2,1)S(1)} collective-permute-done((bf16[8,16,128]{2,1,0:T(8,128)(2,1)S(1)}, bf16[8,16,128]{2,1,0:T(8,128)(2,1)S(1)}, u32[]{:S(2)}, u32[]{:S(2)}) %collective-permute-start.6) | collective-permute-done | bytes 32800 | tf_op jit(solution)/shard_map/ppermute | solution.py:335
  32.9 0.6 %collective-permute-done.5.refs_6_ = bf16[8,16,128]{2,1,0:T(8,128)(2,1)S(1)} collective-permute-done((bf16[8,16,128]{2,1,0:T(8,128)(2,1)S(1)}, bf16[8,16,128]{2,1,0:T(8,128)(2,1)S(1)}, u32[]{:S(2)}, u32[]{:S(2)}) %collective-permute-start.5) | collective-permute-done | bytes 32800 | tf_op jit(solution)/shard_map/ppermute | solution.py:335
  33.5 1.2 %collective-permute-done.4.refs_5_ = bf16[8,16,128]{2,1,0:T(8,128)(2,1)S(1)} collective-permute-done((bf16[8,16,128]{2,1,0:T(8,128)(2,1)S(1)}, bf16[8,16,128]{2,1,0:T(8,128)(2,1)S(1)}, u32[]{:S(2)}, u32[]{:S(2)}) %collective-permute-start.4) | collective-permute-done | bytes 32800 | tf_op jit(solution)/shard_map/ppermute | solution.py:335
  34.7 0.0 copy-done.4
  34.7 0.0 copy-done.5
  34.7 0.0 copy-done.6
  34.7 0.0 copy-done.7
  34.7 0.0 copy-done.8
  34.7 2.4 %finish.1 = (bf16[8,16,256]{2,1,0:T(8,128)(2,1)}, bf16[8,16,256]{2,1,0:T(8,128)(2,1)}) custom-call(bf16[8,16,256]{2,1,0:T(8,128)(2,1)S(1)} %copy-done, bf16[8,16,256]{2,1,0:T(8,128)(2,1)S(1)} %collective-permute-done.refs_1_, bf16[8,16,256]{2,1,0:T(8,128)(2,1)S(1)} %collective-permute-done.1.refs_2_, bf16[8,16,256]{2,1,0:T(8,128)(2,1)S(1)} %collective-permute-done.2.refs_3_, ...), custom_call_target="tpu_custom_call" | custom-call | tf_op jit(solution)/shard_map/finish/pallas_call | solution.py:339
  (1 shorter events, 0.0 us)
Async XLA Ops:
  0.6 0.8 %copy-start = (bf16[8,16,256]{2,1,0:T(8,128)(2,1)S(1)}, bf16[8,16,256]{2,1,0:T(8,128)(2,1)}, u32[]{:S(2)}) copy-start(bf16[8,16,256]{2,1,0:T(8,128)(2,1)} %refs_0_.3) | copy-start | bytes 196612
  0.6 0.9 %copy-start.2 = (bf16[256,128]{1,0:T(8,128)(2,1)S(1)}, bf16[256,128]{1,0:T(8,128)(2,1)}, u32[]{:S(2)}) copy-start(bf16[256,128]{1,0:T(8,128)(2,1)} %value_ref.1) | copy-start | bytes 196612
  0.6 0.9 %copy-start.1 = (bf16[256,128]{1,0:T(8,128)(2,1)S(1)}, bf16[256,128]{1,0:T(8,128)(2,1)}, u32[]{:S(2)}) copy-start(bf16[256,128]{1,0:T(8,128)(2,1)} %key_ref.1) | copy-start | bytes 196612
  2.0 24.4 %copy-start.3 = (bf16[256,128]{1,0:T(8,128)(2,1)S(1)}, bf16[256,128]{1,0:T(8,128)(2,1)}, u32[]{:S(2)}) copy-start(bf16[256,128]{1,0:T(8,128)(2,1)} %refs_4_.1) | copy-start | bytes 196612
  19.2 8.1 %collective-permute-start.3 = (bf16[32,2,16,128]{3,2,1,0:T(8,128)(2,1)S(1)}, bf16[32,2,16,128]{3,2,1,0:T(8,128)(2,1)S(1)}, u32[]{:S(2)}, u32[]{:S(2)}) collective-permute-start(bf16[32,2,16,128]{3,2,1,0:T(8,128)(2,1)S(1)} %all_to_all.5), channel_id=1, source_target_pairs={{0,1},{1,0},{2,3},{3,2},{4,5},{5,4},{6,7},{7,6},{8,9},{9,8},{10,11... | collective-permute-start | bytes 786440 | tf_op jit(solution)/shard_map/ppermute | solution.py:313
  19.9 5.8 %collective-permute-start.2 = (bf16[8,16,256]{2,1,0:T(8,128)(2,1)S(1)}, bf16[8,16,256]{2,1,0:T(8,128)(2,1)S(1)}, u32[]{:S(2)}, u32[]{:S(2)}) collective-permute-start(bf16[8,16,256]{2,1,0:T(8,128)(2,1)S(1)} %copy-done), channel_id=1, source_target_pairs={{0,24},{8,16},{16,8},{24,0},{1,25},{9,17},{17,9},{25,1},{2,26},{10... | collective-permute-start | bytes 196616 | tf_op jit(solution)/shard_map/ppermute | solution.py:302
  20.7 5.2 %collective-permute-start.1 = (bf16[8,16,256]{2,1,0:T(8,128)(2,1)S(1)}, bf16[8,16,256]{2,1,0:T(8,128)(2,1)S(1)}, u32[]{:S(2)}, u32[]{:S(2)}) collective-permute-start(bf16[8,16,256]{2,1,0:T(8,128)(2,1)S(1)} %copy-done), channel_id=1, source_target_pairs={{0,16},{8,24},{16,0},{24,8},{1,17},{9,25},{17,1},{25,9},{2,18},{10... | collective-permute-start | bytes 196616 | tf_op jit(solution)/shard_map/ppermute | solution.py:302
  22.2 4.3 %collective-permute-start = (bf16[8,16,256]{2,1,0:T(8,128)(2,1)S(1)}, bf16[8,16,256]{2,1,0:T(8,128)(2,1)S(1)}, u32[]{:S(2)}, u32[]{:S(2)}) collective-permute-start(bf16[8,16,256]{2,1,0:T(8,128)(2,1)S(1)} %copy-done), channel_id=1, source_target_pairs={{0,8},{8,0},{16,24},{24,16},{1,9},{9,1},{17,25},{25,17},{2,10},{10... | collective-permute-start | bytes 196616 | tf_op jit(solution)/shard_map/ppermute | solution.py:302
  27.3 7.4 %copy-start.4 = (bf16[128,256]{1,0:T(8,128)(2,1)S(1)}, bf16[128,256]{1,0:T(8,128)(2,1)}, u32[]{:S(2)}) copy-start(bf16[128,256]{1,0:T(8,128)(2,1)} %refs_8_.1) | copy-start | bytes 196612
  27.3 7.4 %copy-start.5 = (bf16[256,128]{1,0:T(8,128)(2,1)S(1)}, bf16[256,128]{1,0:T(8,128)(2,1)}, u32[]{:S(2)}) copy-start(bf16[256,128]{1,0:T(8,128)(2,1)} %refs_9_.1) | copy-start | bytes 196612
  27.3 7.4 %copy-start.6 = (bf16[256,128]{1,0:T(8,128)(2,1)S(1)}, bf16[256,128]{1,0:T(8,128)(2,1)}, u32[]{:S(2)}) copy-start(bf16[256,128]{1,0:T(8,128)(2,1)} %refs_10_.1) | copy-start | bytes 196612
  27.3 7.4 %copy-start.7 = (bf16[256,128]{1,0:T(8,128)(2,1)S(1)}, bf16[256,128]{1,0:T(8,128)(2,1)}, u32[]{:S(2)}) copy-start(bf16[256,128]{1,0:T(8,128)(2,1)} %refs_11_.1) | copy-start | bytes 196612
  27.3 7.4 %copy-start.8 = (bf16[128,256]{1,0:T(8,128)(2,1)S(1)}, bf16[128,256]{1,0:T(8,128)(2,1)}, u32[]{:S(2)}) copy-start(bf16[128,256]{1,0:T(8,128)(2,1)} %refs_12_.1) | copy-start | bytes 196612
  28.0 4.9 %collective-permute-start.6 = (bf16[8,16,128]{2,1,0:T(8,128)(2,1)S(1)}, bf16[8,16,128]{2,1,0:T(8,128)(2,1)S(1)}, u32[]{:S(2)}, u32[]{:S(2)}) collective-permute-start(bf16[8,16,128]{2,1,0:T(8,128)(2,1)S(1)} %attend.1.refs_4_), channel_id=1, source_target_pairs={{0,24},{8,16},{16,8},{24,0},{1,25},{9,17},{17,9},{25,1},{2,26},{10... | collective-permute-start | bytes 98312 | tf_op jit(solution)/shard_map/ppermute | solution.py:335
  29.5 3.9 %collective-permute-start.5 = (bf16[8,16,128]{2,1,0:T(8,128)(2,1)S(1)}, bf16[8,16,128]{2,1,0:T(8,128)(2,1)S(1)}, u32[]{:S(2)}, u32[]{:S(2)}) collective-permute-start(bf16[8,16,128]{2,1,0:T(8,128)(2,1)S(1)} %attend.1.refs_4_), channel_id=1, source_target_pairs={{0,16},{8,24},{16,0},{24,8},{1,17},{9,25},{17,1},{25,9},{2,18},{10... | collective-permute-start | bytes 98312 | tf_op jit(solution)/shard_map/ppermute | solution.py:335
  30.7 3.9 %collective-permute-start.4 = (bf16[8,16,128]{2,1,0:T(8,128)(2,1)S(1)}, bf16[8,16,128]{2,1,0:T(8,128)(2,1)S(1)}, u32[]{:S(2)}, u32[]{:S(2)}) collective-permute-start(bf16[8,16,128]{2,1,0:T(8,128)(2,1)S(1)} %attend.1.refs_4_), channel_id=1, source_target_pairs={{0,8},{8,0},{16,24},{24,16},{1,9},{9,1},{17,25},{25,17},{2,10},{10... | collective-permute-start | bytes 98312 | tf_op jit(solution)/shard_map/ppermute | solution.py:335

commit v9 on v8

--- a/solution.py
+++ b/solution.py
@@ -184,14 +184,24 @@
             query_ref[part, own ^ place] = queries[start : start + col_dev]
 
 
-def attend_kernel(scale, mine_ref, other_ref, query_ref, out_ref):
+def half_logits(ref, query_ref, part):
+    seq, col, _, col_dev, lanes = ref.shape
+    logits = jnp.zeros((col_dev, col * col_dev), jnp.float32)
+    for source in range(seq):
+        keys = ref[source, :, 0].reshape(col * col_dev, lanes)
+        logits += contract_last(query_ref[part, source], keys)
+    return logits
+
+
+def half_kernel(mine_ref, query_ref, logits_ref):
+    half = lax.rem(lax.axis_index("col"), 2)
+    logits_ref[...] = half_logits(mine_ref, query_ref, half)
+
+
+def attend_kernel(scale, mine_ref, other_ref, query_ref, logits_ref, out_ref):
     half = lax.rem(lax.axis_index("col"), 2)
     seq, col, _, col_dev, lanes = mine_ref.shape
-    logits = jnp.zeros((col_dev, col * col_dev), jnp.float32)
-    for ref, part in ((mine_ref, half), (other_ref, 1 - half)):
-        for source in range(seq):
-            keys = ref[source, :, 0].reshape(col * col_dev, lanes)
-            logits += contract_last(query_ref[part, source], keys)
+    logits = logits_ref[...] + half_logits(other_ref, query_ref, 1 - half)
     logits = logits * scale
     weights = jnp.exp(logits - jnp.max(logits, axis=-1, keepdims=True))
     probs = (weights / jnp.sum(weights, axis=-1, keepdims=True)).astype(jnp.bfloat16)
@@ -202,10 +212,10 @@
 
 
 def finish_kernel(*refs):
-    tail = refs[-7:]
-    refs, (row_output_ref, query_ref, key_ref, value_ref, output_ref) = refs[:-12], refs[-12:-7]
+    tail = refs[-3:]
+    refs, (row_output_ref, query_ref, key_ref, value_ref, output_ref) = refs[:-8], refs[-8:-3]
     fields, parts = refs[: len(refs) // 2], refs[len(refs) // 2 :]
-    update_ref, layer_ref, middles, queries, keys, values, contexts = tail
+    update_ref, layer_ref, middles = tail
     own = lax.axis_index("seq")
     seq = len(parts)
     _, col_dev, lanes = parts[0].shape
@@ -220,54 +230,51 @@
     rows = seq_dev * col_dev
     seqs = seq * seq_dev
     pair = jnp.concatenate([key_ref[...], value_ref[...]], axis=1)
+    context = []
+    for place in range(seq):
+        for half in range(seq_dev // HEADS):
+            tile = half * seq + (own ^ place)
+            context += swap_groups(
+                [part_ref[tile].astype(jnp.float32) for part_ref in parts], HEAD_DIM
+            )
+    context = jnp.concatenate(context, axis=0).astype(jnp.bfloat16)
+    update = project(context, row_output)
+    update_ref[...] = update[:rows].astype(jnp.bfloat16).reshape(update_ref.shape)
     for place, field_ref in enumerate(fields):
-        source = own ^ place
-        context = []
-        for half in range(seq_dev // HEADS):
-            heads = [part_ref[half * seq + source].astype(jnp.float32) for part_ref in parts]
-            context += swap_groups(heads, HEAD_DIM)
-        context = jnp.concatenate(context, axis=0).astype(jnp.bfloat16)
-        update = project(context, row_output)
-        middle = field_ref[...].reshape(rows, width).astype(jnp.float32) + update
-        normal = norm_rows(middle)
         here = slice(place * rows, (place + 1) * rows)
-        both = project(normal, pair)
-        keys[here, :] = both[:, :lanes]
-        values[here, :] = both[:, lanes:]
-        if place == 0:
-            update_ref[...] = update.astype(jnp.bfloat16).reshape(update_ref.shape)
-            middles[...] = middle
-            queries[...] = project(normal, query_ref[...]) * float(HEAD_DIM) ** (-0.5)
-    group = lanes // seqs
-    head_of = lax.broadcasted_iota(jnp.int32, (seq_dev, lanes), 1) // HEAD_DIM
-    size = group * seqs
-    row_column = lax.broadcasted_iota(jnp.int32, (group * HEADS * seq_dev, size), 0) // (
-        HEADS * seq_dev
-    )
-    same = row_column == lax.broadcasted_iota(jnp.int32, row_column.shape, 1) // seqs
-    ones = jnp.ones((size, lanes), jnp.bfloat16)
-    for first in range(0, col_dev, group):
-        query, key, value = [], [], []
-        for column in range(first, first + group):
-            row = queries[pl.ds(column, seq_dev, stride=col_dev), :]
-            query += [jnp.where(head_of == head, row, 0.0) for head in range(HEADS)]
-            key.append(keys[pl.ds(column, seqs, stride=col_dev), :])
-            value.append(values[pl.ds(column, seqs, stride=col_dev), :])
-        query, key, value = (
-            jnp.concatenate(part, axis=0).astype(jnp.bfloat16) for part in (query, key, value)
-        )
-        scores = jnp.where(same, contract_last(query, key), -jnp.inf)
-        weights = jnp.exp(scores - jnp.max(scores, axis=-1, keepdims=True))
-        both = project(weights.astype(jnp.bfloat16), jnp.concatenate([value, ones], axis=1))
-        for place in range(group):
-            above = jnp.zeros((seq_dev, lanes), jnp.float32)
-            below = jnp.ones((seq_dev, lanes), jnp.float32)
-            for head in range(HEADS):
-                at = (place * HEADS + head) * seq_dev
-                above = jnp.where(head_of == head, both[at : at + seq_dev, :lanes], above)
-                below = jnp.where(head_of == head, both[at : at + seq_dev, lanes:], below)
-            contexts[pl.ds(first + place, seq_dev, stride=col_dev), :] = above / below
-    layer = middles[...] + project(contexts[...].astype(jnp.bfloat16), output_ref[...])
+        field = field_ref[...].reshape(rows, width).astype(jnp.float32)
+        middles[here, :] = field + update[here]
+    normal = norm_rows(middles[...])
+    step = 8
+    both = project(normal, pair).reshape(seqs, col_dev, 2 * lanes)
+    queries = project(normal[:rows], query_ref[...]) * float(HEAD_DIM) ** (-0.5)
+    queries = queries.reshape(seq_dev, col_dev, lanes)
+    size = HEADS * seq_dev * step
+    head_of = lax.broadcasted_iota(jnp.int32, (seq_dev * step, lanes), 1) // HEAD_DIM
+    same = (
+        lax.broadcasted_iota(jnp.int32, (size, seqs * step), 0) % step
+        == lax.broadcasted_iota(jnp.int32, (size, seqs * step), 1) % step
+    )
+    ones = jnp.ones((seqs * step, lanes), jnp.bfloat16)
+    contexts = []
+    for first in range(0, col_dev, step):
+        row = queries[:, first : first + step].reshape(seq_dev * step, lanes)
+        query = jnp.concatenate(
+            [jnp.where(head_of == head, row, 0.0) for head in range(HEADS)], axis=0
+        ).astype(jnp.bfloat16)
+        part = both[:, first : first + step].reshape(seqs * step, 2 * lanes).astype(jnp.bfloat16)
+        scores = jnp.where(same, contract_last(query, part[:, :lanes]), -jnp.inf)
+        weights = jnp.exp(scores - jnp.max(scores, axis=-1, keepdims=True)).astype(jnp.bfloat16)
+        sums = project(weights, jnp.concatenate([part[:, lanes:], ones], axis=1))
+        above = sums[: seq_dev * step, :lanes]
+        below = sums[: seq_dev * step, lanes:]
+        for head in range(1, HEADS):
+            here = slice(head * seq_dev * step, (head + 1) * seq_dev * step)
+            above = jnp.where(head_of == head, sums[here, :lanes], above)
+            below = jnp.where(head_of == head, sums[here, lanes:], below)
+        contexts.append((above / below).reshape(seq_dev, step, lanes))
+    context = jnp.concatenate(contexts, axis=1).reshape(rows, lanes).astype(jnp.bfloat16)
+    layer = middles[:rows, :] + project(context, output_ref[...])
     layer_ref[...] = layer.astype(jnp.bfloat16).reshape(layer_ref.shape)
 
 
@@ -322,19 +329,26 @@
         compiler_params=grant,
         name="query",
     )(*fields, row_query)
+    logits = pl.pallas_call(
+        half_kernel,
+        out_shape=jax.ShapeDtypeStruct((col_dev, col * col_dev), f32),
+        in_specs=[vmem] * 2,
+        out_specs=vmem,
+        compiler_params=grant,
+        name="half",
+    )(mine, queries)
     parts = pl.pallas_call(
         functools.partial(attend_kernel, scale),
         out_shape=jax.ShapeDtypeStruct((halves * seq, col_dev, inner), bf16),
-        in_specs=[vmem] * 3,
+        in_specs=[vmem] * 4,
         out_specs=vmem,
         compiler_params=grant,
         name="attend",
-    )(mine, other, queries)
+    )(mine, other, queries, logits)
     parts = [parts] * seq
     for place in range(seq - 1, 0, -1):
         parts[place] = lax.ppermute(parts[place], "seq", [(i, i ^ place) for i in range(seq)])
     total = seq * seq_dev * col_dev
-    local = seq_dev * col_dev
     like = jax.ShapeDtypeStruct(alignment.shape, bf16)
     return pl.pallas_call(
         finish_kernel,
@@ -342,11 +356,7 @@
         in_specs=[vmem] * (2 * seq + 5),
         out_specs=(vmem, vmem),
         scratch_shapes=[
-            pltpu.VMEM((local, width), f32),
-            pltpu.VMEM((local, inner), f32),
-            pltpu.VMEM((total, inner), f32),
-            pltpu.VMEM((total, inner), f32),
-            pltpu.VMEM((local, inner), f32),
+            pltpu.VMEM((total, width), f32),
         ],
         compiler_params=grant,
         name="finish",

time: 37.3 us -> 36.9 us (0.989)
  Pallas kernels: 4.34 us -> 3.95 us
    pallas_call x1, Pallas kernels: 2.39 us -> 2.01 us  [by_head(): pl.pallas_call(finish_kernel, out_shape=(like, like), in_specs=[vmem] * (...]
  transfers between devices with their start and end apart: 7 -> 7, of which waited for: 6 -> 6; matrix products, arithmetic and copies ran while one was open for 0% -> 0% of each run, Pallas kernels for 2% -> 3%
where the time goes in v9:
time: 36.9 us; the launch traced here: 36.7 us
  blocking collectives  17.1 us (46%)
  starting transfers between devices  7.77 us (21%)
  waiting for transfers between devices  6.15 us (17%)
  Pallas kernels  3.95 us (11%)
  local copies, waits for them, and re-layouts  0.92 us (2%)
  between operations  0.74 us (2%)
    all_to_all x1, blocking collectives, by_head(): lax.all_to_all(blocks.reshape(seq * col, 2, col_dev, inner), ('seq', 'col...  17.1 us
    ppermute x3, starting transfers between devices, by_head(): lax.ppermute(parts[place], 'seq', [(i, i ^ place) for i in range(seq)])  3.53 us
    ppermute x3, starting transfers between devices, by_head(): lax.ppermute(alignment, 'seq', [(i, i ^ place) for i in range(seq)])  3.49 us
    ppermute x3, waiting for transfers between devices, by_head(): lax.ppermute(parts[place], 'seq', [(i, i ^ place) for i in range(seq)])  3.08 us
    ppermute x3, waiting for transfers between devices, by_head(): lax.ppermute(alignment, 'seq', [(i, i ^ place) for i in range(seq)])  3.06 us
    pallas_call x1, Pallas kernels, by_head(): pl.pallas_call(finish_kernel, out_shape=(like, like), in_specs=[vmem] * (...  2.01 us
    unnamed x18, local copies, waits for them, and re-layouts  0.92 us
    pallas_call x1, Pallas kernels, by_head(): pl.pallas_call(query_kernel, out_shape=jax.ShapeDtypeStruct((halves, seq,...  0.79 us
  transfers between devices with their start and end apart: 7, of which 6 were waited for; matrix products, arithmetic and copies ran while one was open for 0% of the time, Pallas kernels for 3%

profile of v9, /device:TPU:0, one launch (start us, length us, event | category | flops | bytes accessed | tf_op | source)
XLA Modules:
  0.0 36.7 jit_solution(5461829275824682319)
XLA Ops:
  0.6 0.0 copy-start
  0.6 0.0 copy-start.2
  0.6 0.0 copy-start.1
  0.7 0.8 %copy-done = bf16[8,16,256]{2,1,0:T(8,128)(2,1)S(1)} copy-done((bf16[8,16,256]{2,1,0:T(8,128)(2,1)S(1)}, bf16[8,16,256]{2,1,0:T(8,128)(2,1)}, u32[]{:S(2)}) %copy-start) | copy-done | bytes 65560
  1.5 0.0 copy-done.2
  1.5 0.0 copy-done.1
  1.5 0.5 %project.1 = bf16[4,4,2,2,16,128]{5,4,3,2,1,0:T(8,128)(2,1)S(1)} custom-call(bf16[8,16,256]{2,1,0:T(8,128)(2,1)S(1)} %copy-done, bf16[256,128]{1,0:T(8,128)(2,1)S(1)} %copy-done.1, bf16[256,128]{1,0:T(8,128)(2,1)S(1)} %copy-done.2, f32[8,128]{1,0:T(8,128)S(1)} %gate.1.gate_ref), custom_call_target="tpu_custom_call" | custom-call | tf_op jit(solution)/shard_map/project/pallas_call | solution.py:311
  2.0 0.0 copy-start.3
  2.0 17.1 %all_to_all.5 = bf16[32,2,16,128]{3,2,1,0:T(8,128)(2,1)S(1)} all-to-all(bf16[32,2,16,128]{3,2,1,0:T(8,128)(2,1)S(1)} %bitcast.5), channel_id=1, replica_groups=mesh['seq'=4,'col'=8] {'seq','col'}, dimensions={0} | all-to-all | bytes 524288 | tf_op jit(solution)/shard_map/all_to_all | solution.py:319
  19.2 0.7 %collective-permute-start.3 = (bf16[32,2,16,128]{3,2,1,0:T(8,128)(2,1)S(1)}, bf16[32,2,16,128]{3,2,1,0:T(8,128)(2,1)S(1)}, u32[]{:S(2)}, u32[]{:S(2)}) collective-permute-start(bf16[32,2,16,128]{3,2,1,0:T(8,128)(2,1)S(1)} %all_to_all.5), channel_id=1, source_target_pairs={{0,1},{1,0},{2,3},{3,2},{4,5},{5,4},{6,7},{7,6},{8,9},{9,8},{10,11... | collective-permute-start | bytes 786440 | tf_op jit(solution)/shard_map/ppermute | solution.py:320
  19.9 0.8 %collective-permute-start.2 = (bf16[8,16,256]{2,1,0:T(8,128)(2,1)S(1)}, bf16[8,16,256]{2,1,0:T(8,128)(2,1)S(1)}, u32[]{:S(2)}, u32[]{:S(2)}) collective-permute-start(bf16[8,16,256]{2,1,0:T(8,128)(2,1)S(1)} %copy-done), channel_id=1, source_target_pairs={{0,24},{8,16},{16,8},{24,0},{1,25},{9,17},{17,9},{25,1},{2,26},{10... | collective-permute-start | bytes 196616 | tf_op jit(solution)/shard_map/ppermute | solution.py:309
  20.7 1.5 %collective-permute-start.1 = (bf16[8,16,256]{2,1,0:T(8,128)(2,1)S(1)}, bf16[8,16,256]{2,1,0:T(8,128)(2,1)S(1)}, u32[]{:S(2)}, u32[]{:S(2)}) collective-permute-start(bf16[8,16,256]{2,1,0:T(8,128)(2,1)S(1)} %copy-done), channel_id=1, source_target_pairs={{0,16},{8,24},{16,0},{24,8},{1,17},{9,25},{17,1},{25,9},{2,18},{10... | collective-permute-start | bytes 196616 | tf_op jit(solution)/shard_map/ppermute | solution.py:309
  22.2 1.2 %collective-permute-start = (bf16[8,16,256]{2,1,0:T(8,128)(2,1)S(1)}, bf16[8,16,256]{2,1,0:T(8,128)(2,1)S(1)}, u32[]{:S(2)}, u32[]{:S(2)}) collective-permute-start(bf16[8,16,256]{2,1,0:T(8,128)(2,1)S(1)} %copy-done), channel_id=1, source_target_pairs={{0,8},{8,0},{16,24},{24,16},{1,9},{9,1},{17,25},{25,17},{2,10},{10... | collective-permute-start | bytes 196616 | tf_op jit(solution)/shard_map/ppermute | solution.py:309
  23.4 2.3 %collective-permute-done.2.refs_3_ = bf16[8,16,256]{2,1,0:T(8,128)(2,1)S(1)} collective-permute-done((bf16[8,16,256]{2,1,0:T(8,128)(2,1)S(1)}, bf16[8,16,256]{2,1,0:T(8,128)(2,1)S(1)}, u32[]{:S(2)}, u32[]{:S(2)}) %collective-permute-start.2) | collective-permute-done | bytes 65568 | tf_op jit(solution)/shard_map/ppermute | solution.py:309
  25.7 0.2 collective-permute-done.1.refs_2_
  25.9 0.5 %collective-permute-done.refs_1_ = bf16[8,16,256]{2,1,0:T(8,128)(2,1)S(1)} collective-permute-done((bf16[8,16,256]{2,1,0:T(8,128)(2,1)S(1)}, bf16[8,16,256]{2,1,0:T(8,128)(2,1)S(1)}, u32[]{:S(2)}, u32[]{:S(2)}) %collective-permute-start) | collective-permute-done | bytes 65568 | tf_op jit(solution)/shard_map/ppermute | solution.py:309
  26.5 0.0 copy-done.3
  26.5 0.8 %query.1.query_ref = bf16[2,4,16,128]{3,2,1,0:T(8,128)(2,1)S(1)} custom-call(bf16[8,16,256]{2,1,0:T(8,128)(2,1)S(1)} %copy-done, bf16[8,16,256]{2,1,0:T(8,128)(2,1)S(1)} %collective-permute-done.refs_1_, bf16[8,16,256]{2,1,0:T(8,128)(2,1)S(1)} %collective-permute-done.1.refs_2_, bf16[8,16,256]{2,1,0:T(8,128)(2,1)S(1)} %collective-permute-done.2.refs_3_, ...), custom_call_target="tpu_custom_call" | custom-call | tf_op jit(solution)/shard_map/query/pallas_call | solution.py:324
  27.3 0.2 half.1.logits_ref
  27.4 0.0 collective-permute-done.3
  27.4 0.0 copy-start.4
  27.4 0.0 copy-start.5
  27.5 0.0 copy-start.6
  27.5 0.0 copy-start.7
  27.5 0.0 copy-start.8
  27.5 0.5 %attend.1.refs_4_ = bf16[8,16,128]{2,1,0:T(8,128)(2,1)S(1)} custom-call(bf16[4,8,2,16,128]{4,3,2,1,0:T(8,128)(2,1)S(1)} %bitcast.4, bf16[4,8,2,16,128]{4,3,2,1,0:T(8,128)(2,1)S(1)} %bitcast.6, bf16[2,4,16,128]{3,2,1,0:T(8,128)(2,1)S(1)} %query.1.query_ref, f32[16,128]{1,0:T(8,128)S(1)} %half.1.logits_ref), custom_call_target="tpu_custom_call" | custom-call | tf_op jit(solution)/shard_map/attend/pallas_call | solution.py:340
  28.0 1.5 %collective-permute-start.6 = (bf16[8,16,128]{2,1,0:T(8,128)(2,1)S(1)}, bf16[8,16,128]{2,1,0:T(8,128)(2,1)S(1)}, u32[]{:S(2)}, u32[]{:S(2)}) collective-permute-start(bf16[8,16,128]{2,1,0:T(8,128)(2,1)S(1)} %attend.1.refs_4_), channel_id=1, source_target_pairs={{0,24},{8,16},{16,8},{24,0},{1,25},{9,17},{17,9},{25,1},{2,26},{10... | collective-permute-start | bytes 98312 | tf_op jit(solution)/shard_map/ppermute | solution.py:350
  29.5 1.2 %collective-permute-start.5 = (bf16[8,16,128]{2,1,0:T(8,128)(2,1)S(1)}, bf16[8,16,128]{2,1,0:T(8,128)(2,1)S(1)}, u32[]{:S(2)}, u32[]{:S(2)}) collective-permute-start(bf16[8,16,128]{2,1,0:T(8,128)(2,1)S(1)} %attend.1.refs_4_), channel_id=1, source_target_pairs={{0,16},{8,24},{16,0},{24,8},{1,17},{9,25},{17,1},{25,9},{2,18},{10... | collective-permute-start | bytes 98312 | tf_op jit(solution)/shard_map/ppermute | solution.py:350
  30.7 0.8 %collective-permute-start.4 = (bf16[8,16,128]{2,1,0:T(8,128)(2,1)S(1)}, bf16[8,16,128]{2,1,0:T(8,128)(2,1)S(1)}, u32[]{:S(2)}, u32[]{:S(2)}) collective-permute-start(bf16[8,16,128]{2,1,0:T(8,128)(2,1)S(1)} %attend.1.refs_4_), channel_id=1, source_target_pairs={{0,8},{8,0},{16,24},{24,16},{1,9},{9,1},{17,25},{25,17},{2,10},{10... | collective-permute-start | bytes 98312 | tf_op jit(solution)/shard_map/ppermute | solution.py:350
  31.5 1.3 %collective-permute-done.6.refs_7_ = bf16[8,16,128]{2,1,0:T(8,128)(2,1)S(1)} collective-permute-done((bf16[8,16,128]{2,1,0:T(8,128)(2,1)S(1)}, bf16[8,16,128]{2,1,0:T(8,128)(2,1)S(1)}, u32[]{:S(2)}, u32[]{:S(2)}) %collective-permute-start.6) | collective-permute-done | bytes 32800 | tf_op jit(solution)/shard_map/ppermute | solution.py:350
  32.9 0.6 %collective-permute-done.5.refs_6_ = bf16[8,16,128]{2,1,0:T(8,128)(2,1)S(1)} collective-permute-done((bf16[8,16,128]{2,1,0:T(8,128)(2,1)S(1)}, bf16[8,16,128]{2,1,0:T(8,128)(2,1)S(1)}, u32[]{:S(2)}, u32[]{:S(2)}) %collective-permute-start.5) | collective-permute-done | bytes 32800 | tf_op jit(solution)/shard_map/ppermute | solution.py:350
  33.4 1.2 %collective-permute-done.4.refs_5_ = bf16[8,16,128]{2,1,0:T(8,128)(2,1)S(1)} collective-permute-done((bf16[8,16,128]{2,1,0:T(8,128)(2,1)S(1)}, bf16[8,16,128]{2,1,0:T(8,128)(2,1)S(1)}, u32[]{:S(2)}, u32[]{:S(2)}) %collective-permute-start.4) | collective-permute-done | bytes 32800 | tf_op jit(solution)/shard_map/ppermute | solution.py:350
  34.6 0.0 copy-done.4
  34.6 0.0 copy-done.5
  34.6 0.0 copy-done.6
  34.6 0.0 copy-done.7
  34.6 0.0 copy-done.8
  34.6 2.0 %finish.1 = (bf16[8,16,256]{2,1,0:T(8,128)(2,1)}, bf16[8,16,256]{2,1,0:T(8,128)(2,1)}) custom-call(bf16[8,16,256]{2,1,0:T(8,128)(2,1)S(1)} %copy-done, bf16[8,16,256]{2,1,0:T(8,128)(2,1)S(1)} %collective-permute-done.refs_1_, bf16[8,16,256]{2,1,0:T(8,128)(2,1)S(1)} %collective-permute-done.1.refs_2_, bf16[8,16,256]{2,1,0:T(8,128)(2,1)S(1)} %collective-permute-done.2.refs_3_, ...), custom_call_target="tpu_custom_call" | custom-call | tf_op jit(solution)/shard_map/finish/pallas_call | solution.py:353
  (1 shorter events, 0.0 us)
Async XLA Ops:
  0.6 0.8 %copy-start = (bf16[8,16,256]{2,1,0:T(8,128)(2,1)S(1)}, bf16[8,16,256]{2,1,0:T(8,128)(2,1)}, u32[]{:S(2)}) copy-start(bf16[8,16,256]{2,1,0:T(8,128)(2,1)} %refs_0_.3) | copy-start | bytes 196612
  0.6 0.9 %copy-start.2 = (bf16[256,128]{1,0:T(8,128)(2,1)S(1)}, bf16[256,128]{1,0:T(8,128)(2,1)}, u32[]{:S(2)}) copy-start(bf16[256,128]{1,0:T(8,128)(2,1)} %value_ref.1) | copy-start | bytes 196612
  0.6 0.9 %copy-start.1 = (bf16[256,128]{1,0:T(8,128)(2,1)S(1)}, bf16[256,128]{1,0:T(8,128)(2,1)}, u32[]{:S(2)}) copy-start(bf16[256,128]{1,0:T(8,128)(2,1)} %key_ref.1) | copy-start | bytes 196612
  2.0 24.4 %copy-start.3 = (bf16[256,128]{1,0:T(8,128)(2,1)S(1)}, bf16[256,128]{1,0:T(8,128)(2,1)}, u32[]{:S(2)}) copy-start(bf16[256,128]{1,0:T(8,128)(2,1)} %refs_4_.1) | copy-start | bytes 196612
  19.2 8.3 %collective-permute-start.3 = (bf16[32,2,16,128]{3,2,1,0:T(8,128)(2,1)S(1)}, bf16[32,2,16,128]{3,2,1,0:T(8,128)(2,1)S(1)}, u32[]{:S(2)}, u32[]{:S(2)}) collective-permute-start(bf16[32,2,16,128]{3,2,1,0:T(8,128)(2,1)S(1)} %all_to_all.5), channel_id=1, source_target_pairs={{0,1},{1,0},{2,3},{3,2},{4,5},{5,4},{6,7},{7,6},{8,9},{9,8},{10,11... | collective-permute-start | bytes 786440 | tf_op jit(solution)/shard_map/ppermute | solution.py:320
  19.9 5.8 %collective-permute-start.2 = (bf16[8,16,256]{2,1,0:T(8,128)(2,1)S(1)}, bf16[8,16,256]{2,1,0:T(8,128)(2,1)S(1)}, u32[]{:S(2)}, u32[]{:S(2)}) collective-permute-start(bf16[8,16,256]{2,1,0:T(8,128)(2,1)S(1)} %copy-done), channel_id=1, source_target_pairs={{0,24},{8,16},{16,8},{24,0},{1,25},{9,17},{17,9},{25,1},{2,26},{10... | collective-permute-start | bytes 196616 | tf_op jit(solution)/shard_map/ppermute | solution.py:309
  20.7 5.2 %collective-permute-start.1 = (bf16[8,16,256]{2,1,0:T(8,128)(2,1)S(1)}, bf16[8,16,256]{2,1,0:T(8,128)(2,1)S(1)}, u32[]{:S(2)}, u32[]{:S(2)}) collective-permute-start(bf16[8,16,256]{2,1,0:T(8,128)(2,1)S(1)} %copy-done), channel_id=1, source_target_pairs={{0,16},{8,24},{16,0},{24,8},{1,17},{9,25},{17,1},{25,9},{2,18},{10... | collective-permute-start | bytes 196616 | tf_op jit(solution)/shard_map/ppermute | solution.py:309
  22.2 4.3 %collective-permute-start = (bf16[8,16,256]{2,1,0:T(8,128)(2,1)S(1)}, bf16[8,16,256]{2,1,0:T(8,128)(2,1)S(1)}, u32[]{:S(2)}, u32[]{:S(2)}) collective-permute-start(bf16[8,16,256]{2,1,0:T(8,128)(2,1)S(1)} %copy-done), channel_id=1, source_target_pairs={{0,8},{8,0},{16,24},{24,16},{1,9},{9,1},{17,25},{25,17},{2,10},{10... | collective-permute-start | bytes 196616 | tf_op jit(solution)/shard_map/ppermute | solution.py:309
  27.4 7.2 %copy-start.4 = (bf16[128,256]{1,0:T(8,128)(2,1)S(1)}, bf16[128,256]{1,0:T(8,128)(2,1)}, u32[]{:S(2)}) copy-start(bf16[128,256]{1,0:T(8,128)(2,1)} %refs_8_.1) | copy-start | bytes 196612
  27.4 7.2 %copy-start.5 = (bf16[256,128]{1,0:T(8,128)(2,1)S(1)}, bf16[256,128]{1,0:T(8,128)(2,1)}, u32[]{:S(2)}) copy-start(bf16[256,128]{1,0:T(8,128)(2,1)} %refs_9_.1) | copy-start | bytes 196612
  27.5 7.2 %copy-start.6 = (bf16[256,128]{1,0:T(8,128)(2,1)S(1)}, bf16[256,128]{1,0:T(8,128)(2,1)}, u32[]{:S(2)}) copy-start(bf16[256,128]{1,0:T(8,128)(2,1)} %refs_10_.1) | copy-start | bytes 196612
  27.5 7.2 %copy-start.7 = (bf16[256,128]{1,0:T(8,128)(2,1)S(1)}, bf16[256,128]{1,0:T(8,128)(2,1)}, u32[]{:S(2)}) copy-start(bf16[256,128]{1,0:T(8,128)(2,1)} %refs_11_.1) | copy-start | bytes 196612
  27.5 7.2 %copy-start.8 = (bf16[128,256]{1,0:T(8,128)(2,1)S(1)}, bf16[128,256]{1,0:T(8,128)(2,1)}, u32[]{:S(2)}) copy-start(bf16[128,256]{1,0:T(8,128)(2,1)} %refs_12_.1) | copy-start | bytes 196612
  28.0 4.9 %collective-permute-start.6 = (bf16[8,16,128]{2,1,0:T(8,128)(2,1)S(1)}, bf16[8,16,128]{2,1,0:T(8,128)(2,1)S(1)}, u32[]{:S(2)}, u32[]{:S(2)}) collective-permute-start(bf16[8,16,128]{2,1,0:T(8,128)(2,1)S(1)} %attend.1.refs_4_), channel_id=1, source_target_pairs={{0,24},{8,16},{16,8},{24,0},{1,25},{9,17},{17,9},{25,1},{2,26},{10... | collective-permute-start | bytes 98312 | tf_op jit(solution)/shard_map/ppermute | solution.py:350
  29.5 3.9 %collective-permute-start.5 = (bf16[8,16,128]{2,1,0:T(8,128)(2,1)S(1)}, bf16[8,16,128]{2,1,0:T(8,128)(2,1)S(1)}, u32[]{:S(2)}, u32[]{:S(2)}) collective-permute-start(bf16[8,16,128]{2,1,0:T(8,128)(2,1)S(1)} %attend.1.refs_4_), channel_id=1, source_target_pairs={{0,16},{8,24},{16,0},{24,8},{1,17},{9,25},{17,1},{25,9},{2,18},{10... | collective-permute-start | bytes 98312 | tf_op jit(solution)/shard_map/ppermute | solution.py:350
  30.7 3.9 %collective-permute-start.4 = (bf16[8,16,128]{2,1,0:T(8,128)(2,1)S(1)}, bf16[8,16,128]{2,1,0:T(8,128)(2,1)S(1)}, u32[]{:S(2)}, u32[]{:S(2)}) collective-permute-start(bf16[8,16,128]{2,1,0:T(8,128)(2,1)S(1)} %attend.1.refs_4_), channel_id=1, source_target_pairs={{0,8},{8,0},{16,24},{24,16},{1,9},{9,1},{17,25},{25,17},{2,10},{10... | collective-permute-start | bytes 98312 | tf_op jit(solution)/shard_map/ppermute | solution.py:350

commit v10 on v9

--- a/solution.py
+++ b/solution.py
@@ -187,9 +187,11 @@
 def half_logits(ref, query_ref, part):
     seq, col, _, col_dev, lanes = ref.shape
     logits = jnp.zeros((col_dev, col * col_dev), jnp.float32)
-    for source in range(seq):
-        keys = ref[source, :, 0].reshape(col * col_dev, lanes)
-        logits += contract_last(query_ref[part, source], keys)
+    for first in range(0, seq, 2):
+        both = range(first, first + 2)
+        keys = [ref[source, :, 0].reshape(col * col_dev, lanes) for source in both]
+        queries = [query_ref[part, source] for source in both]
+        logits += contract_last(jnp.concatenate(queries, axis=1), jnp.concatenate(keys, axis=1))
     return logits
 
 
@@ -204,11 +206,16 @@
     logits = logits_ref[...] + half_logits(other_ref, query_ref, 1 - half)
     logits = logits * scale
     weights = jnp.exp(logits - jnp.max(logits, axis=-1, keepdims=True))
-    probs = (weights / jnp.sum(weights, axis=-1, keepdims=True)).astype(jnp.bfloat16)
+    share = 1.0 / jnp.sum(weights, axis=-1, keepdims=True)
+    weights = weights.astype(jnp.bfloat16)
     for ref, part in ((mine_ref, half), (other_ref, 1 - half)):
-        for source in range(seq):
-            values = ref[source, :, 1].reshape(col * col_dev, lanes)
-            out_ref[part * seq + source] = project(probs, values).astype(jnp.bfloat16)
+        for first in range(0, seq, 2):
+            values = [
+                ref[source, :, 1].reshape(col * col_dev, lanes) for source in (first, first + 1)
+            ]
+            context = project(weights, jnp.concatenate(values, axis=1)) * share
+            out_ref[part * seq + first] = context[:, :lanes].astype(jnp.bfloat16)
+            out_ref[part * seq + first + 1] = context[:, lanes:].astype(jnp.bfloat16)
 
 
 def finish_kernel(*refs):

time: 36.9 us -> 36.7 us (level)
  no operation moved by 1% of the time
where the time goes in v10:
time: 36.7 us; the launch traced here: 36.5 us
  blocking collectives  17.1 us (47%)
  starting transfers between devices  7.78 us (21%)
  waiting for transfers between devices  6.15 us (17%)
  Pallas kernels  3.77 us (10%)
  local copies, waits for them, and re-layouts  0.92 us (3%)
  between operations  0.74 us (2%)
    all_to_all x1, blocking collectives, by_head(): lax.all_to_all(blocks.reshape(seq * col, 2, col_dev, inner), ('seq', 'col...  17.1 us
    ppermute x3, starting transfers between devices, by_head(): lax.ppermute(parts[place], 'seq', [(i, i ^ place) for i in range(seq)])  3.55 us
    ppermute x3, starting transfers between devices, by_head(): lax.ppermute(alignment, 'seq', [(i, i ^ place) for i in range(seq)])  3.49 us
    ppermute x3, waiting for transfers between devices, by_head(): lax.ppermute(parts[place], 'seq', [(i, i ^ place) for i in range(seq)])  3.08 us
    ppermute x3, waiting for transfers between devices, by_head(): lax.ppermute(alignment, 'seq', [(i, i ^ place) for i in range(seq)])  3.06 us
    pallas_call x1, Pallas kernels, by_head(): pl.pallas_call(finish_kernel, out_shape=(like, like), in_specs=[vmem] * (...  2.01 us
    unnamed x18, local copies, waits for them, and re-layouts  0.92 us
    pallas_call x1, Pallas kernels, by_head(): pl.pallas_call(query_kernel, out_shape=jax.ShapeDtypeStruct((halves, seq,...  0.79 us
  transfers between devices with their start and end apart: 7, of which 6 were waited for; matrix products, arithmetic and copies ran while one was open for 0% of the time, Pallas kernels for 3%

profile of v10, /device:TPU:0, one launch (start us, length us, event | category | flops | bytes accessed | tf_op | source)
XLA Modules:
  0.0 36.5 jit_solution(8430062707528867095)
XLA Ops:
  0.6 0.0 copy-start
  0.6 0.0 copy-start.2
  0.6 0.0 copy-start.1
  0.7 0.8 %copy-done = bf16[8,16,256]{2,1,0:T(8,128)(2,1)S(1)} copy-done((bf16[8,16,256]{2,1,0:T(8,128)(2,1)S(1)}, bf16[8,16,256]{2,1,0:T(8,128)(2,1)}, u32[]{:S(2)}) %copy-start) | copy-done | bytes 65560
  1.5 0.0 copy-done.2
  1.5 0.0 copy-done.1
  1.5 0.5 %project.1 = bf16[4,4,2,2,16,128]{5,4,3,2,1,0:T(8,128)(2,1)S(1)} custom-call(bf16[8,16,256]{2,1,0:T(8,128)(2,1)S(1)} %copy-done, bf16[256,128]{1,0:T(8,128)(2,1)S(1)} %copy-done.1, bf16[256,128]{1,0:T(8,128)(2,1)S(1)} %copy-done.2, f32[8,128]{1,0:T(8,128)S(1)} %gate.1.gate_ref), custom_call_target="tpu_custom_call" | custom-call | tf_op jit(solution)/shard_map/project/pallas_call | solution.py:318
  2.0 0.0 copy-start.3
  2.0 17.1 %all_to_all.5 = bf16[32,2,16,128]{3,2,1,0:T(8,128)(2,1)S(1)} all-to-all(bf16[32,2,16,128]{3,2,1,0:T(8,128)(2,1)S(1)} %bitcast.5), channel_id=1, replica_groups=mesh['seq'=4,'col'=8] {'seq','col'}, dimensions={0} | all-to-all | bytes 524288 | tf_op jit(solution)/shard_map/all_to_all | solution.py:326
  19.2 0.7 %collective-permute-start.3 = (bf16[32,2,16,128]{3,2,1,0:T(8,128)(2,1)S(1)}, bf16[32,2,16,128]{3,2,1,0:T(8,128)(2,1)S(1)}, u32[]{:S(2)}, u32[]{:S(2)}) collective-permute-start(bf16[32,2,16,128]{3,2,1,0:T(8,128)(2,1)S(1)} %all_to_all.5), channel_id=1, source_target_pairs={{0,1},{1,0},{2,3},{3,2},{4,5},{5,4},{6,7},{7,6},{8,9},{9,8},{10,11... | collective-permute-start | bytes 786440 | tf_op jit(solution)/shard_map/ppermute | solution.py:327
  19.9 0.8 %collective-permute-start.2 = (bf16[8,16,256]{2,1,0:T(8,128)(2,1)S(1)}, bf16[8,16,256]{2,1,0:T(8,128)(2,1)S(1)}, u32[]{:S(2)}, u32[]{:S(2)}) collective-permute-start(bf16[8,16,256]{2,1,0:T(8,128)(2,1)S(1)} %copy-done), channel_id=1, source_target_pairs={{0,24},{8,16},{16,8},{24,0},{1,25},{9,17},{17,9},{25,1},{2,26},{10... | collective-permute-start | bytes 196616 | tf_op jit(solution)/shard_map/ppermute | solution.py:316
  20.7 1.5 %collective-permute-start.1 = (bf16[8,16,256]{2,1,0:T(8,128)(2,1)S(1)}, bf16[8,16,256]{2,1,0:T(8,128)(2,1)S(1)}, u32[]{:S(2)}, u32[]{:S(2)}) collective-permute-start(bf16[8,16,256]{2,1,0:T(8,128)(2,1)S(1)} %copy-done), channel_id=1, source_target_pairs={{0,16},{8,24},{16,0},{24,8},{1,17},{9,25},{17,1},{25,9},{2,18},{10... | collective-permute-start | bytes 196616 | tf_op jit(solution)/shard_map/ppermute | solution.py:316
  22.2 1.2 %collective-permute-start = (bf16[8,16,256]{2,1,0:T(8,128)(2,1)S(1)}, bf16[8,16,256]{2,1,0:T(8,128)(2,1)S(1)}, u32[]{:S(2)}, u32[]{:S(2)}) collective-permute-start(bf16[8,16,256]{2,1,0:T(8,128)(2,1)S(1)} %copy-done), channel_id=1, source_target_pairs={{0,8},{8,0},{16,24},{24,16},{1,9},{9,1},{17,25},{25,17},{2,10},{10... | collective-permute-start | bytes 196616 | tf_op jit(solution)/shard_map/ppermute | solution.py:316
  23.4 2.3 %collective-permute-done.2.refs_3_ = bf16[8,16,256]{2,1,0:T(8,128)(2,1)S(1)} collective-permute-done((bf16[8,16,256]{2,1,0:T(8,128)(2,1)S(1)}, bf16[8,16,256]{2,1,0:T(8,128)(2,1)S(1)}, u32[]{:S(2)}, u32[]{:S(2)}) %collective-permute-start.2) | collective-permute-done | bytes 65568 | tf_op jit(solution)/shard_map/ppermute | solution.py:316
  25.7 0.2 collective-permute-done.1.refs_2_
  25.9 0.5 %collective-permute-done.refs_1_ = bf16[8,16,256]{2,1,0:T(8,128)(2,1)S(1)} collective-permute-done((bf16[8,16,256]{2,1,0:T(8,128)(2,1)S(1)}, bf16[8,16,256]{2,1,0:T(8,128)(2,1)S(1)}, u32[]{:S(2)}, u32[]{:S(2)}) %collective-permute-start) | collective-permute-done | bytes 65568 | tf_op jit(solution)/shard_map/ppermute | solution.py:316
  26.5 0.0 copy-done.3
  26.5 0.8 %query.1.query_ref = bf16[2,4,16,128]{3,2,1,0:T(8,128)(2,1)S(1)} custom-call(bf16[8,16,256]{2,1,0:T(8,128)(2,1)S(1)} %copy-done, bf16[8,16,256]{2,1,0:T(8,128)(2,1)S(1)} %collective-permute-done.refs_1_, bf16[8,16,256]{2,1,0:T(8,128)(2,1)S(1)} %collective-permute-done.1.refs_2_, bf16[8,16,256]{2,1,0:T(8,128)(2,1)S(1)} %collective-permute-done.2.refs_3_, ...), custom_call_target="tpu_custom_call" | custom-call | tf_op jit(solution)/shard_map/query/pallas_call | solution.py:331
  27.3 0.1 half.1.logits_ref
  27.4 0.0 collective-permute-done.3
  27.4 0.0 copy-start.4
  27.4 0.0 copy-start.5
  27.4 0.0 copy-start.6
  27.4 0.0 copy-start.7
  27.4 0.0 copy-start.8
  27.5 0.4 attend.1.refs_4_
  27.8 1.5 %collective-permute-start.6 = (bf16[8,16,128]{2,1,0:T(8,128)(2,1)S(1)}, bf16[8,16,128]{2,1,0:T(8,128)(2,1)S(1)}, u32[]{:S(2)}, u32[]{:S(2)}) collective-permute-start(bf16[8,16,128]{2,1,0:T(8,128)(2,1)S(1)} %attend.1.refs_4_), channel_id=1, source_target_pairs={{0,24},{8,16},{16,8},{24,0},{1,25},{9,17},{17,9},{25,1},{2,26},{10... | collective-permute-start | bytes 98312 | tf_op jit(solution)/shard_map/ppermute | solution.py:357
  29.3 1.2 %collective-permute-start.5 = (bf16[8,16,128]{2,1,0:T(8,128)(2,1)S(1)}, bf16[8,16,128]{2,1,0:T(8,128)(2,1)S(1)}, u32[]{:S(2)}, u32[]{:S(2)}) collective-permute-start(bf16[8,16,128]{2,1,0:T(8,128)(2,1)S(1)} %attend.1.refs_4_), channel_id=1, source_target_pairs={{0,16},{8,24},{16,0},{24,8},{1,17},{9,25},{17,1},{25,9},{2,18},{10... | collective-permute-start | bytes 98312 | tf_op jit(solution)/shard_map/ppermute | solution.py:357
  30.5 0.8 %collective-permute-start.4 = (bf16[8,16,128]{2,1,0:T(8,128)(2,1)S(1)}, bf16[8,16,128]{2,1,0:T(8,128)(2,1)S(1)}, u32[]{:S(2)}, u32[]{:S(2)}) collective-permute-start(bf16[8,16,128]{2,1,0:T(8,128)(2,1)S(1)} %attend.1.refs_4_), channel_id=1, source_target_pairs={{0,8},{8,0},{16,24},{24,16},{1,9},{9,1},{17,25},{25,17},{2,10},{10... | collective-permute-start | bytes 98312 | tf_op jit(solution)/shard_map/ppermute | solution.py:357
  31.4 1.3 %collective-permute-done.6.refs_7_ = bf16[8,16,128]{2,1,0:T(8,128)(2,1)S(1)} collective-permute-done((bf16[8,16,128]{2,1,0:T(8,128)(2,1)S(1)}, bf16[8,16,128]{2,1,0:T(8,128)(2,1)S(1)}, u32[]{:S(2)}, u32[]{:S(2)}) %collective-permute-start.6) | collective-permute-done | bytes 32800 | tf_op jit(solution)/shard_map/ppermute | solution.py:357
  32.7 0.6 %collective-permute-done.5.refs_6_ = bf16[8,16,128]{2,1,0:T(8,128)(2,1)S(1)} collective-permute-done((bf16[8,16,128]{2,1,0:T(8,128)(2,1)S(1)}, bf16[8,16,128]{2,1,0:T(8,128)(2,1)S(1)}, u32[]{:S(2)}, u32[]{:S(2)}) %collective-permute-start.5) | collective-permute-done | bytes 32800 | tf_op jit(solution)/shard_map/ppermute | solution.py:357
  33.3 1.2 %collective-permute-done.4.refs_5_ = bf16[8,16,128]{2,1,0:T(8,128)(2,1)S(1)} collective-permute-done((bf16[8,16,128]{2,1,0:T(8,128)(2,1)S(1)}, bf16[8,16,128]{2,1,0:T(8,128)(2,1)S(1)}, u32[]{:S(2)}, u32[]{:S(2)}) %collective-permute-start.4) | collective-permute-done | bytes 32800 | tf_op jit(solution)/shard_map/ppermute | solution.py:357
  34.5 0.0 copy-done.4
  34.5 0.0 copy-done.5
  34.5 0.0 copy-done.6
  34.5 0.0 copy-done.7
  34.5 0.0 copy-done.8
  34.5 2.0 %finish.1 = (bf16[8,16,256]{2,1,0:T(8,128)(2,1)}, bf16[8,16,256]{2,1,0:T(8,128)(2,1)}) custom-call(bf16[8,16,256]{2,1,0:T(8,128)(2,1)S(1)} %copy-done, bf16[8,16,256]{2,1,0:T(8,128)(2,1)S(1)} %collective-permute-done.refs_1_, bf16[8,16,256]{2,1,0:T(8,128)(2,1)S(1)} %collective-permute-done.1.refs_2_, bf16[8,16,256]{2,1,0:T(8,128)(2,1)S(1)} %collective-permute-done.2.refs_3_, ...), custom_call_target="tpu_custom_call" | custom-call | tf_op jit(solution)/shard_map/finish/pallas_call | solution.py:360
  (1 shorter events, 0.0 us)
Async XLA Ops:
  0.6 0.8 %copy-start = (bf16[8,16,256]{2,1,0:T(8,128)(2,1)S(1)}, bf16[8,16,256]{2,1,0:T(8,128)(2,1)}, u32[]{:S(2)}) copy-start(bf16[8,16,256]{2,1,0:T(8,128)(2,1)} %refs_0_.3) | copy-start | bytes 196612
  0.6 0.9 %copy-start.2 = (bf16[256,128]{1,0:T(8,128)(2,1)S(1)}, bf16[256,128]{1,0:T(8,128)(2,1)}, u32[]{:S(2)}) copy-start(bf16[256,128]{1,0:T(8,128)(2,1)} %value_ref.1) | copy-start | bytes 196612
  0.6 0.9 %copy-start.1 = (bf16[256,128]{1,0:T(8,128)(2,1)S(1)}, bf16[256,128]{1,0:T(8,128)(2,1)}, u32[]{:S(2)}) copy-start(bf16[256,128]{1,0:T(8,128)(2,1)} %key_ref.1) | copy-start | bytes 196612
  2.0 24.4 %copy-start.3 = (bf16[256,128]{1,0:T(8,128)(2,1)S(1)}, bf16[256,128]{1,0:T(8,128)(2,1)}, u32[]{:S(2)}) copy-start(bf16[256,128]{1,0:T(8,128)(2,1)} %refs_4_.1) | copy-start | bytes 196612
  19.2 8.2 %collective-permute-start.3 = (bf16[32,2,16,128]{3,2,1,0:T(8,128)(2,1)S(1)}, bf16[32,2,16,128]{3,2,1,0:T(8,128)(2,1)S(1)}, u32[]{:S(2)}, u32[]{:S(2)}) collective-permute-start(bf16[32,2,16,128]{3,2,1,0:T(8,128)(2,1)S(1)} %all_to_all.5), channel_id=1, source_target_pairs={{0,1},{1,0},{2,3},{3,2},{4,5},{5,4},{6,7},{7,6},{8,9},{9,8},{10,11... | collective-permute-start | bytes 786440 | tf_op jit(solution)/shard_map/ppermute | solution.py:327
  19.9 5.8 %collective-permute-start.2 = (bf16[8,16,256]{2,1,0:T(8,128)(2,1)S(1)}, bf16[8,16,256]{2,1,0:T(8,128)(2,1)S(1)}, u32[]{:S(2)}, u32[]{:S(2)}) collective-permute-start(bf16[8,16,256]{2,1,0:T(8,128)(2,1)S(1)} %copy-done), channel_id=1, source_target_pairs={{0,24},{8,16},{16,8},{24,0},{1,25},{9,17},{17,9},{25,1},{2,26},{10... | collective-permute-start | bytes 196616 | tf_op jit(solution)/shard_map/ppermute | solution.py:316
  20.7 5.2 %collective-permute-start.1 = (bf16[8,16,256]{2,1,0:T(8,128)(2,1)S(1)}, bf16[8,16,256]{2,1,0:T(8,128)(2,1)S(1)}, u32[]{:S(2)}, u32[]{:S(2)}) collective-permute-start(bf16[8,16,256]{2,1,0:T(8,128)(2,1)S(1)} %copy-done), channel_id=1, source_target_pairs={{0,16},{8,24},{16,0},{24,8},{1,17},{9,25},{17,1},{25,9},{2,18},{10... | collective-permute-start | bytes 196616 | tf_op jit(solution)/shard_map/ppermute | solution.py:316
  22.2 4.3 %collective-permute-start = (bf16[8,16,256]{2,1,0:T(8,128)(2,1)S(1)}, bf16[8,16,256]{2,1,0:T(8,128)(2,1)S(1)}, u32[]{:S(2)}, u32[]{:S(2)}) collective-permute-start(bf16[8,16,256]{2,1,0:T(8,128)(2,1)S(1)} %copy-done), channel_id=1, source_target_pairs={{0,8},{8,0},{16,24},{24,16},{1,9},{9,1},{17,25},{25,17},{2,10},{10... | collective-permute-start | bytes 196616 | tf_op jit(solution)/shard_map/ppermute | solution.py:316
  27.4 7.1 %copy-start.4 = (bf16[128,256]{1,0:T(8,128)(2,1)S(1)}, bf16[128,256]{1,0:T(8,128)(2,1)}, u32[]{:S(2)}) copy-start(bf16[128,256]{1,0:T(8,128)(2,1)} %refs_8_.1) | copy-start | bytes 196612
  27.4 7.1 %copy-start.5 = (bf16[256,128]{1,0:T(8,128)(2,1)S(1)}, bf16[256,128]{1,0:T(8,128)(2,1)}, u32[]{:S(2)}) copy-start(bf16[256,128]{1,0:T(8,128)(2,1)} %refs_9_.1) | copy-start | bytes 196612
  27.4 7.0 %copy-start.6 = (bf16[256,128]{1,0:T(8,128)(2,1)S(1)}, bf16[256,128]{1,0:T(8,128)(2,1)}, u32[]{:S(2)}) copy-start(bf16[256,128]{1,0:T(8,128)(2,1)} %refs_10_.1) | copy-start | bytes 196612
  27.4 7.0 %copy-start.7 = (bf16[256,128]{1,0:T(8,128)(2,1)S(1)}, bf16[256,128]{1,0:T(8,128)(2,1)}, u32[]{:S(2)}) copy-start(bf16[256,128]{1,0:T(8,128)(2,1)} %refs_11_.1) | copy-start | bytes 196612
  27.4 7.0 %copy-start.8 = (bf16[128,256]{1,0:T(8,128)(2,1)S(1)}, bf16[128,256]{1,0:T(8,128)(2,1)}, u32[]{:S(2)}) copy-start(bf16[128,256]{1,0:T(8,128)(2,1)} %refs_12_.1) | copy-start | bytes 196612
  27.8 4.9 %collective-permute-start.6 = (bf16[8,16,128]{2,1,0:T(8,128)(2,1)S(1)}, bf16[8,16,128]{2,1,0:T(8,128)(2,1)S(1)}, u32[]{:S(2)}, u32[]{:S(2)}) collective-permute-start(bf16[8,16,128]{2,1,0:T(8,128)(2,1)S(1)} %attend.1.refs_4_), channel_id=1, source_target_pairs={{0,24},{8,16},{16,8},{24,0},{1,25},{9,17},{17,9},{25,1},{2,26},{10... | collective-permute-start | bytes 98312 | tf_op jit(solution)/shard_map/ppermute | solution.py:357
  29.3 3.9 %collective-permute-start.5 = (bf16[8,16,128]{2,1,0:T(8,128)(2,1)S(1)}, bf16[8,16,128]{2,1,0:T(8,128)(2,1)S(1)}, u32[]{:S(2)}, u32[]{:S(2)}) collective-permute-start(bf16[8,16,128]{2,1,0:T(8,128)(2,1)S(1)} %attend.1.refs_4_), channel_id=1, source_target_pairs={{0,16},{8,24},{16,0},{24,8},{1,17},{9,25},{17,1},{25,9},{2,18},{10... | collective-permute-start | bytes 98312 | tf_op jit(solution)/shard_map/ppermute | solution.py:357
  30.5 3.9 %collective-permute-start.4 = (bf16[8,16,128]{2,1,0:T(8,128)(2,1)S(1)}, bf16[8,16,128]{2,1,0:T(8,128)(2,1)S(1)}, u32[]{:S(2)}, u32[]{:S(2)}) collective-permute-start(bf16[8,16,128]{2,1,0:T(8,128)(2,1)S(1)} %attend.1.refs_4_), channel_id=1, source_target_pairs={{0,8},{8,0},{16,24},{24,16},{1,9},{9,1},{17,25},{25,17},{2,10},{10... | collective-permute-start | bytes 98312 | tf_op jit(solution)/shard_map/ppermute | solution.py:357

commit v11 on v10

--- a/solution.py
+++ b/solution.py
@@ -137,8 +137,10 @@
     seq_dev, col_dev, width = field_ref.shape
     heads, chips, cores = out_ref.shape[:3]
     normed = norm_rows(field_ref[...].astype(jnp.float32).reshape(seq_dev * col_dev, width))
-    for kind, weight_ref in enumerate((key_ref, value_ref)):
-        rows = project(normed, weight_ref[...])
+    inner = key_ref.shape[1]
+    pair = project(normed, jnp.concatenate([key_ref[...], value_ref[...]], axis=1))
+    for kind in range(2):
+        rows = pair[:, kind * inner : (kind + 1) * inner]
         for core in range(cores):
             first = core * heads
             tiles = [
@@ -365,7 +367,7 @@
         scratch_shapes=[
             pltpu.VMEM((total, width), f32),
         ],
-        compiler_params=grant,
+        compiler_params=pltpu.CompilerParams(vmem_limit_bytes=8 << 20),
         name="finish",
     )(*fields, *parts, row_output, column_query, column_key, column_value, column_output)
 

time: 36.7 us -> 36.7 us (level)
  no operation moved by 1% of the time
where the time goes in v11:
time: 36.7 us; the launch traced here: 36.5 us
  blocking collectives  17.1 us (47%)
  starting transfers between devices  7.78 us (21%)
  waiting for transfers between devices  6.15 us (17%)
  Pallas kernels  3.76 us (10%)
  local copies, waits for them, and re-layouts  0.92 us (3%)
  between operations  0.74 us (2%)
    all_to_all x1, blocking collectives, by_head(): lax.all_to_all(blocks.reshape(seq * col, 2, col_dev, inner), ('seq', 'col...  17.1 us
    ppermute x3, starting transfers between devices, by_head(): lax.ppermute(parts[place], 'seq', [(i, i ^ place) for i in range(seq)])  3.55 us
    ppermute x3, starting transfers between devices, by_head(): lax.ppermute(alignment, 'seq', [(i, i ^ place) for i in range(seq)])  3.49 us
    ppermute x3, waiting for transfers between devices, by_head(): lax.ppermute(parts[place], 'seq', [(i, i ^ place) for i in range(seq)])  3.09 us
    ppermute x3, waiting for transfers between devices, by_head(): lax.ppermute(alignment, 'seq', [(i, i ^ place) for i in range(seq)])  3.06 us
    pallas_call x1, Pallas kernels, by_head(): pl.pallas_call(finish_kernel, out_shape=(like, like), in_specs=[vmem] * (...  2.01 us
    unnamed x18, local copies, waits for them, and re-layouts  0.92 us
    pallas_call x1, Pallas kernels, by_head(): pl.pallas_call(query_kernel, out_shape=jax.ShapeDtypeStruct((halves, seq,...  0.8 us
  transfers between devices with their start and end apart: 7, of which 6 were waited for; matrix products, arithmetic and copies ran while one was open for 0% of the time, Pallas kernels for 3%

profile of v11, /device:TPU:0, one launch (start us, length us, event | category | flops | bytes accessed | tf_op | source)
XLA Modules:
  0.0 36.5 jit_solution(17847146837539901084)
XLA Ops:
  0.6 0.0 copy-start
  0.6 0.0 copy-start.2
  0.6 0.0 copy-start.1
  0.7 0.8 %copy-done = bf16[8,16,256]{2,1,0:T(8,128)(2,1)S(1)} copy-done((bf16[8,16,256]{2,1,0:T(8,128)(2,1)S(1)}, bf16[8,16,256]{2,1,0:T(8,128)(2,1)}, u32[]{:S(2)}) %copy-start) | copy-done | bytes 65560
  1.5 0.0 copy-done.2
  1.5 0.0 copy-done.1
  1.5 0.5 %project.1 = bf16[4,4,2,2,16,128]{5,4,3,2,1,0:T(8,128)(2,1)S(1)} custom-call(bf16[8,16,256]{2,1,0:T(8,128)(2,1)S(1)} %copy-done, bf16[256,128]{1,0:T(8,128)(2,1)S(1)} %copy-done.1, bf16[256,128]{1,0:T(8,128)(2,1)S(1)} %copy-done.2, f32[8,128]{1,0:T(8,128)S(1)} %gate.1.gate_ref), custom_call_target="tpu_custom_call" | custom-call | tf_op jit(solution)/shard_map/project/pallas_call | solution.py:320
  2.0 0.0 copy-start.3
  2.0 17.1 %all_to_all.5 = bf16[32,2,16,128]{3,2,1,0:T(8,128)(2,1)S(1)} all-to-all(bf16[32,2,16,128]{3,2,1,0:T(8,128)(2,1)S(1)} %bitcast.5), channel_id=1, replica_groups=mesh['seq'=4,'col'=8] {'seq','col'}, dimensions={0} | all-to-all | bytes 524288 | tf_op jit(solution)/shard_map/all_to_all | solution.py:328
  19.1 0.7 %collective-permute-start.3 = (bf16[32,2,16,128]{3,2,1,0:T(8,128)(2,1)S(1)}, bf16[32,2,16,128]{3,2,1,0:T(8,128)(2,1)S(1)}, u32[]{:S(2)}, u32[]{:S(2)}) collective-permute-start(bf16[32,2,16,128]{3,2,1,0:T(8,128)(2,1)S(1)} %all_to_all.5), channel_id=1, source_target_pairs={{0,1},{1,0},{2,3},{3,2},{4,5},{5,4},{6,7},{7,6},{8,9},{9,8},{10,11... | collective-permute-start | bytes 786440 | tf_op jit(solution)/shard_map/ppermute | solution.py:329
  19.9 0.8 %collective-permute-start.2 = (bf16[8,16,256]{2,1,0:T(8,128)(2,1)S(1)}, bf16[8,16,256]{2,1,0:T(8,128)(2,1)S(1)}, u32[]{:S(2)}, u32[]{:S(2)}) collective-permute-start(bf16[8,16,256]{2,1,0:T(8,128)(2,1)S(1)} %copy-done), channel_id=1, source_target_pairs={{0,24},{8,16},{16,8},{24,0},{1,25},{9,17},{17,9},{25,1},{2,26},{10... | collective-permute-start | bytes 196616 | tf_op jit(solution)/shard_map/ppermute | solution.py:318
  20.7 1.5 %collective-permute-start.1 = (bf16[8,16,256]{2,1,0:T(8,128)(2,1)S(1)}, bf16[8,16,256]{2,1,0:T(8,128)(2,1)S(1)}, u32[]{:S(2)}, u32[]{:S(2)}) collective-permute-start(bf16[8,16,256]{2,1,0:T(8,128)(2,1)S(1)} %copy-done), channel_id=1, source_target_pairs={{0,16},{8,24},{16,0},{24,8},{1,17},{9,25},{17,1},{25,9},{2,18},{10... | collective-permute-start | bytes 196616 | tf_op jit(solution)/shard_map/ppermute | solution.py:318
  22.2 1.2 %collective-permute-start = (bf16[8,16,256]{2,1,0:T(8,128)(2,1)S(1)}, bf16[8,16,256]{2,1,0:T(8,128)(2,1)S(1)}, u32[]{:S(2)}, u32[]{:S(2)}) collective-permute-start(bf16[8,16,256]{2,1,0:T(8,128)(2,1)S(1)} %copy-done), channel_id=1, source_target_pairs={{0,8},{8,0},{16,24},{24,16},{1,9},{9,1},{17,25},{25,17},{2,10},{10... | collective-permute-start | bytes 196616 | tf_op jit(solution)/shard_map/ppermute | solution.py:318
  23.4 2.3 %collective-permute-done.2.refs_3_ = bf16[8,16,256]{2,1,0:T(8,128)(2,1)S(1)} collective-permute-done((bf16[8,16,256]{2,1,0:T(8,128)(2,1)S(1)}, bf16[8,16,256]{2,1,0:T(8,128)(2,1)S(1)}, u32[]{:S(2)}, u32[]{:S(2)}) %collective-permute-start.2) | collective-permute-done | bytes 65568 | tf_op jit(solution)/shard_map/ppermute | solution.py:318
  25.7 0.2 collective-permute-done.1.refs_2_
  25.9 0.5 %collective-permute-done.refs_1_ = bf16[8,16,256]{2,1,0:T(8,128)(2,1)S(1)} collective-permute-done((bf16[8,16,256]{2,1,0:T(8,128)(2,1)S(1)}, bf16[8,16,256]{2,1,0:T(8,128)(2,1)S(1)}, u32[]{:S(2)}, u32[]{:S(2)}) %collective-permute-start) | collective-permute-done | bytes 65568 | tf_op jit(solution)/shard_map/ppermute | solution.py:318
  26.4 0.0 copy-done.3
  26.4 0.8 %query.1.query_ref = bf16[2,4,16,128]{3,2,1,0:T(8,128)(2,1)S(1)} custom-call(bf16[8,16,256]{2,1,0:T(8,128)(2,1)S(1)} %copy-done, bf16[8,16,256]{2,1,0:T(8,128)(2,1)S(1)} %collective-permute-done.refs_1_, bf16[8,16,256]{2,1,0:T(8,128)(2,1)S(1)} %collective-permute-done.1.refs_2_, bf16[8,16,256]{2,1,0:T(8,128)(2,1)S(1)} %collective-permute-done.2.refs_3_, ...), custom_call_target="tpu_custom_call" | custom-call | tf_op jit(solution)/shard_map/query/pallas_call | solution.py:333
  27.2 0.1 half.1.logits_ref
  27.4 0.0 collective-permute-done.3
  27.4 0.0 copy-start.4
  27.4 0.0 copy-start.5
  27.4 0.0 copy-start.6
  27.4 0.0 copy-start.7
  27.4 0.0 copy-start.8
  27.4 0.4 attend.1.refs_4_
  27.8 1.5 %collective-permute-start.6 = (bf16[8,16,128]{2,1,0:T(8,128)(2,1)S(1)}, bf16[8,16,128]{2,1,0:T(8,128)(2,1)S(1)}, u32[]{:S(2)}, u32[]{:S(2)}) collective-permute-start(bf16[8,16,128]{2,1,0:T(8,128)(2,1)S(1)} %attend.1.refs_4_), channel_id=1, source_target_pairs={{0,24},{8,16},{16,8},{24,0},{1,25},{9,17},{17,9},{25,1},{2,26},{10... | collective-permute-start | bytes 98312 | tf_op jit(solution)/shard_map/ppermute | solution.py:359
  29.3 1.2 %collective-permute-start.5 = (bf16[8,16,128]{2,1,0:T(8,128)(2,1)S(1)}, bf16[8,16,128]{2,1,0:T(8,128)(2,1)S(1)}, u32[]{:S(2)}, u32[]{:S(2)}) collective-permute-start(bf16[8,16,128]{2,1,0:T(8,128)(2,1)S(1)} %attend.1.refs_4_), channel_id=1, source_target_pairs={{0,16},{8,24},{16,0},{24,8},{1,17},{9,25},{17,1},{25,9},{2,18},{10... | collective-permute-start | bytes 98312 | tf_op jit(solution)/shard_map/ppermute | solution.py:359
  30.5 0.8 %collective-permute-start.4 = (bf16[8,16,128]{2,1,0:T(8,128)(2,1)S(1)}, bf16[8,16,128]{2,1,0:T(8,128)(2,1)S(1)}, u32[]{:S(2)}, u32[]{:S(2)}) collective-permute-start(bf16[8,16,128]{2,1,0:T(8,128)(2,1)S(1)} %attend.1.refs_4_), channel_id=1, source_target_pairs={{0,8},{8,0},{16,24},{24,16},{1,9},{9,1},{17,25},{25,17},{2,10},{10... | collective-permute-start | bytes 98312 | tf_op jit(solution)/shard_map/ppermute | solution.py:359
  31.4 1.3 %collective-permute-done.6.refs_7_ = bf16[8,16,128]{2,1,0:T(8,128)(2,1)S(1)} collective-permute-done((bf16[8,16,128]{2,1,0:T(8,128)(2,1)S(1)}, bf16[8,16,128]{2,1,0:T(8,128)(2,1)S(1)}, u32[]{:S(2)}, u32[]{:S(2)}) %collective-permute-start.6) | collective-permute-done | bytes 32800 | tf_op jit(solution)/shard_map/ppermute | solution.py:359
  32.7 0.6 %collective-permute-done.5.refs_6_ = bf16[8,16,128]{2,1,0:T(8,128)(2,1)S(1)} collective-permute-done((bf16[8,16,128]{2,1,0:T(8,128)(2,1)S(1)}, bf16[8,16,128]{2,1,0:T(8,128)(2,1)S(1)}, u32[]{:S(2)}, u32[]{:S(2)}) %collective-permute-start.5) | collective-permute-done | bytes 32800 | tf_op jit(solution)/shard_map/ppermute | solution.py:359
  33.2 1.2 %collective-permute-done.4.refs_5_ = bf16[8,16,128]{2,1,0:T(8,128)(2,1)S(1)} collective-permute-done((bf16[8,16,128]{2,1,0:T(8,128)(2,1)S(1)}, bf16[8,16,128]{2,1,0:T(8,128)(2,1)S(1)}, u32[]{:S(2)}, u32[]{:S(2)}) %collective-permute-start.4) | collective-permute-done | bytes 32800 | tf_op jit(solution)/shard_map/ppermute | solution.py:359
  34.4 0.0 copy-done.4
  34.5 0.0 copy-done.5
  34.5 0.0 copy-done.6
  34.5 0.0 copy-done.7
  34.5 0.0 copy-done.8
  34.5 2.0 %finish.1 = (bf16[8,16,256]{2,1,0:T(8,128)(2,1)}, bf16[8,16,256]{2,1,0:T(8,128)(2,1)}) custom-call(bf16[8,16,256]{2,1,0:T(8,128)(2,1)S(1)} %copy-done, bf16[8,16,256]{2,1,0:T(8,128)(2,1)S(1)} %collective-permute-done.refs_1_, bf16[8,16,256]{2,1,0:T(8,128)(2,1)S(1)} %collective-permute-done.1.refs_2_, bf16[8,16,256]{2,1,0:T(8,128)(2,1)S(1)} %collective-permute-done.2.refs_3_, ...), custom_call_target="tpu_custom_call" | custom-call | tf_op jit(solution)/shard_map/finish/pallas_call | solution.py:362
  (1 shorter events, 0.0 us)
Async XLA Ops:
  0.6 0.8 %copy-start = (bf16[8,16,256]{2,1,0:T(8,128)(2,1)S(1)}, bf16[8,16,256]{2,1,0:T(8,128)(2,1)}, u32[]{:S(2)}) copy-start(bf16[8,16,256]{2,1,0:T(8,128)(2,1)} %refs_0_.3) | copy-start | bytes 196612
  0.6 0.9 %copy-start.2 = (bf16[256,128]{1,0:T(8,128)(2,1)S(1)}, bf16[256,128]{1,0:T(8,128)(2,1)}, u32[]{:S(2)}) copy-start(bf16[256,128]{1,0:T(8,128)(2,1)} %value_ref.1) | copy-start | bytes 196612
  0.6 0.9 %copy-start.1 = (bf16[256,128]{1,0:T(8,128)(2,1)S(1)}, bf16[256,128]{1,0:T(8,128)(2,1)}, u32[]{:S(2)}) copy-start(bf16[256,128]{1,0:T(8,128)(2,1)} %key_ref.1) | copy-start | bytes 196612
  2.0 24.4 %copy-start.3 = (bf16[256,128]{1,0:T(8,128)(2,1)S(1)}, bf16[256,128]{1,0:T(8,128)(2,1)}, u32[]{:S(2)}) copy-start(bf16[256,128]{1,0:T(8,128)(2,1)} %refs_4_.1) | copy-start | bytes 196612
  19.1 8.2 %collective-permute-start.3 = (bf16[32,2,16,128]{3,2,1,0:T(8,128)(2,1)S(1)}, bf16[32,2,16,128]{3,2,1,0:T(8,128)(2,1)S(1)}, u32[]{:S(2)}, u32[]{:S(2)}) collective-permute-start(bf16[32,2,16,128]{3,2,1,0:T(8,128)(2,1)S(1)} %all_to_all.5), channel_id=1, source_target_pairs={{0,1},{1,0},{2,3},{3,2},{4,5},{5,4},{6,7},{7,6},{8,9},{9,8},{10,11... | collective-permute-start | bytes 786440 | tf_op jit(solution)/shard_map/ppermute | solution.py:329
  19.9 5.8 %collective-permute-start.2 = (bf16[8,16,256]{2,1,0:T(8,128)(2,1)S(1)}, bf16[8,16,256]{2,1,0:T(8,128)(2,1)S(1)}, u32[]{:S(2)}, u32[]{:S(2)}) collective-permute-start(bf16[8,16,256]{2,1,0:T(8,128)(2,1)S(1)} %copy-done), channel_id=1, source_target_pairs={{0,24},{8,16},{16,8},{24,0},{1,25},{9,17},{17,9},{25,1},{2,26},{10... | collective-permute-start | bytes 196616 | tf_op jit(solution)/shard_map/ppermute | solution.py:318
  20.7 5.2 %collective-permute-start.1 = (bf16[8,16,256]{2,1,0:T(8,128)(2,1)S(1)}, bf16[8,16,256]{2,1,0:T(8,128)(2,1)S(1)}, u32[]{:S(2)}, u32[]{:S(2)}) collective-permute-start(bf16[8,16,256]{2,1,0:T(8,128)(2,1)S(1)} %copy-done), channel_id=1, source_target_pairs={{0,16},{8,24},{16,0},{24,8},{1,17},{9,25},{17,1},{25,9},{2,18},{10... | collective-permute-start | bytes 196616 | tf_op jit(solution)/shard_map/ppermute | solution.py:318
  22.2 4.3 %collective-permute-start = (bf16[8,16,256]{2,1,0:T(8,128)(2,1)S(1)}, bf16[8,16,256]{2,1,0:T(8,128)(2,1)S(1)}, u32[]{:S(2)}, u32[]{:S(2)}) collective-permute-start(bf16[8,16,256]{2,1,0:T(8,128)(2,1)S(1)} %copy-done), channel_id=1, source_target_pairs={{0,8},{8,0},{16,24},{24,16},{1,9},{9,1},{17,25},{25,17},{2,10},{10... | collective-permute-start | bytes 196616 | tf_op jit(solution)/shard_map/ppermute | solution.py:318
  27.4 7.1 %copy-start.4 = (bf16[128,256]{1,0:T(8,128)(2,1)S(1)}, bf16[128,256]{1,0:T(8,128)(2,1)}, u32[]{:S(2)}) copy-start(bf16[128,256]{1,0:T(8,128)(2,1)} %refs_8_.1) | copy-start | bytes 196612
  27.4 7.1 %copy-start.5 = (bf16[256,128]{1,0:T(8,128)(2,1)S(1)}, bf16[256,128]{1,0:T(8,128)(2,1)}, u32[]{:S(2)}) copy-start(bf16[256,128]{1,0:T(8,128)(2,1)} %refs_9_.1) | copy-start | bytes 196612
  27.4 7.0 %copy-start.6 = (bf16[256,128]{1,0:T(8,128)(2,1)S(1)}, bf16[256,128]{1,0:T(8,128)(2,1)}, u32[]{:S(2)}) copy-start(bf16[256,128]{1,0:T(8,128)(2,1)} %refs_10_.1) | copy-start | bytes 196612
  27.4 7.0 %copy-start.7 = (bf16[256,128]{1,0:T(8,128)(2,1)S(1)}, bf16[256,128]{1,0:T(8,128)(2,1)}, u32[]{:S(2)}) copy-start(bf16[256,128]{1,0:T(8,128)(2,1)} %refs_11_.1) | copy-start | bytes 196612
  27.4 7.0 %copy-start.8 = (bf16[128,256]{1,0:T(8,128)(2,1)S(1)}, bf16[128,256]{1,0:T(8,128)(2,1)}, u32[]{:S(2)}) copy-start(bf16[128,256]{1,0:T(8,128)(2,1)} %refs_12_.1) | copy-start | bytes 196612
  27.8 4.9 %collective-permute-start.6 = (bf16[8,16,128]{2,1,0:T(8,128)(2,1)S(1)}, bf16[8,16,128]{2,1,0:T(8,128)(2,1)S(1)}, u32[]{:S(2)}, u32[]{:S(2)}) collective-permute-start(bf16[8,16,128]{2,1,0:T(8,128)(2,1)S(1)} %attend.1.refs_4_), channel_id=1, source_target_pairs={{0,24},{8,16},{16,8},{24,0},{1,25},{9,17},{17,9},{25,1},{2,26},{10... | collective-permute-start | bytes 98312 | tf_op jit(solution)/shard_map/ppermute | solution.py:359
  29.3 3.9 %collective-permute-start.5 = (bf16[8,16,128]{2,1,0:T(8,128)(2,1)S(1)}, bf16[8,16,128]{2,1,0:T(8,128)(2,1)S(1)}, u32[]{:S(2)}, u32[]{:S(2)}) collective-permute-start(bf16[8,16,128]{2,1,0:T(8,128)(2,1)S(1)} %attend.1.refs_4_), channel_id=1, source_target_pairs={{0,16},{8,24},{16,0},{24,8},{1,17},{9,25},{17,1},{25,9},{2,18},{10... | collective-permute-start | bytes 98312 | tf_op jit(solution)/shard_map/ppermute | solution.py:359
  30.5 3.9 %collective-permute-start.4 = (bf16[8,16,128]{2,1,0:T(8,128)(2,1)S(1)}, bf16[8,16,128]{2,1,0:T(8,128)(2,1)S(1)}, u32[]{:S(2)}, u32[]{:S(2)}) collective-permute-start(bf16[8,16,128]{2,1,0:T(8,128)(2,1)S(1)} %attend.1.refs_4_), channel_id=1, source_target_pairs={{0,8},{8,0},{16,24},{24,16},{1,9},{9,1},{17,25},{25,17},{2,10},{10... | collective-permute-start | bytes 98312 | tf_op jit(solution)/shard_map/ppermute | solution.py:359
